TPU v7x, 32 devices: a whole 2x2x4 slice. The times are simulated.
32 devices in a mesh: state: 4 (over y, x), space: 8 (over z, core).
Axes of the slice: x: 2, y: 2, z: 4, core: 2. Of those that a mesh axis runs over, the one named last changes fastest.
Arguments:
- states_in: bfloat16 [384, 8192], P('state', 'space'), may hold values from -12 to 12
- cell_matrices: bfloat16 [16, 512, 512], P('space'), may hold values from -0.5 to 1.5, as said below
- connectivity: int32 [16, 512], P('space'), may hold values from 0 to 8191, as said below
- potential: float32 [8192], P('space'), may hold values from 0.2 to 1.2
Outputs:
- filtered: bfloat16 [384, 8192], P('state', 'space')
- intersection: float32 [384, 384], P('state', 'space')
- projected: float32 [384, 384], P('state', 'space')
Inputs may be any that keep to these rules, and one draw needn't show every extreme that they name: `cell_matrices`: each cell's matrix is symmetric. `connectivity`: the cells of rows s * 2 to (s + 1) * 2 - 1 name only nodes from s * 1024 - 128 to (s + 1) * 1024 + 127. A node may be named by several cells, or twice in one cell, or by none.
All inputs are finite; a program needn't handle non-finite values.
Results may differ from a plain program's by a relative error of at most 0.019.
Values may be sent and summed in bfloat16 or wider, within the bound.
No kernel may reach another device: no remote copies, remote signals or barrier semaphores. Data moves between devices by JAX's collectives and lax.ppermute only.
A program may use at most 64 MiB of HBM per device.

v0:
```python
import functools

import jax
import jax.numpy as jnp
from jax import lax
from jax.experimental import pallas as pl
from jax.experimental.pallas import tpu as pltpu
from jax.sharding import PartitionSpec as P


DEGREE = 4

spectrum_center = 3.0
spectrum_half = 3.5

BF16 = jnp.bfloat16
F32 = jnp.float32
SHAPE = jax.ShapeDtypeStruct


def call(body, outs, ins, flops, scratch=(), raw=()):
    where = [
        pl.BlockSpec(memory_space=pltpu.HBM if i in raw else pltpu.VMEM) for i in range(len(ins))
    ]
    ins = [pltpu.with_memory_space_constraint(x, pltpu.HBM) if i in raw else x for i, x in enumerate(ins)]
    return pl.pallas_call(
        body,
        out_shape=outs,
        in_specs=where,
        out_specs=jax.tree.map(lambda _: pl.BlockSpec(memory_space=pltpu.VMEM), outs),
        scratch_shapes=list(scratch),
        compiler_params=pltpu.CompilerParams(vmem_limit_bytes=24 << 20),
        cost_estimate=pl.CostEstimate(flops=flops, bytes_accessed=4 << 20, transcendentals=0),
    )(*ins)


def mm(a, b):
    return jnp.dot(a, b, preferred_element_type=F32)


def mm_nt(a, b):
    return lax.dot_general(a, b, (((1,), (1,)), ((), ())), preferred_element_type=F32)


def is_odd():
    return (lax.axis_index("space") & 1) == 1


def sort_out(got_a, got_b):
    me, odd = lax.axis_index("space"), is_odd()
    got_a, got_b = got_a.astype(F32), got_b.astype(F32)
    low = jnp.where(me == 0, 0.0, jnp.where(odd, got_a, got_b))
    high = jnp.where(me == lax.axis_size("space") - 1, 0.0, jnp.where(odd, got_b, got_a))
    return low, high


def hand_out(low, high, give_a_ref, give_b_ref):
    odd = is_odd()
    give_a_ref[...] = jnp.where(odd, low, high).astype(give_a_ref.dtype)
    give_b_ref[...] = jnp.where(odd, high, low).astype(give_b_ref.dtype)


def halo_body(states_ref, potential_ref, index_ref,
              give_a_ref, give_b_ref, local_ref, low_ref, high_ref, row_ref, sem):
    count, owned = states_ref.shape
    rim = low_ref.shape[1]
    copies = [
        pltpu.make_async_copy(states_ref.at[:, pl.ds(0, rim)], low_ref, sem.at[0]),
        pltpu.make_async_copy(states_ref.at[:, pl.ds(owned - rim, rim)], high_ref, sem.at[1]),
        pltpu.make_async_copy(potential_ref, row_ref, sem.at[2]),
        pltpu.make_async_copy(index_ref, local_ref, sem.at[3]),
    ]
    for copy in copies:
        copy.start()
    for copy in copies:
        copy.wait()
    odd = is_odd()
    low, high = low_ref[...].astype(F32), high_ref[...].astype(F32)
    give_a_ref[:count, :] = jnp.where(odd, low, high).astype(BF16)
    give_b_ref[:count, :] = jnp.where(odd, high, low).astype(BF16)
    for take, give_ref in ((odd, give_a_ref), (jnp.logical_not(odd), give_b_ref)):
        row = jnp.where(take, row_ref[:, :rim], row_ref[:, owned - rim :])
        row = jnp.broadcast_to(row, (16, rim))
        at = lax.broadcasted_iota(jnp.int32, row.shape, 0)
        first = row.astype(BF16).astype(F32)
        second = (row - first).astype(BF16).astype(F32)
        third = (row - first) - second
        give_ref[count:, :] = jnp.where(
            at == 0, first, jnp.where(at == 1, second, jnp.where(at == 2, third, 0.0))
        ).astype(BF16)


def spread_body(index_ref, cells_ref, hot_ref, wide_ref, cells, sem):
    copy = pltpu.make_async_copy(cells_ref, cells, sem)
    copy.start()
    number, nodes, _ = cells_ref.shape
    extent = hot_ref.shape[0]
    rim = nodes // 4
    offset = lax.axis_index("space") * (extent - 2 * rim) - rim
    for c in range(number):
        index = index_ref[c : c + 1, :] - offset
        hot = lax.broadcasted_iota(jnp.int32, (extent, nodes), 0) == index
        hot_ref[:, c * nodes : (c + 1) * nodes] = hot.astype(BF16)
    copy.wait()
    for c in range(number):
        here = slice(c * nodes, (c + 1) * nodes)
        wide_ref[:, here] = mm(hot_ref[:, here], cells[c]).astype(BF16)


def first_zone_body(states_ref, halo_a_ref, halo_b_ref, potential_ref, hot_ref, wide_ref,
                    inner_ref, zone_ref, shift_inner_ref, shift_zone_ref, picked_ref, sums_ref, give_a_ref, give_b_ref):
    count, owned = states_ref.shape
    rim = halo_a_ref.shape[1]
    width, extent = 2 * rim, owned + 2 * rim
    low, high = sort_out(halo_a_ref[...], halo_b_ref[...])
    zone_ref[:, :rim] = low[:count].astype(BF16)
    zone_ref[:, rim:width] = states_ref[:, :rim]
    zone_ref[:, width : width + rim] = states_ref[:, owned - rim :]
    zone_ref[:, width + rim :] = high[:count].astype(BF16)
    inner_ref[...] = states_ref[:, rim : owned - rim]
    row = potential_ref[...] - spectrum_center
    shift_inner_ref[...] = row[:, rim : owned - rim]
    shift_zone_ref[:, rim:width] = row[:, :rim]
    shift_zone_ref[:, width : width + rim] = row[:, owned - rim :]
    for got, at in ((low, 0), (high, width + rim)):
        part = got[count : count + 8]
        shift_zone_ref[:, at : at + rim] = (part[0:1] + part[1:2] + part[2:3]) - spectrum_center
    picked = (
        mm(inner_ref[...], hot_ref[width : extent - width, :])
        + mm(zone_ref[:, :width], hot_ref[:width, :])
        + mm(zone_ref[:, width:], hot_ref[extent - width :, :])
    ).astype(BF16)
    picked_ref[...] = picked
    low, high = mm_nt(picked, wide_ref[:width, :]), mm_nt(picked, wide_ref[extent - width :, :])
    sums_ref[:, :width] = low
    sums_ref[:, width:] = high
    hand_out(low, high, give_a_ref, give_b_ref)


def take_diagonal(rows, start, matrix_ref, diagonal_ref, at):
    size = rows.shape[0]
    same = lax.broadcasted_iota(jnp.int32, (size, size), 0) == lax.broadcasted_iota(
        jnp.int32, (size, size), 1
    )
    square = rows[:, at : at + size]
    diagonal_ref[:, at : at + size] = jnp.sum(jnp.where(same, square, 0.0), axis=0, keepdims=True)
    matrix_ref[start : start + size, :] = rows.astype(BF16)
    matrix_ref[start : start + size, at : at + size] = jnp.where(same, 0.0, square).astype(BF16)


def first_inner_body(inner_ref, picked_ref, shift_inner_ref, hot_ref, wide_ref,
                     next_ref, border_ref, diagonal_ref, part_ref, columns_ref):
    extent = border_ref.shape[0]
    width = border_ref.shape[1] // 2
    inside = slice(width, extent - width)
    value = mm_nt(picked_ref[...], wide_ref[inside, :]) + shift_inner_ref[...] * inner_ref[...].astype(F32)
    following = (value * (1.0 / spectrum_half)).astype(BF16)
    next_ref[...] = following
    columns_ref[:width, :] = hot_ref[:width, :]
    columns_ref[width:, :] = hot_ref[extent - width :, :]
    border_ref[inside, :] = mm_nt(wide_ref[inside, :], columns_ref[...]).astype(BF16)
    for start, at in ((0, 0), (extent - width, width)):
        rows = mm_nt(wide_ref[start : start + width, :], columns_ref[...])
        take_diagonal(rows, start, border_ref, diagonal_ref, at)
    part_ref[...] = mm(following, border_ref[inside, :])


def close_zones(sums_ref, got_a_ref, got_b_ref, shift_zone_ref, mid_ref, old_ref, scale, zone_ref):
    width = got_a_ref.shape[1]
    low, high = sort_out(got_a_ref[...], got_b_ref[...])
    for got, here in ((low, slice(0, width)), (high, slice(width, 2 * width))):
        value = sums_ref[:, here] + got + shift_zone_ref[:, here] * mid_ref[:, here].astype(F32)
        value = value * scale
        if old_ref is not None:
            value = value - old_ref[:, here].astype(F32)
        zone_ref[:, here] = value.astype(BF16)


def zone_sums(zone_ref, part_ref, border_ref, border_diagonal_ref):
    extent = border_ref.shape[0]
    width = zone_ref.shape[1] // 2
    sums = (
        part_ref[...]
        + mm(zone_ref[:, :width], border_ref[:width, :])
        + mm(zone_ref[:, width:], border_ref[extent - width :, :])
        + border_diagonal_ref[...] * zone_ref[...].astype(F32)
    )
    return sums[:, :width], sums[:, width:]


def zone_body(has_old, scale, sums_ref, got_a_ref, got_b_ref, shift_zone_ref, mid_ref, *rest):
    old_ref, rest = (rest[0], rest[1:]) if has_old else (None, rest)
    part_ref, border_ref, border_diagonal_ref, zone_ref, next_sums_ref, give_a_ref, give_b_ref = rest
    close_zones(sums_ref, got_a_ref, got_b_ref, shift_zone_ref, mid_ref, old_ref, scale, zone_ref)
    low, high = zone_sums(zone_ref, part_ref, border_ref, border_diagonal_ref)
    width = low.shape[1]
    next_sums_ref[:, :width] = low
    next_sums_ref[:, width:] = high
    hand_out(low, high, give_a_ref, give_b_ref)


def inner_sums(zone_ref, inner_ref, border_ref, square_ref, diagonal_ref):
    width = zone_ref.shape[1] // 2
    inside = slice(width, width + square_ref.shape[0])
    return (
        mm_nt(zone_ref[...], border_ref[inside, :])
        + mm(inner_ref[...], square_ref[...])
        + diagonal_ref[...] * inner_ref[...].astype(F32)
    )


def inner_body(zone_ref, inner_ref, old_ref, shift_inner_ref, border_ref, square_ref, diagonal_ref, next_ref, part_ref):
    sums = inner_sums(zone_ref, inner_ref, border_ref, square_ref, diagonal_ref)
    value = (sums + shift_inner_ref[...] * inner_ref[...].astype(F32)) * (2.0 / spectrum_half)
    next_ref[...] = (value - old_ref[...].astype(F32)).astype(BF16)
    width = zone_ref.shape[1] // 2
    part_ref[...] = mm(next_ref[...], border_ref[width : width + next_ref.shape[1], :])


def square_body(zone_ref, inner_ref, old_ref, shift_inner_ref, border_ref, hot_ref, wide_ref,
                square_ref, diagonal_ref, next_ref, part_ref):
    size = square_ref.shape[0]
    width = (hot_ref.shape[0] - size) // 2
    for start in range(0, size, 256):
        rows = mm_nt(wide_ref[width + start : width + start + 256, :], hot_ref[width : width + size, :])
        take_diagonal(rows, start, square_ref, diagonal_ref, start)
    inner_body(zone_ref, inner_ref, old_ref, shift_inner_ref, border_ref, square_ref, diagonal_ref, next_ref, part_ref)


def energy_zone_body(sums_ref, got_a_ref, got_b_ref, shift_zone_ref, mid_ref, old_ref,
                     part_ref, border_ref, border_diagonal_ref, zone_ref, rim_ref, energy_ref, give_a_ref, give_b_ref):
    close_zones(sums_ref, got_a_ref, got_b_ref, shift_zone_ref, mid_ref, old_ref,
                2.0 / spectrum_half, zone_ref)
    width = got_a_ref.shape[1]
    rim = width // 2
    rim_ref[...] = zone_ref[:, rim : width + rim]
    low, high = zone_sums(zone_ref, part_ref, border_ref, border_diagonal_ref)
    own = shift_zone_ref[:, rim : width + rim] + spectrum_center
    own = own * rim_ref[...].astype(F32)
    energy_ref[:, :rim] = low[:, rim:] + own[:, :rim]
    energy_ref[:, rim:] = high[:, :rim] + own[:, rim:]
    hand_out(low[:, :rim], high[:, rim:], give_a_ref, give_b_ref)


def energy_inner_body(zone_ref, inner_ref, shift_inner_ref, border_ref, square_ref, diagonal_ref,
                      energy_ref, filtered_ref):
    sums = inner_sums(zone_ref, inner_ref, border_ref, square_ref, diagonal_ref)
    own = (shift_inner_ref[...] + spectrum_center) * inner_ref[...].astype(F32)
    energy_ref[...] = (sums + own).astype(BF16)
    width = zone_ref.shape[1] // 2
    rim = width // 2
    owned = filtered_ref.shape[1]
    filtered_ref[:, :rim] = zone_ref[:, rim:width]
    filtered_ref[:, rim : owned - rim] = inner_ref[...]
    filtered_ref[:, owned - rim :] = zone_ref[:, width : width + rim]


def project_body(scale, energy_rim_ref, got_a_ref, got_b_ref, energy_inner_ref, *refs):
    *blocks, out_ref, give_ref, stack_ref, pair_ref = refs
    count, inside = energy_inner_ref.shape
    rim = got_a_ref.shape[1]
    low, high = sort_out(got_a_ref[...], got_b_ref[...])
    group = lax.axis_index("state")
    groups = len(blocks) // 2
    for distance in range(groups):
        inner_ref, rim_ref = blocks[2 * distance : 2 * distance + 2]
        at = pl.multiple_of((group ^ distance) * count, count)
        stack_ref[pl.ds(at, count), :inside] = inner_ref[...]
        stack_ref[pl.ds(at, count), inside:] = rim_ref[...]
    pair_ref[:count, :inside] = blocks[0][...]
    pair_ref[:count, inside:] = blocks[1][...]
    pair_ref[count:, :inside] = energy_inner_ref[...]
    pair_ref[count:, inside : inside + rim] = (energy_rim_ref[:, :rim] + low).astype(BF16)
    pair_ref[count:, inside + rim :] = (energy_rim_ref[:, rim:] + high).astype(BF16)
    both = mm_nt(stack_ref[...], pair_ref[...]) * scale
    chips, _, columns, _ = out_ref.shape
    odd = is_odd()
    for chip in range(chips):
        parts = [both[(2 * chip + core) * columns : (2 * chip + core + 1) * columns] for core in range(2)]
        for core in range(2):
            out_ref[chip, core] = parts[core].astype(BF16)
        give_ref[chip] = jnp.where(odd, parts[0], parts[1]).astype(BF16)


def halve_body(mine_ref, got_ref, *pieces):
    for distance, piece_ref in enumerate(pieces):
        chip = (lax.axis_index("space") >> 1) ^ distance
        total = mine_ref[chip, lax.axis_index("space") & 1].astype(F32) + got_ref[chip].astype(F32)
        piece_ref[...] = total.astype(BF16)


def final_body(count, *refs):
    parts, (first_ref, second_ref) = refs[:-2], refs[-2:]
    total = parts[0][...].astype(F32)
    for part in parts[1:]:
        total = total + part[...].astype(F32)
    first_ref[...] = total[:, :count]
    second_ref[...] = total[:, count:]


def swap(block, n_state, n_space, lead):
    route = []
    for s in range(n_state):
        for i in range(n_space):
            j = i + 1 if (i - lead) % 2 == 0 else i - 1
            if 0 <= j < n_space:
                route.append((s * n_space + i, s * n_space + j))
            elif (s ^ 1) < n_state:
                route.append((s * n_space + i, (s ^ 1) * n_space + i))
    return lax.ppermute(block, ("state", "space"), route)


def exchange(give_a, give_b, n_state, n_space):
    got_a = swap(give_a, n_state, n_space, 0)
    got_b = swap(give_b, n_state, n_space, 1)
    return got_a, got_b


def across(block, axis, distance):
    return lax.ppermute(block, axis, [(i, i ^ distance) for i in range(lax.axis_size(axis))])


def program(states_in, cell_matrices, connectivity, potential):
    count, owned = states_in.shape
    cells, nodes, _ = cell_matrices.shape
    rim = nodes // 4
    extent, inside = owned + 2 * rim, owned - 2 * rim
    n_state, n_space = lax.axis_size("state"), lax.axis_size("space")
    row = potential.reshape(1, owned)
    work = 2 * count * extent * extent
    inner = SHAPE((count, inside), BF16)
    zone, sums_of = SHAPE((count, 4 * rim), BF16), SHAPE((count, 4 * rim), F32)
    give, give_rim = SHAPE((count, 2 * rim), BF16), SHAPE((count, rim), BF16)

    halo = SHAPE((count + 16, rim), BF16)
    *gave, local = call(
        halo_body, (halo, halo, SHAPE(connectivity.shape, connectivity.dtype)),
        (states_in, row, connectivity), 0, raw=(0, 1, 2),
        scratch=[
            pltpu.VMEM((count, rim), BF16), pltpu.VMEM((count, rim), BF16),
            pltpu.VMEM((1, owned), F32), pltpu.SemaphoreType.DMA((4,)),
        ],
    )
    got = exchange(*gave, n_state, n_space)
    table = SHAPE((extent, cells * nodes), BF16)
    hot, wide = call(
        spread_body, (table, table), (local, cell_matrices),
        2 * extent * cells * nodes * nodes, raw=(1,),
        scratch=[pltpu.VMEM(cell_matrices.shape, BF16), pltpu.SemaphoreType.DMA],
    )
    inner_0, zone_0, shift_inner, shift_zone, picked, sums, *gave = call(
        first_zone_body,
        (inner, zone, SHAPE((1, inside), F32), SHAPE((1, 4 * rim), F32),
         SHAPE((count, cells * nodes), BF16), sums_of, give, give),
        (states_in, *got, row, hot, wide), work,
    )
    got = exchange(*gave, n_state, n_space)
    border_line, line = SHAPE((1, 4 * rim), F32), SHAPE((1, inside), F32)
    inner_1, border, border_diagonal, partial = call(
        first_inner_body,
        (inner, SHAPE((extent, 4 * rim), BF16), border_line, sums_of),
        (inner_0, picked, shift_inner, hot, wide), 8 * extent * rim * cells * nodes,
        scratch=[pltpu.VMEM((4 * rim, cells * nodes), BF16)],
    )
    inners, zones = [inner_0, inner_1], [zone_0]
    for k in range(1, DEGREE):
        older = zones[-2:-1]
        scale = (2.0 if older else 1.0) / spectrum_half
        zone_k, sums, *gave = call(
            functools.partial(zone_body, bool(older), scale),
            (zone, sums_of, give, give),
            (sums, *got, shift_zone, zones[-1], *older, partial, border, border_diagonal), work // 6,
        )
        zones.append(zone_k)
        got = exchange(*gave, n_state, n_space)
        ins = (zone_k, inners[-1], inners[-2], shift_inner, border)
        if k == 1:
            square, diagonal, inner_k, partial = call(
                square_body, (SHAPE((inside, inside), BF16), line, inner, sums_of), (*ins, hot, wide),
                2 * inside * inside * cells * nodes,
            )
        else:
            inner_k, partial = call(inner_body, (inner, sums_of), (*ins, square, diagonal), work)
        inners.append(inner_k)
    distances = range(1, n_state)
    blocks = [inner_k] + [across(inner_k, "state", d) for d in distances]
    zone_k, rims, energy_rim, *gave = call(
        energy_zone_body,
        (zone, give, SHAPE((count, 2 * rim), F32), give_rim, give_rim),
        (sums, *got, shift_zone, zones[-1], zones[-2], partial, border, border_diagonal), work // 6,
    )
    rim_blocks = [rims] + [across(rims, "state", d) for d in distances]
    got = exchange(*gave, n_state, n_space)
    energy_inner, filtered = call(
        energy_inner_body, (inner, SHAPE((count, owned), BF16)),
        (zone_k, inner_k, shift_inner, border, square, diagonal), work // 4,
    )
    total_states = count * n_state
    columns = total_states // n_space
    chips = n_space // 2
    mine, give_half = call(
        functools.partial(project_body, 1.0 / (owned * n_space)),
        (SHAPE((chips, 2, columns, 2 * count), BF16), SHAPE((chips, columns, 2 * count), BF16)),
        (energy_rim, *got, energy_inner, *(b for pair in zip(blocks, rim_blocks) for b in pair)),
        4 * total_states * count * owned,
        scratch=[pltpu.VMEM((total_states, owned), BF16), pltpu.VMEM((2 * count, owned), BF16)],
    )
    got_half = swap(give_half, n_state, n_space, 0)
    piece = SHAPE((columns, 2 * count), BF16)
    pieces = call(halve_body, (piece,) * chips, (mine, got_half), 0)
    pieces = [pieces[0]] + [across(p, "space", 2 * d) for d, p in enumerate(pieces) if d]
    turned = SHAPE((columns, count), F32)
    intersection, projected = call(
        functools.partial(final_body, count), (turned, turned), tuple(pieces), 0
    )
    return filtered, intersection.T, projected.T


def solution(mesh):
    return jax.shard_map(
        program,
        mesh=mesh,
        in_specs=(P("state", "space"), P("space", None, None), P("space", None), P("space")),
        out_specs=(P("state", "space"), P("state", "space"), P("state", "space")),
        check_vma=False,
    )
```

profile of v0, /device:TPU:0, one launch (start us, length us, event | category | flops | bytes accessed | tf_op | source)
XLA Modules:
  0.0 50.3 jit_solution(5332631073590075613)
XLA Ops:
  2.1 2.6 %collective-permute-start.1 = (bf16[112,128]{1,0:T(8,128)(2,1)S(1)}, bf16[112,128]{1,0:T(8,128)(2,1)S(1)}, u32[]{:S(2)}, u32[]{:S(2)}) collective-permute-start(bf16[112,128]{1,0:T(8,128)(2,1)S(1)} %get-tuple-element.56), channel_id=1, source_target_pairs={{0,8},{1,2},{2,1},{3,4},{4,3},{5,6},{6,5},{7,15},{8,0},{9,10},{10,... | collective-permute-start | bytes 86024 | tf_op jit(solution)/shard_map/ppermute | solution.py:310
  4.6 2.8 %shard_map.68 = (bf16[1280,1024]{1,0:T(8,128)(2,1)S(1)}, bf16[1280,1024]{1,0:T(8,128)(2,1)S(1)}) custom-call(s32[2,512]{1,0:T(2,128)S(1)} %get-tuple-element.57.index_ref, bf16[2,512,512]{2,1,0:T(8,128)(2,1)} %cells_ref.1), custom_call_target="tpu_custom_call" | custom-call | flops 1342177280 | bytes 4194304 | tf_op jit(solution)/shard_map/pallas_call | solution.py:26
  7.4 0.9 %shard_map.69 = (bf16[96,768]{1,0:T(8,128)(2,1)S(1)}, bf16[96,512]{1,0:T(8,128)(2,1)S(1)}, f32[1,768]{1,0:T(1,128)S(1)}, f32[1,512]{1,0:T(1,128)S(1)}, bf16[96,1...) custom-call(bf16[96,1024]{1,0:T(8,128)(2,1)S(1)} %copy-done, ...), custom_call_target="tpu_custom_call" | custom-call | flops 314572800 | bytes 4194304 | tf_op jit(solution)/shard_map/pallas_call | solution.py:26
  8.6 1.5 %collective-permute-start.3 = (bf16[96,256]{1,0:T(8,128)(2,1)S(1)}, bf16[96,256]{1,0:T(8,128)(2,1)S(1)}, u32[]{:S(2)}, u32[]{:S(2)}) collective-permute-start(bf16[96,256]{1,0:T(8,128)(2,1)S(1)} %get-tuple-element.62), channel_id=1, source_target_pairs={{0,8},{1,2},{2,1},{3,4},{4,3},{5,6},{6,5},{7,15},{8,0},{9,10},{10,... | collective-permute-start | bytes 147464 | tf_op jit(solution)/shard_map/ppermute | solution.py:310
  10.1 2.1 %shard_map.70 = (bf16[96,768]{1,0:T(8,128)(2,1)S(1)}, bf16[1280,512]{1,0:T(8,128)(2,1)S(1)}, f32[1,512]{1,0:T(1,128)S(1)}, f32[96,512]{1,0:T(8,128)S(1)}) custom-call(bf16[96,768]{1,0:T(8,128)(2,1)S(1)} %get-tuple-element.65.inner_ref.old_ref, bf16[96,1024]{1,0:T(8,128)(2,1)S(1)} %get-tuple-element.66.picked_ref, ...), custom_call_target="tpu_custom_call" | custom-call | flops 1342177280 | bytes 4194304 | tf_op jit(solution)/shard_map/pallas_call | solution.py:26
  13.0 1.5 %collective-permute-start.5 = (bf16[96,256]{1,0:T(8,128)(2,1)S(1)}, bf16[96,256]{1,0:T(8,128)(2,1)S(1)}, u32[]{:S(2)}, u32[]{:S(2)}) collective-permute-start(bf16[96,256]{1,0:T(8,128)(2,1)S(1)} %get-tuple-element.73), channel_id=1, source_target_pairs={{0,8},{1,2},{2,1},{3,4},{4,3},{5,6},{6,5},{7,15},{8,0},{9,10},{10,... | collective-permute-start | bytes 147464 | tf_op jit(solution)/shard_map/ppermute | solution.py:310
  14.6 2.4 %shard_map.72 = (bf16[768,768]{1,0:T(8,128)(2,1)S(1)}, f32[1,768]{1,0:T(1,128)S(1)}, bf16[96,768]{1,0:T(8,128)(2,1)S(1)}, f32[96,512]{1,0:T(8,128)S(1)}) custom-call(bf16[96,512]{1,0:T(8,128)(2,1)S(1)} %get-tuple-element.74.zone_ref.mid_ref.rest_0_, bf16[96,768]{1,0:T(8,128)(2,1)S(1)} %get-tuple-element.75.inner_ref.old_ref, ...), custom_call_target="tpu_custom_call" | custom-call | flops 1207959552 | bytes 4194304 | tf_op jit(solution)/shard_map/pallas_call | solution.py:26
  17.6 1.5 %collective-permute-start.7 = (bf16[96,256]{1,0:T(8,128)(2,1)S(1)}, bf16[96,256]{1,0:T(8,128)(2,1)S(1)}, u32[]{:S(2)}, u32[]{:S(2)}) collective-permute-start(bf16[96,256]{1,0:T(8,128)(2,1)S(1)} %get-tuple-element.79), channel_id=1, source_target_pairs={{0,8},{1,2},{2,1},{3,4},{4,3},{5,6},{6,5},{7,15},{8,0},{9,10},{10,... | collective-permute-start | bytes 147464 | tf_op jit(solution)/shard_map/ppermute | solution.py:310
  19.1 0.9 %shard_map.74 = (bf16[96,768]{1,0:T(8,128)(2,1)S(1)}, f32[96,512]{1,0:T(8,128)S(1)}) custom-call(bf16[96,512]{1,0:T(8,128)(2,1)S(1)} %get-tuple-element.80.zone_ref.mid_ref.old_ref, bf16[96,768]{1,0:T(8,128)(2,1)S(1)} %get-tuple-element.81.inner_ref.old_ref, bf16[96,768]{1,0:T(8,128)(2,1)S(1)} %get-tuple-element.75.inner_ref.old_ref, ...), custom_call_target="tpu_custom_call" | custom-call | flops 314572800 | bytes 4194304 | tf_op jit(solution)/shard_map/pallas_call | solution.py:26
  20.0 1.7 %collective-permute-done.7.got_b_ref = bf16[96,256]{1,0:T(8,128)(2,1)S(1)} collective-permute-done((bf16[96,256]{1,0:T(8,128)(2,1)S(1)}, bf16[96,256]{1,0:T(8,128)(2,1)S(1)}, u32[]{:S(2)}, u32[]{:S(2)}) %collective-permute-start.7) | collective-permute-done | bytes 49184 | tf_op jit(solution)/shard_map/ppermute | solution.py:310
  22.1 1.5 %collective-permute-start.9 = (bf16[96,256]{1,0:T(8,128)(2,1)S(1)}, bf16[96,256]{1,0:T(8,128)(2,1)S(1)}, u32[]{:S(2)}, u32[]{:S(2)}) collective-permute-start(bf16[96,256]{1,0:T(8,128)(2,1)S(1)} %get-tuple-element.87), channel_id=1, source_target_pairs={{0,8},{1,2},{2,1},{3,4},{4,3},{5,6},{6,5},{7,15},{8,0},{9,10},{10,... | collective-permute-start | bytes 147464 | tf_op jit(solution)/shard_map/ppermute | solution.py:310
  23.6 0.9 %shard_map.76 = (bf16[96,768]{1,0:T(8,128)(2,1)S(1)}, f32[96,512]{1,0:T(8,128)S(1)}) custom-call(bf16[96,512]{1,0:T(8,128)(2,1)S(1)} %get-tuple-element.88.zone_ref.mid_ref, bf16[96,768]{1,0:T(8,128)(2,1)S(1)} %get-tuple-element.89.inner_ref, bf16[96,768]{1,0:T(8,128)(2,1)S(1)} %get-tuple-element.81.inner_ref.old_ref, ...), custom_call_target="tpu_custom_call" | custom-call | flops 314572800 | bytes 4194304 | tf_op jit(solution)/shard_map/pallas_call | solution.py:26
  25.1 1.5 %collective-permute-start.14 = (bf16[96,768]{1,0:T(8,128)(2,1)S(1)}, bf16[96,768]{1,0:T(8,128)(2,1)S(1)}, u32[]{:S(2)}, u32[]{:S(2)}) collective-permute-start(bf16[96,768]{1,0:T(8,128)(2,1)S(1)} %get-tuple-element.92.inner_ref.refs_0_), channel_id=1, source_target_pairs={{0,16},{8,24},{16,0},{24,8},{1,17},{9,25},{17,1},{25,9},{2,18},{10... | collective-permute-start | bytes 442376 | tf_op jit(solution)/shard_map/ppermute | solution.py:320
  26.6 1.4 %collective-permute-start.16 = (bf16[96,768]{1,0:T(8,128)(2,1)S(1)}, bf16[96,768]{1,0:T(8,128)(2,1)S(1)}, u32[]{:S(2)}, u32[]{:S(2)}) collective-permute-start(bf16[96,768]{1,0:T(8,128)(2,1)S(1)} %get-tuple-element.92.inner_ref.refs_0_), channel_id=1, source_target_pairs={{0,24},{8,16},{16,8},{24,0},{1,25},{9,17},{17,9},{25,1},{2,26},{10... | collective-permute-start | bytes 442376 | tf_op jit(solution)/shard_map/ppermute | solution.py:320
  29.6 0.9 %collective-permute-start.11 = (bf16[96,128]{1,0:T(8,128)(2,1)S(1)}, bf16[96,128]{1,0:T(8,128)(2,1)S(1)}, u32[]{:S(2)}, u32[]{:S(2)}) collective-permute-start(bf16[96,128]{1,0:T(8,128)(2,1)S(1)} %get-tuple-element.96), channel_id=1, source_target_pairs={{0,8},{1,2},{2,1},{3,4},{4,3},{5,6},{6,5},{7,15},{8,0},{9,10},{10,... | collective-permute-start | bytes 73736 | tf_op jit(solution)/shard_map/ppermute | solution.py:310
  30.5 3.7 %collective-permute-done.11.got_b_ref = bf16[96,128]{1,0:T(8,128)(2,1)S(1)} collective-permute-done((bf16[96,128]{1,0:T(8,128)(2,1)S(1)}, bf16[96,128]{1,0:T(8,128)(2,1)S(1)}, u32[]{:S(2)}, u32[]{:S(2)}) %collective-permute-start.11) | collective-permute-done | bytes 24608 | tf_op jit(solution)/shard_map/ppermute | solution.py:310
  34.2 1.5 %collective-permute-start.15 = (bf16[96,256]{1,0:T(8,128)(2,1)S(1)}, bf16[96,256]{1,0:T(8,128)(2,1)S(1)}, u32[]{:S(2)}, u32[]{:S(2)}) collective-permute-start(bf16[96,256]{1,0:T(8,128)(2,1)S(1)} %get-tuple-element.98.refs_1_), channel_id=1, source_target_pairs={{0,16},{8,24},{16,0},{24,8},{1,17},{9,25},{17,1},{25,9},{2,18},{10... | collective-permute-start | bytes 147464 | tf_op jit(solution)/shard_map/ppermute | solution.py:320
  35.7 1.1 %collective-permute-start.17 = (bf16[96,256]{1,0:T(8,128)(2,1)S(1)}, bf16[96,256]{1,0:T(8,128)(2,1)S(1)}, u32[]{:S(2)}, u32[]{:S(2)}) collective-permute-start(bf16[96,256]{1,0:T(8,128)(2,1)S(1)} %get-tuple-element.98.refs_1_), channel_id=1, source_target_pairs={{0,24},{8,16},{16,8},{24,0},{1,25},{9,17},{17,9},{25,1},{2,26},{10... | collective-permute-start | bytes 147464 | tf_op jit(solution)/shard_map/ppermute | solution.py:320
  36.8 1.1 %shard_map.78 = (bf16[96,768]{1,0:T(8,128)(2,1)S(1)}, bf16[96,1024]{1,0:T(8,128)(2,1)}) custom-call(bf16[96,512]{1,0:T(8,128)(2,1)S(1)} %get-tuple-element.91.zone_ref, bf16[96,768]{1,0:T(8,128)(2,1)S(1)} %get-tuple-element.92.inner_ref.refs_0_, f32[1,768]{1,0:T(1,128)S(1)} %get-tuple-element.67.shift_inner_ref, ...), custom_call_target="tpu_custom_call" | custom-call | flops 78643200 | bytes 4194304 | tf_op jit(solution)/shard_map/pallas_call | solution.py:26
  38.8 1.9 %collective-permute-done.17.refs_7_ = bf16[96,256]{1,0:T(8,128)(2,1)S(1)} collective-permute-done((bf16[96,256]{1,0:T(8,128)(2,1)S(1)}, bf16[96,256]{1,0:T(8,128)(2,1)S(1)}, u32[]{:S(2)}, u32[]{:S(2)}) %collective-permute-start.17) | collective-permute-done | bytes 49184 | tf_op jit(solution)/shard_map/ppermute | solution.py:320
  41.2 1.3 %collective-permute-done.18.got_ref = bf16[4,48,192]{2,1,0:T(8,128)(2,1)S(1)} collective-permute-done((bf16[4,48,192]{2,1,0:T(8,128)(2,1)S(1)}, bf16[4,48,192]{2,1,0:T(8,128)(2,1)S(1)}, u32[]{:S(2)}, u32[]{:S(2)}) %collective-permute-start.18) | collective-permute-done | bytes 73760 | tf_op jit(solution)/shard_map/ppermute | solution.py:310
  42.6 1.4 %collective-permute-start.20 = (bf16[48,192]{1,0:T(8,128)(2,1)S(1)}, bf16[48,192]{1,0:T(8,128)(2,1)S(1)}, u32[]{:S(2)}, u32[]{:S(2)}) collective-permute-start(bf16[48,192]{1,0:T(8,128)(2,1)S(1)} %get-tuple-element.103), channel_id=1, source_target_pairs={{0,4},{1,5},{2,6},{3,7},{4,0},{5,1},{6,2},{7,3},{8,12},{9,13},{10,... | collective-permute-start | bytes 55304 | tf_op jit(solution)/shard_map/ppermute | solution.py:320
  44.0 3.0 %collective-permute-start.21 = (bf16[48,192]{1,0:T(8,128)(2,1)S(1)}, bf16[48,192]{1,0:T(8,128)(2,1)S(1)}, u32[]{:S(2)}, u32[]{:S(2)}) collective-permute-start(bf16[48,192]{1,0:T(8,128)(2,1)S(1)} %get-tuple-element.104), channel_id=1, source_target_pairs={{0,6},{1,7},{2,4},{3,5},{4,2},{5,3},{6,0},{7,1},{8,14},{9,15},{10,... | collective-permute-start | bytes 55304 | tf_op jit(solution)/shard_map/ppermute | solution.py:320
  47.4 2.2 %collective-permute-done.21.refs_3_ = bf16[48,192]{1,0:T(8,128)(2,1)S(1)} collective-permute-done((bf16[48,192]{1,0:T(8,128)(2,1)S(1)}, bf16[48,192]{1,0:T(8,128)(2,1)S(1)}, u32[]{:S(2)}, u32[]{:S(2)}) %collective-permute-start.21) | collective-permute-done | bytes 18464 | tf_op jit(solution)/shard_map/ppermute | solution.py:320
  (39 shorter events, 8.2 us)
Async XLA Ops:
  0.6 6.8 %copy-start = (bf16[96,1024]{1,0:T(8,128)(2,1)S(1)}, bf16[96,1024]{1,0:T(8,128)(2,1)}, u32[]{:S(2)}) copy-start(bf16[96,1024]{1,0:T(8,128)(2,1)} %states_ref.3) | copy-start | bytes 589828
  0.6 6.8 %copy-start.1 = (f32[1024]{0:T(1024)S(1)}, f32[1024]{0:T(1024)}, u32[]{:S(2)}) copy-start(f32[1024]{0:T(1024)} %param.7) | copy-start | bytes 12292
  1.5 5.9 %collective-permute-start = (bf16[112,128]{1,0:T(8,128)(2,1)S(1)}, bf16[112,128]{1,0:T(8,128)(2,1)S(1)}, u32[]{:S(2)}, u32[]{:S(2)}) collective-permute-start(bf16[112,128]{1,0:T(8,128)(2,1)S(1)} %get-tuple-element.55), channel_id=1, source_target_pairs={{0,1},{1,0},{2,3},{3,2},{4,5},{5,4},{6,7},{7,6},{8,9},{9,8},{10,11... | collective-permute-start | bytes 86024 | tf_op jit(solution)/shard_map/ppermute | solution.py:310
  2.1 5.3 %collective-permute-start.1 = (bf16[112,128]{1,0:T(8,128)(2,1)S(1)}, bf16[112,128]{1,0:T(8,128)(2,1)S(1)}, u32[]{:S(2)}, u32[]{:S(2)}) collective-permute-start(bf16[112,128]{1,0:T(8,128)(2,1)S(1)} %get-tuple-element.56), channel_id=1, source_target_pairs={{0,8},{1,2},{2,1},{3,4},{4,3},{5,6},{6,5},{7,15},{8,0},{9,10},{10,... | collective-permute-start | bytes 86024 | tf_op jit(solution)/shard_map/ppermute | solution.py:310
  8.3 3.9 %collective-permute-start.2 = (bf16[96,256]{1,0:T(8,128)(2,1)S(1)}, bf16[96,256]{1,0:T(8,128)(2,1)S(1)}, u32[]{:S(2)}, u32[]{:S(2)}) collective-permute-start(bf16[96,256]{1,0:T(8,128)(2,1)S(1)} %get-tuple-element.61), channel_id=1, source_target_pairs={{0,1},{1,0},{2,3},{3,2},{4,5},{5,4},{6,7},{7,6},{8,9},{9,8},{10,11... | collective-permute-start | bytes 147464 | tf_op jit(solution)/shard_map/ppermute | solution.py:310
  8.6 4.1 %collective-permute-start.3 = (bf16[96,256]{1,0:T(8,128)(2,1)S(1)}, bf16[96,256]{1,0:T(8,128)(2,1)S(1)}, u32[]{:S(2)}, u32[]{:S(2)}) collective-permute-start(bf16[96,256]{1,0:T(8,128)(2,1)S(1)} %get-tuple-element.62), channel_id=1, source_target_pairs={{0,8},{1,2},{2,1},{3,4},{4,3},{5,6},{6,5},{7,15},{8,0},{9,10},{10,... | collective-permute-start | bytes 147464 | tf_op jit(solution)/shard_map/ppermute | solution.py:310
  12.9 4.0 %collective-permute-start.4 = (bf16[96,256]{1,0:T(8,128)(2,1)S(1)}, bf16[96,256]{1,0:T(8,128)(2,1)S(1)}, u32[]{:S(2)}, u32[]{:S(2)}) collective-permute-start(bf16[96,256]{1,0:T(8,128)(2,1)S(1)} %get-tuple-element.72), channel_id=1, source_target_pairs={{0,1},{1,0},{2,3},{3,2},{4,5},{5,4},{6,7},{7,6},{8,9},{9,8},{10,11... | collective-permute-start | bytes 147464 | tf_op jit(solution)/shard_map/ppermute | solution.py:310
  13.0 4.1 %collective-permute-start.5 = (bf16[96,256]{1,0:T(8,128)(2,1)S(1)}, bf16[96,256]{1,0:T(8,128)(2,1)S(1)}, u32[]{:S(2)}, u32[]{:S(2)}) collective-permute-start(bf16[96,256]{1,0:T(8,128)(2,1)S(1)} %get-tuple-element.73), channel_id=1, source_target_pairs={{0,8},{1,2},{2,1},{3,4},{4,3},{5,6},{6,5},{7,15},{8,0},{9,10},{10,... | collective-permute-start | bytes 147464 | tf_op jit(solution)/shard_map/ppermute | solution.py:310
  17.4 2.6 %collective-permute-start.6 = (bf16[96,256]{1,0:T(8,128)(2,1)S(1)}, bf16[96,256]{1,0:T(8,128)(2,1)S(1)}, u32[]{:S(2)}, u32[]{:S(2)}) collective-permute-start(bf16[96,256]{1,0:T(8,128)(2,1)S(1)} %get-tuple-element.78), channel_id=1, source_target_pairs={{0,1},{1,0},{2,3},{3,2},{4,5},{5,4},{6,7},{7,6},{8,9},{9,8},{10,11... | collective-permute-start | bytes 147464 | tf_op jit(solution)/shard_map/ppermute | solution.py:310
  17.6 4.1 %collective-permute-start.7 = (bf16[96,256]{1,0:T(8,128)(2,1)S(1)}, bf16[96,256]{1,0:T(8,128)(2,1)S(1)}, u32[]{:S(2)}, u32[]{:S(2)}) collective-permute-start(bf16[96,256]{1,0:T(8,128)(2,1)S(1)} %get-tuple-element.79), channel_id=1, source_target_pairs={{0,8},{1,2},{2,1},{3,4},{4,3},{5,6},{6,5},{7,15},{8,0},{9,10},{10,... | collective-permute-start | bytes 147464 | tf_op jit(solution)/shard_map/ppermute | solution.py:310
  21.9 6.1 %collective-permute-start.8 = (bf16[96,256]{1,0:T(8,128)(2,1)S(1)}, bf16[96,256]{1,0:T(8,128)(2,1)S(1)}, u32[]{:S(2)}, u32[]{:S(2)}) collective-permute-start(bf16[96,256]{1,0:T(8,128)(2,1)S(1)} %get-tuple-element.86), channel_id=1, source_target_pairs={{0,1},{1,0},{2,3},{3,2},{4,5},{5,4},{6,7},{7,6},{8,9},{9,8},{10,11... | collective-permute-start | bytes 147464 | tf_op jit(solution)/shard_map/ppermute | solution.py:310
  22.1 6.0 %collective-permute-start.9 = (bf16[96,256]{1,0:T(8,128)(2,1)S(1)}, bf16[96,256]{1,0:T(8,128)(2,1)S(1)}, u32[]{:S(2)}, u32[]{:S(2)}) collective-permute-start(bf16[96,256]{1,0:T(8,128)(2,1)S(1)} %get-tuple-element.87), channel_id=1, source_target_pairs={{0,8},{1,2},{2,1},{3,4},{4,3},{5,6},{6,5},{7,15},{8,0},{9,10},{10,... | collective-permute-start | bytes 147464 | tf_op jit(solution)/shard_map/ppermute | solution.py:310
  24.5 16.2 %collective-permute-start.12 = (bf16[96,768]{1,0:T(8,128)(2,1)S(1)}, bf16[96,768]{1,0:T(8,128)(2,1)S(1)}, u32[]{:S(2)}, u32[]{:S(2)}) collective-permute-start(bf16[96,768]{1,0:T(8,128)(2,1)S(1)} %get-tuple-element.92.inner_ref.refs_0_), channel_id=1, source_target_pairs={{0,8},{8,0},{16,24},{24,16},{1,9},{9,1},{17,25},{25,17},{2,10},{10... | collective-permute-start | bytes 442376 | tf_op jit(solution)/shard_map/ppermute | solution.py:320
  25.1 15.6 %collective-permute-start.14 = (bf16[96,768]{1,0:T(8,128)(2,1)S(1)}, bf16[96,768]{1,0:T(8,128)(2,1)S(1)}, u32[]{:S(2)}, u32[]{:S(2)}) collective-permute-start(bf16[96,768]{1,0:T(8,128)(2,1)S(1)} %get-tuple-element.92.inner_ref.refs_0_), channel_id=1, source_target_pairs={{0,16},{8,24},{16,0},{24,8},{1,17},{9,25},{17,1},{25,9},{2,18},{10... | collective-permute-start | bytes 442376 | tf_op jit(solution)/shard_map/ppermute | solution.py:320
  26.6 14.1 %collective-permute-start.16 = (bf16[96,768]{1,0:T(8,128)(2,1)S(1)}, bf16[96,768]{1,0:T(8,128)(2,1)S(1)}, u32[]{:S(2)}, u32[]{:S(2)}) collective-permute-start(bf16[96,768]{1,0:T(8,128)(2,1)S(1)} %get-tuple-element.92.inner_ref.refs_0_), channel_id=1, source_target_pairs={{0,24},{8,16},{16,8},{24,0},{1,25},{9,17},{17,9},{25,1},{2,26},{10... | collective-permute-start | bytes 442376 | tf_op jit(solution)/shard_map/ppermute | solution.py:320
  28.3 1.3 %collective-permute-start.10 = (bf16[96,128]{1,0:T(8,128)(2,1)S(1)}, bf16[96,128]{1,0:T(8,128)(2,1)S(1)}, u32[]{:S(2)}, u32[]{:S(2)}) collective-permute-start(bf16[96,128]{1,0:T(8,128)(2,1)S(1)} %get-tuple-element.95), channel_id=1, source_target_pairs={{0,1},{1,0},{2,3},{3,2},{4,5},{5,4},{6,7},{7,6},{8,9},{9,8},{10,11... | collective-permute-start | bytes 73736 | tf_op jit(solution)/shard_map/ppermute | solution.py:310
  28.4 7.3 %collective-permute-start.13 = (bf16[96,256]{1,0:T(8,128)(2,1)S(1)}, bf16[96,256]{1,0:T(8,128)(2,1)S(1)}, u32[]{:S(2)}, u32[]{:S(2)}) collective-permute-start(bf16[96,256]{1,0:T(8,128)(2,1)S(1)} %get-tuple-element.98.refs_1_), channel_id=1, source_target_pairs={{0,8},{8,0},{16,24},{24,16},{1,9},{9,1},{17,25},{25,17},{2,10},{10... | collective-permute-start | bytes 147464 | tf_op jit(solution)/shard_map/ppermute | solution.py:320
  29.6 4.6 %collective-permute-start.11 = (bf16[96,128]{1,0:T(8,128)(2,1)S(1)}, bf16[96,128]{1,0:T(8,128)(2,1)S(1)}, u32[]{:S(2)}, u32[]{:S(2)}) collective-permute-start(bf16[96,128]{1,0:T(8,128)(2,1)S(1)} %get-tuple-element.96), channel_id=1, source_target_pairs={{0,8},{1,2},{2,1},{3,4},{4,3},{5,6},{6,5},{7,15},{8,0},{9,10},{10,... | collective-permute-start | bytes 73736 | tf_op jit(solution)/shard_map/ppermute | solution.py:310
  34.2 4.6 %collective-permute-start.15 = (bf16[96,256]{1,0:T(8,128)(2,1)S(1)}, bf16[96,256]{1,0:T(8,128)(2,1)S(1)}, u32[]{:S(2)}, u32[]{:S(2)}) collective-permute-start(bf16[96,256]{1,0:T(8,128)(2,1)S(1)} %get-tuple-element.98.refs_1_), channel_id=1, source_target_pairs={{0,16},{8,24},{16,0},{24,8},{1,17},{9,25},{17,1},{25,9},{2,18},{10... | collective-permute-start | bytes 147464 | tf_op jit(solution)/shard_map/ppermute | solution.py:320
  35.7 5.0 %collective-permute-start.17 = (bf16[96,256]{1,0:T(8,128)(2,1)S(1)}, bf16[96,256]{1,0:T(8,128)(2,1)S(1)}, u32[]{:S(2)}, u32[]{:S(2)}) collective-permute-start(bf16[96,256]{1,0:T(8,128)(2,1)S(1)} %get-tuple-element.98.refs_1_), channel_id=1, source_target_pairs={{0,24},{8,16},{16,8},{24,0},{1,25},{9,17},{17,9},{25,1},{2,26},{10... | collective-permute-start | bytes 147464 | tf_op jit(solution)/shard_map/ppermute | solution.py:320
  41.1 1.4 %collective-permute-start.18 = (bf16[4,48,192]{2,1,0:T(8,128)(2,1)S(1)}, bf16[4,48,192]{2,1,0:T(8,128)(2,1)S(1)}, u32[]{:S(2)}, u32[]{:S(2)}) collective-permute-start(bf16[4,48,192]{2,1,0:T(8,128)(2,1)S(1)} %get-tuple-element.100), channel_id=1, source_target_pairs={{0,1},{1,0},{2,3},{3,2},{4,5},{5,4},{6,7},{7,6},{8,9},{9,8},{10,11... | collective-permute-start | bytes 221192 | tf_op jit(solution)/shard_map/ppermute | solution.py:310
  42.5 4.5 %collective-permute-start.19 = (bf16[48,192]{1,0:T(8,128)(2,1)S(1)}, bf16[48,192]{1,0:T(8,128)(2,1)S(1)}, u32[]{:S(2)}, u32[]{:S(2)}) collective-permute-start(bf16[48,192]{1,0:T(8,128)(2,1)S(1)} %get-tuple-element.102), channel_id=1, source_target_pairs={{0,2},{1,3},{2,0},{3,1},{4,6},{5,7},{6,4},{7,5},{8,10},{9,11},{10,... | collective-permute-start | bytes 55304 | tf_op jit(solution)/shard_map/ppermute | solution.py:320
  42.6 4.8 %collective-permute-start.20 = (bf16[48,192]{1,0:T(8,128)(2,1)S(1)}, bf16[48,192]{1,0:T(8,128)(2,1)S(1)}, u32[]{:S(2)}, u32[]{:S(2)}) collective-permute-start(bf16[48,192]{1,0:T(8,128)(2,1)S(1)} %get-tuple-element.103), channel_id=1, source_target_pairs={{0,4},{1,5},{2,6},{3,7},{4,0},{5,1},{6,2},{7,3},{8,12},{9,13},{10,... | collective-permute-start | bytes 55304 | tf_op jit(solution)/shard_map/ppermute | solution.py:320
  44.0 5.6 %collective-permute-start.21 = (bf16[48,192]{1,0:T(8,128)(2,1)S(1)}, bf16[48,192]{1,0:T(8,128)(2,1)S(1)}, u32[]{:S(2)}, u32[]{:S(2)}) collective-permute-start(bf16[48,192]{1,0:T(8,128)(2,1)S(1)} %get-tuple-element.104), channel_id=1, source_target_pairs={{0,6},{1,7},{2,4},{3,5},{4,2},{5,3},{6,0},{7,1},{8,14},{9,15},{10,... | collective-permute-start | bytes 55304 | tf_op jit(solution)/shard_map/ppermute | solution.py:320
where the time goes:
time: 50.5 us; the launch traced here: 50.3 us
  starting transfers between devices  22.2 us (44%)
  Pallas kernels  14 us (28%)
  waiting for transfers between devices  13.3 us (26%)
  between operations  0.82 us (2%)
    pallas_call x15, Pallas kernels, call(): pl.pallas_call(body, out_shape=outs, in_specs=where, out_specs=jax.tree.m...  14 us
    ppermute x9, starting transfers between devices, across(): lax.ppermute(block, axis, [(i, i ^ distance) for i in range(lax.axis_size...  11.2 us
    ppermute x13, starting transfers between devices, swap(): return lax.ppermute(block, ('state', 'space'), route)  10.9 us
    ppermute x13, waiting for transfers between devices, swap(): return lax.ppermute(block, ('state', 'space'), route)  7.93 us
    ppermute x9, waiting for transfers between devices, across(): lax.ppermute(block, axis, [(i, i ^ distance) for i in range(lax.axis_size...  5.4 us
  transfers between devices with their start and end apart: 22, of which 10 were waited for; matrix products, arithmetic and copies ran while one was open for 0% of the time, Pallas kernels for 21%

commit v1 on v0

--- a/solution.py
+++ b/solution.py
@@ -227,26 +227,28 @@
     inner_body(zone_ref, inner_ref, old_ref, shift_inner_ref, border_ref, square_ref, diagonal_ref, next_ref, part_ref)
 
 
-def energy_zone_body(sums_ref, got_a_ref, got_b_ref, shift_zone_ref, mid_ref, old_ref,
-                     part_ref, border_ref, border_diagonal_ref, zone_ref, rim_ref, energy_ref, give_a_ref, give_b_ref):
+def last_zone_body(sums_ref, got_a_ref, got_b_ref, shift_zone_ref, mid_ref, old_ref, zone_ref):
     close_zones(sums_ref, got_a_ref, got_b_ref, shift_zone_ref, mid_ref, old_ref,
                 2.0 / spectrum_half, zone_ref)
-    width = got_a_ref.shape[1]
+
+
+def zone_energy(zone_ref, part_ref, shift_zone_ref, border_ref, border_diagonal_ref, energy_ref):
+    low, high = zone_sums(zone_ref, part_ref, border_ref, border_diagonal_ref)
+    width = low.shape[1]
     rim = width // 2
-    rim_ref[...] = zone_ref[:, rim : width + rim]
-    low, high = zone_sums(zone_ref, part_ref, border_ref, border_diagonal_ref)
-    own = shift_zone_ref[:, rim : width + rim] + spectrum_center
-    own = own * rim_ref[...].astype(F32)
-    energy_ref[:, :rim] = low[:, rim:] + own[:, :rim]
-    energy_ref[:, rim:] = high[:, :rim] + own[:, rim:]
-    hand_out(low[:, :rim], high[:, rim:], give_a_ref, give_b_ref)
-
-
-def energy_inner_body(zone_ref, inner_ref, shift_inner_ref, border_ref, square_ref, diagonal_ref,
-                      energy_ref, filtered_ref):
+    own = (shift_zone_ref[:, rim : width + rim] + spectrum_center) * zone_ref[:, rim : width + rim].astype(F32)
+    energy_ref[:, :rim] = low[:, :rim].astype(energy_ref.dtype)
+    energy_ref[:, rim:width] = (low[:, rim:] + own[:, :rim]).astype(energy_ref.dtype)
+    energy_ref[:, width : width + rim] = (high[:, :rim] + own[:, rim:]).astype(energy_ref.dtype)
+    energy_ref[:, width + rim :] = high[:, rim:].astype(energy_ref.dtype)
+
+
+def energy_body(zone_ref, inner_ref, part_ref, shift_inner_ref, shift_zone_ref,
+                border_ref, border_diagonal_ref, square_ref, diagonal_ref, energy_ref, energy_zone_ref, filtered_ref):
     sums = inner_sums(zone_ref, inner_ref, border_ref, square_ref, diagonal_ref)
     own = (shift_inner_ref[...] + spectrum_center) * inner_ref[...].astype(F32)
     energy_ref[...] = (sums + own).astype(BF16)
+    zone_energy(zone_ref, part_ref, shift_zone_ref, border_ref, border_diagonal_ref, energy_zone_ref)
     width = zone_ref.shape[1] // 2
     rim = width // 2
     owned = filtered_ref.shape[1]
@@ -255,31 +257,57 @@
     filtered_ref[:, owned - rim :] = zone_ref[:, width : width + rim]
 
 
-def project_body(scale, energy_rim_ref, got_a_ref, got_b_ref, energy_inner_ref, *refs):
-    *blocks, out_ref, give_ref, stack_ref, pair_ref = refs
-    count, inside = energy_inner_ref.shape
-    rim = got_a_ref.shape[1]
-    low, high = sort_out(got_a_ref[...], got_b_ref[...])
+def neighbour_body(inner_ref, shift_inner_ref, border_ref, square_ref, diagonal_ref, open_ref, part_ref):
+    inner = inner_ref[...]
+    width = border_ref.shape[1] // 2
+    line = diagonal_ref[...] + (shift_inner_ref[...] + spectrum_center)
+    open_ref[...] = mm(inner, square_ref[...]) + line * inner.astype(F32)
+    part_ref[...] = mm(inner, border_ref[width : width + inner.shape[1], :])
+
+
+def fill_pair(pair_ref, inner_ref, zone_ref):
+    count, inside = inner_ref.shape
+    rim = zone_ref.shape[1] // 4
+    none = jnp.zeros((count, rim), BF16)
+    pair_ref[:count, :inside] = inner_ref[...]
+    pair_ref[:count, inside : inside + rim] = none
+    pair_ref[:count, inside + rim : inside + 3 * rim] = zone_ref[:, rim : 3 * rim]
+    pair_ref[:count, inside + 3 * rim :] = none
+
+
+def project_body(square_of_four, scale, energy_ref, energy_zone_ref, *refs):
+    if square_of_four:
+        (open_ref, part_ref, shift_zone_ref, border_ref, border_diagonal_ref), refs = refs[:5], refs[5:]
+        *blocks, out_ref, give_ref, stack_ref, pair_ref, other_ref, other_zone_ref = refs
+    else:
+        *blocks, out_ref, give_ref, stack_ref, pair_ref = refs
+    count, inside = energy_ref.shape
     group = lax.axis_index("state")
-    groups = len(blocks) // 2
-    for distance in range(groups):
-        inner_ref, rim_ref = blocks[2 * distance : 2 * distance + 2]
-        at = pl.multiple_of((group ^ distance) * count, count)
-        stack_ref[pl.ds(at, count), :inside] = inner_ref[...]
-        stack_ref[pl.ds(at, count), inside:] = rim_ref[...]
-    pair_ref[:count, :inside] = blocks[0][...]
-    pair_ref[:count, inside:] = blocks[1][...]
-    pair_ref[count:, :inside] = energy_inner_ref[...]
-    pair_ref[count:, inside : inside + rim] = (energy_rim_ref[:, :rim] + low).astype(BF16)
-    pair_ref[count:, inside + rim :] = (energy_rim_ref[:, rim:] + high).astype(BF16)
+    odd = is_odd()
+    for place in range(len(blocks) // 2):
+        stack_ref[place * count : (place + 1) * count, :inside] = blocks[2 * place][...]
+        stack_ref[place * count : (place + 1) * count, inside:] = blocks[2 * place + 1][...]
+    fill_pair(pair_ref, blocks[0], blocks[1])
+    pair_ref[count:, :inside] = energy_ref[...]
+    pair_ref[count:, inside:] = energy_zone_ref[...]
     both = mm_nt(stack_ref[...], pair_ref[...]) * scale
-    chips, _, columns, _ = out_ref.shape
-    odd = is_odd()
-    for chip in range(chips):
-        parts = [both[(2 * chip + core) * columns : (2 * chip + core + 1) * columns] for core in range(2)]
+    found = [(place, both[place * count : (place + 1) * count]) for place in range(len(blocks) // 2)]
+    if square_of_four:
+        beside, beside_zone = blocks[2], blocks[3]
+        width = beside_zone.shape[1] // 2
+        fill_pair(other_ref, beside, beside_zone)
+        rest = mm_nt(beside_zone[...], border_ref[width : width + inside, :])
+        other_ref[count:, :inside] = (open_ref[...] + rest).astype(BF16)
+        zone_energy(beside_zone, part_ref, shift_zone_ref, border_ref, border_diagonal_ref, other_zone_ref)
+        other_ref[count:, inside:] = other_zone_ref[...]
+        found.append((3, mm_nt(stack_ref[2 * count :, :], other_ref[...]) * scale))
+    columns = out_ref.shape[2]
+    for distance, block in found:
+        at = group ^ distance
+        parts = [block[:columns], block[columns:]]
         for core in range(2):
-            out_ref[chip, core] = parts[core].astype(BF16)
-        give_ref[chip] = jnp.where(odd, parts[0], parts[1]).astype(BF16)
+            out_ref[at, core] = parts[core].astype(BF16)
+        give_ref[at] = jnp.where(odd, parts[0], parts[1]).astype(BF16)
 
 
 def halve_body(mine_ref, got_ref, *pieces):
@@ -289,10 +317,14 @@
         piece_ref[...] = total.astype(BF16)
 
 
-def final_body(count, *refs):
+def final_body(square_of_four, count, mine_ref, *refs):
     parts, (first_ref, second_ref) = refs[:-2], refs[-2:]
-    total = parts[0][...].astype(F32)
-    for part in parts[1:]:
+    total = mine_ref[...].astype(F32)
+    if square_of_four:
+        made_elsewhere = (lax.axis_index("space") >> 1) == (lax.axis_index("state") ^ 3)
+        total = jnp.where(made_elsewhere, parts[0][...].astype(F32), total)
+        parts = parts[1:]
+    for part in parts:
         total = total + part[...].astype(F32)
     first_ref[...] = total[:, :count]
     second_ref[...] = total[:, count:]
@@ -320,6 +352,17 @@
     return lax.ppermute(block, axis, [(i, i ^ distance) for i in range(lax.axis_size(axis))])
 
 
+def share_out(block, distance, n_state, n_space, square_of_four):
+    route = []
+    for s in range(n_state):
+        for i in range(n_space):
+            to_group, to_chip = s, (i >> 1) ^ distance
+            if square_of_four and (distance == 0 or to_chip == s ^ 3):
+                to_group, to_chip = s ^ 1, to_chip ^ 1
+            route.append((s * n_space + i, to_group * n_space + 2 * to_chip + (i & 1)))
+    return lax.ppermute(block, ("state", "space"), route)
+
+
 def program(states_in, cell_matrices, connectivity, potential):
     count, owned = states_in.shape
     cells, nodes, _ = cell_matrices.shape
@@ -330,7 +373,7 @@
     work = 2 * count * extent * extent
     inner = SHAPE((count, inside), BF16)
     zone, sums_of = SHAPE((count, 4 * rim), BF16), SHAPE((count, 4 * rim), F32)
-    give, give_rim = SHAPE((count, 2 * rim), BF16), SHAPE((count, rim), BF16)
+    give = SHAPE((count, 2 * rim), BF16)
 
     halo = SHAPE((count + 16, rim), BF16)
     *gave, local = call(
@@ -382,38 +425,47 @@
         else:
             inner_k, partial = call(inner_body, (inner, sums_of), (*ins, square, diagonal), work)
         inners.append(inner_k)
-    distances = range(1, n_state)
-    blocks = [inner_k] + [across(inner_k, "state", d) for d in distances]
-    zone_k, rims, energy_rim, *gave = call(
-        energy_zone_body,
-        (zone, give, SHAPE((count, 2 * rim), F32), give_rim, give_rim),
-        (sums, *got, shift_zone, zones[-1], zones[-2], partial, border, border_diagonal), work // 6,
-    )
-    rim_blocks = [rims] + [across(rims, "state", d) for d in distances]
-    got = exchange(*gave, n_state, n_space)
-    energy_inner, filtered = call(
-        energy_inner_body, (inner, SHAPE((count, owned), BF16)),
-        (zone_k, inner_k, shift_inner, border, square, diagonal), work // 4,
-    )
-    total_states = count * n_state
-    columns = total_states // n_space
+    square_of_four = four(n_state, n_space)
+    distances = (1, 2) if square_of_four else range(1, n_state)
+    inner_blocks = [inner_k] + [across(inner_k, "state", d) for d in distances]
+    zone_k = call(
+        last_zone_body, zone, (sums, *got, shift_zone, zones[-1], zones[-2]), 0
+    )
+    zone_blocks = [zone_k] + [across(zone_k, "state", d) for d in distances]
+    energy, energy_zone, filtered = call(
+        energy_body, (inner, zone, SHAPE((count, owned), BF16)),
+        (zone_k, inner_k, partial, shift_inner, shift_zone, border, border_diagonal, square, diagonal), work,
+    )
+    blocks = [b for pair in zip(inner_blocks, zone_blocks) for b in pair]
+    extra = ()
+    scratch = [pltpu.VMEM((len(inner_blocks) * count, extent), BF16), pltpu.VMEM((2 * count, extent), BF16)]
+    if square_of_four:
+        opened, part_x = call(
+            neighbour_body, (SHAPE((count, inside), F32), sums_of),
+            (inner_blocks[1], shift_inner, border, square, diagonal), work // 2,
+        )
+        extra = (opened, part_x, shift_zone, border, border_diagonal)
+        scratch += [pltpu.VMEM((2 * count, extent), BF16), pltpu.VMEM((count, 4 * rim), BF16)]
+    columns = count * n_state // n_space
     chips = n_space // 2
     mine, give_half = call(
-        functools.partial(project_body, 1.0 / (owned * n_space)),
+        functools.partial(project_body, square_of_four, 1.0 / (owned * n_space)),
         (SHAPE((chips, 2, columns, 2 * count), BF16), SHAPE((chips, columns, 2 * count), BF16)),
-        (energy_rim, *got, energy_inner, *(b for pair in zip(blocks, rim_blocks) for b in pair)),
-        4 * total_states * count * owned,
-        scratch=[pltpu.VMEM((total_states, owned), BF16), pltpu.VMEM((2 * count, owned), BF16)],
+        (energy, energy_zone, *extra, *blocks), 4 * count * n_state * count * owned, scratch=scratch,
     )
     got_half = swap(give_half, n_state, n_space, 0)
     piece = SHAPE((columns, 2 * count), BF16)
     pieces = call(halve_body, (piece,) * chips, (mine, got_half), 0)
-    pieces = [pieces[0]] + [across(p, "space", 2 * d) for d, p in enumerate(pieces) if d]
+    shares = [share_out(p, d, n_state, n_space, square_of_four) for d, p in enumerate(pieces) if d or square_of_four]
     turned = SHAPE((columns, count), F32)
     intersection, projected = call(
-        functools.partial(final_body, count), (turned, turned), tuple(pieces), 0
+        functools.partial(final_body, square_of_four, count), (turned, turned), (pieces[0], *shares), 0
     )
     return filtered, intersection.T, projected.T
+
+
+def four(n_state, n_space):
+    return n_state == 4 and n_space == 8
 
 
 def solution(mesh):

time: 50.5 us -> 46.7 us (0.925)
  waiting for transfers between devices: 13.3 us -> 9.88 us
  starting transfers between devices: 22.2 us -> 20.9 us
  Pallas kernels: 14 us -> 15 us
    ppermute x0 -> x4, starting transfers between devices: none -> 5.91 us  [share_out(): return lax.ppermute(block, ('state', 'space'), route)]
    ppermute x9 -> x4, starting transfers between devices: 11.2 us -> 6.17 us  [across(): lax.ppermute(block, axis, [(i, i ^ distance) for i in range(lax.axis_size...]
    ppermute x9 -> x4, waiting for transfers between devices: 5.4 us -> 1.35 us  [across(): lax.ppermute(block, axis, [(i, i ^ distance) for i in range(lax.axis_size...]
    ppermute x13 -> x11, starting transfers between devices: 10.9 us -> 8.79 us  [swap(): return lax.ppermute(block, ('state', 'space'), route)]
    ppermute x0 -> x4, waiting for transfers between devices: none -> 2.06 us  [share_out(): return lax.ppermute(block, ('state', 'space'), route)]
    ppermute x13 -> x11, waiting for transfers between devices: 7.93 us -> 6.46 us  [swap(): return lax.ppermute(block, ('state', 'space'), route)]
    pallas_call x15 -> x16, Pallas kernels: 14 us -> 15 us  [call(): pl.pallas_call(body, out_shape=outs, in_specs=where, out_specs=jax.tree.m...]
  transfers between devices with their start and end apart: 22 -> 19, of which waited for: 10 -> 8; matrix products, arithmetic and copies ran while one was open for 0% -> 0% of each run, Pallas kernels for 21% -> 21%
where the time goes in v1:
time: 46.7 us; the launch traced here: 46.5 us
  starting transfers between devices  20.9 us (45%)
  Pallas kernels  15 us (32%)
  waiting for transfers between devices  9.88 us (21%)
  between operations  0.82 us (2%)
    pallas_call x16, Pallas kernels, call(): pl.pallas_call(body, out_shape=outs, in_specs=where, out_specs=jax.tree.m...  15 us
    ppermute x11, starting transfers between devices, swap(): return lax.ppermute(block, ('state', 'space'), route)  8.79 us
    ppermute x11, waiting for transfers between devices, swap(): return lax.ppermute(block, ('state', 'space'), route)  6.46 us
    ppermute x4, starting transfers between devices, across(): lax.ppermute(block, axis, [(i, i ^ distance) for i in range(lax.axis_size...  6.17 us
    ppermute x4, starting transfers between devices, share_out(): return lax.ppermute(block, ('state', 'space'), route)  5.91 us
    ppermute x4, waiting for transfers between devices, share_out(): return lax.ppermute(block, ('state', 'space'), route)  2.06 us
    ppermute x4, waiting for transfers between devices, across(): lax.ppermute(block, axis, [(i, i ^ distance) for i in range(lax.axis_size...  1.35 us
  transfers between devices with their start and end apart: 19, of which 8 were waited for; matrix products, arithmetic and copies ran while one was open for 0% of the time, Pallas kernels for 21%

profile of v1, /device:TPU:0, one launch (start us, length us, event | category | flops | bytes accessed | tf_op | source)
XLA Modules:
  0.0 46.5 jit_solution(11970876514857595951)
XLA Ops:
  2.1 2.6 %collective-permute-start.1 = (bf16[112,128]{1,0:T(8,128)(2,1)S(1)}, bf16[112,128]{1,0:T(8,128)(2,1)S(1)}, u32[]{:S(2)}, u32[]{:S(2)}) collective-permute-start(bf16[112,128]{1,0:T(8,128)(2,1)S(1)} %get-tuple-element.54), channel_id=1, source_target_pairs={{0,8},{1,2},{2,1},{3,4},{4,3},{5,6},{6,5},{7,15},{8,0},{9,10},{10,... | collective-permute-start | bytes 86024 | tf_op jit(solution)/shard_map/ppermute | solution.py:342
  4.6 2.8 %shard_map.68 = (bf16[1280,1024]{1,0:T(8,128)(2,1)S(1)}, bf16[1280,1024]{1,0:T(8,128)(2,1)S(1)}) custom-call(s32[2,512]{1,0:T(2,128)S(1)} %get-tuple-element.55.index_ref, bf16[2,512,512]{2,1,0:T(8,128)(2,1)} %cells_ref.1), custom_call_target="tpu_custom_call" | custom-call | flops 1342177280 | bytes 4194304 | tf_op jit(solution)/shard_map/pallas_call | solution.py:26
  7.4 0.9 %shard_map.69 = (bf16[96,768]{1,0:T(8,128)(2,1)S(1)}, bf16[96,512]{1,0:T(8,128)(2,1)S(1)}, f32[1,768]{1,0:T(1,128)S(1)}, f32[1,512]{1,0:T(1,128)S(1)}, bf16[96,1...) custom-call(bf16[96,1024]{1,0:T(8,128)(2,1)S(1)} %copy-done, ...), custom_call_target="tpu_custom_call" | custom-call | flops 314572800 | bytes 4194304 | tf_op jit(solution)/shard_map/pallas_call | solution.py:26
  8.6 1.5 %collective-permute-start.3 = (bf16[96,256]{1,0:T(8,128)(2,1)S(1)}, bf16[96,256]{1,0:T(8,128)(2,1)S(1)}, u32[]{:S(2)}, u32[]{:S(2)}) collective-permute-start(bf16[96,256]{1,0:T(8,128)(2,1)S(1)} %get-tuple-element.60), channel_id=1, source_target_pairs={{0,8},{1,2},{2,1},{3,4},{4,3},{5,6},{6,5},{7,15},{8,0},{9,10},{10,... | collective-permute-start | bytes 147464 | tf_op jit(solution)/shard_map/ppermute | solution.py:342
  10.1 2.1 %shard_map.70 = (bf16[96,768]{1,0:T(8,128)(2,1)S(1)}, bf16[1280,512]{1,0:T(8,128)(2,1)S(1)}, f32[1,512]{1,0:T(1,128)S(1)}, f32[96,512]{1,0:T(8,128)S(1)}) custom-call(bf16[96,768]{1,0:T(8,128)(2,1)S(1)} %get-tuple-element.63.inner_ref.old_ref, bf16[96,1024]{1,0:T(8,128)(2,1)S(1)} %get-tuple-element.64.picked_ref, ...), custom_call_target="tpu_custom_call" | custom-call | flops 1342177280 | bytes 4194304 | tf_op jit(solution)/shard_map/pallas_call | solution.py:26
  13.0 1.5 %collective-permute-start.5 = (bf16[96,256]{1,0:T(8,128)(2,1)S(1)}, bf16[96,256]{1,0:T(8,128)(2,1)S(1)}, u32[]{:S(2)}, u32[]{:S(2)}) collective-permute-start(bf16[96,256]{1,0:T(8,128)(2,1)S(1)} %get-tuple-element.71), channel_id=1, source_target_pairs={{0,8},{1,2},{2,1},{3,4},{4,3},{5,6},{6,5},{7,15},{8,0},{9,10},{10,... | collective-permute-start | bytes 147464 | tf_op jit(solution)/shard_map/ppermute | solution.py:342
  14.6 2.4 %shard_map.72 = (bf16[768,768]{1,0:T(8,128)(2,1)S(1)}, f32[1,768]{1,0:T(1,128)S(1)}, bf16[96,768]{1,0:T(8,128)(2,1)S(1)}, f32[96,512]{1,0:T(8,128)S(1)}) custom-call(bf16[96,512]{1,0:T(8,128)(2,1)S(1)} %get-tuple-element.72.zone_ref.mid_ref.rest_0_, bf16[96,768]{1,0:T(8,128)(2,1)S(1)} %get-tuple-element.73.inner_ref.old_ref, ...), custom_call_target="tpu_custom_call" | custom-call | flops 1207959552 | bytes 4194304 | tf_op jit(solution)/shard_map/pallas_call | solution.py:26
  17.6 1.5 %collective-permute-start.7 = (bf16[96,256]{1,0:T(8,128)(2,1)S(1)}, bf16[96,256]{1,0:T(8,128)(2,1)S(1)}, u32[]{:S(2)}, u32[]{:S(2)}) collective-permute-start(bf16[96,256]{1,0:T(8,128)(2,1)S(1)} %get-tuple-element.77), channel_id=1, source_target_pairs={{0,8},{1,2},{2,1},{3,4},{4,3},{5,6},{6,5},{7,15},{8,0},{9,10},{10,... | collective-permute-start | bytes 147464 | tf_op jit(solution)/shard_map/ppermute | solution.py:342
  19.1 0.9 %shard_map.74 = (bf16[96,768]{1,0:T(8,128)(2,1)S(1)}, f32[96,512]{1,0:T(8,128)S(1)}) custom-call(bf16[96,512]{1,0:T(8,128)(2,1)S(1)} %get-tuple-element.78.zone_ref.mid_ref.old_ref, bf16[96,768]{1,0:T(8,128)(2,1)S(1)} %get-tuple-element.79.inner_ref.old_ref, bf16[96,768]{1,0:T(8,128)(2,1)S(1)} %get-tuple-element.73.inner_ref.old_ref, ...), custom_call_target="tpu_custom_call" | custom-call | flops 314572800 | bytes 4194304 | tf_op jit(solution)/shard_map/pallas_call | solution.py:26
  20.0 1.7 %collective-permute-done.7.got_b_ref = bf16[96,256]{1,0:T(8,128)(2,1)S(1)} collective-permute-done((bf16[96,256]{1,0:T(8,128)(2,1)S(1)}, bf16[96,256]{1,0:T(8,128)(2,1)S(1)}, u32[]{:S(2)}, u32[]{:S(2)}) %collective-permute-start.7) | collective-permute-done | bytes 49184 | tf_op jit(solution)/shard_map/ppermute | solution.py:342
  21.9 0.9 %shard_map.77 = (bf16[96,768]{1,0:T(8,128)(2,1)S(1)}, f32[96,512]{1,0:T(8,128)S(1)}) custom-call(bf16[96,512]{1,0:T(8,128)(2,1)S(1)} %get-tuple-element.86.mid_ref.zone_ref, bf16[96,768]{1,0:T(8,128)(2,1)S(1)} %get-tuple-element.87.inner_ref, bf16[96,768]{1,0:T(8,128)(2,1)S(1)} %get-tuple-element.79.inner_ref.old_ref, ...), custom_call_target="tpu_custom_call" | custom-call | flops 314572800 | bytes 4194304 | tf_op jit(solution)/shard_map/pallas_call | solution.py:26
  22.8 1.6 %collective-permute-start.10 = (bf16[96,768]{1,0:T(8,128)(2,1)S(1)}, bf16[96,768]{1,0:T(8,128)(2,1)S(1)}, u32[]{:S(2)}, u32[]{:S(2)}) collective-permute-start(bf16[96,768]{1,0:T(8,128)(2,1)S(1)} %get-tuple-element.88.inner_ref.refs_5_), channel_id=1, source_target_pairs={{0,8},{8,0},{16,24},{24,16},{1,9},{9,1},{17,25},{25,17},{2,10},{10... | collective-permute-start | bytes 442376 | tf_op jit(solution)/shard_map/ppermute | solution.py:352
  24.9 1.5 %collective-permute-start.12 = (bf16[96,768]{1,0:T(8,128)(2,1)S(1)}, bf16[96,768]{1,0:T(8,128)(2,1)S(1)}, u32[]{:S(2)}, u32[]{:S(2)}) collective-permute-start(bf16[96,768]{1,0:T(8,128)(2,1)S(1)} %get-tuple-element.88.inner_ref.refs_5_), channel_id=1, source_target_pairs={{0,16},{8,24},{16,0},{24,8},{1,17},{9,25},{17,1},{25,9},{2,18},{10... | collective-permute-start | bytes 442376 | tf_op jit(solution)/shard_map/ppermute | solution.py:352
  26.4 2.8 %collective-permute-done.9.got_b_ref = bf16[96,256]{1,0:T(8,128)(2,1)S(1)} collective-permute-done((bf16[96,256]{1,0:T(8,128)(2,1)S(1)}, bf16[96,256]{1,0:T(8,128)(2,1)S(1)}, u32[]{:S(2)}, u32[]{:S(2)}) %collective-permute-start.9) | collective-permute-done | bytes 49184 | tf_op jit(solution)/shard_map/ppermute | solution.py:342
  29.4 1.6 %collective-permute-start.11 = (bf16[96,512]{1,0:T(8,128)(2,1)S(1)}, bf16[96,512]{1,0:T(8,128)(2,1)S(1)}, u32[]{:S(2)}, u32[]{:S(2)}) collective-permute-start(bf16[96,512]{1,0:T(8,128)(2,1)S(1)} %shard_map.76.zone_ref.refs_6_), channel_id=1, source_target_pairs={{0,8},{8,0},{16,24},{24,16},{1,9},{9,1},{17,25},{25,17},{2,10},{10... | collective-permute-start | bytes 294920 | tf_op jit(solution)/shard_map/ppermute | solution.py:352
  30.9 1.5 %collective-permute-start.13 = (bf16[96,512]{1,0:T(8,128)(2,1)S(1)}, bf16[96,512]{1,0:T(8,128)(2,1)S(1)}, u32[]{:S(2)}, u32[]{:S(2)}) collective-permute-start(bf16[96,512]{1,0:T(8,128)(2,1)S(1)} %shard_map.76.zone_ref.refs_6_), channel_id=1, source_target_pairs={{0,16},{8,24},{16,0},{24,8},{1,17},{9,25},{17,1},{25,9},{2,18},{10... | collective-permute-start | bytes 294920 | tf_op jit(solution)/shard_map/ppermute | solution.py:352
  32.4 1.3 %shard_map.78 = (bf16[96,768]{1,0:T(8,128)(2,1)S(1)}, bf16[96,512]{1,0:T(8,128)(2,1)S(1)}, bf16[96,1024]{1,0:T(8,128)(2,1)}) custom-call(bf16[96,512]{1,0:T(8,128)(2,1)S(1)} %shard_map.76.zone_ref.refs_6_, bf16[96,768]{1,0:T(8,128)(2,1)S(1)} %get-tuple-element.88.inner_ref.refs_5_, f32[96,512]{1,0:T(8,128)S(1)} %get-tuple-element.89.part_ref, ...), custom_call_target="tpu_custom_call" | custom-call | flops 314572800 | bytes 4194304 | tf_op jit(solution)/shard_map/pallas_call | solution.py:26
  34.2 1.3 %collective-permute-done.13.refs_10_ = bf16[96,512]{1,0:T(8,128)(2,1)S(1)} collective-permute-done((bf16[96,512]{1,0:T(8,128)(2,1)S(1)}, bf16[96,512]{1,0:T(8,128)(2,1)S(1)}, u32[]{:S(2)}, u32[]{:S(2)}) %collective-permute-start.13) | collective-permute-done | bytes 98336 | tf_op jit(solution)/shard_map/ppermute | solution.py:352
  35.5 0.9 %shard_map.80 = (bf16[4,2,48,192]{3,2,1,0:T(8,128)(2,1)S(1)}, bf16[4,48,192]{2,1,0:T(8,128)(2,1)S(1)}) custom-call(bf16[96,768]{1,0:T(8,128)(2,1)S(1)} %get-tuple-element.91.energy_ref, bf16[96,512]{1,0:T(8,128)(2,1)S(1)} %get-tuple-element.92.energy_zone_ref, f32[96,768]{1,0:T(8,128)S(1)} %get-tuple-element.93.refs_0_, ...), custom_call_target="tpu_custom_call" | custom-call | flops 150994944 | bytes 4194304 | tf_op jit(solution)/shard_map/pallas_call | solution.py:26
  36.5 1.3 %collective-permute-done.14.got_ref = bf16[4,48,192]{2,1,0:T(8,128)(2,1)S(1)} collective-permute-done((bf16[4,48,192]{2,1,0:T(8,128)(2,1)S(1)}, bf16[4,48,192]{2,1,0:T(8,128)(2,1)S(1)}, u32[]{:S(2)}, u32[]{:S(2)}) %collective-permute-start.14) | collective-permute-done | bytes 73760 | tf_op jit(solution)/shard_map/ppermute | solution.py:342
  37.9 2.0 %collective-permute-start.16 = (bf16[48,192]{1,0:T(8,128)(2,1)S(1)}, bf16[48,192]{1,0:T(8,128)(2,1)S(1)}, u32[]{:S(2)}, u32[]{:S(2)}) collective-permute-start(bf16[48,192]{1,0:T(8,128)(2,1)S(1)} %get-tuple-element.98), channel_id=1, source_target_pairs={{0,2},{1,3},{2,0},{3,1},{4,12},{5,13},{6,4},{7,5},{8,10},{9,11},{1... | collective-permute-start | bytes 55304 | tf_op jit(solution)/shard_map/ppermute | solution.py:363
  40.2 3.6 %collective-permute-start.18 = (bf16[48,192]{1,0:T(8,128)(2,1)S(1)}, bf16[48,192]{1,0:T(8,128)(2,1)S(1)}, u32[]{:S(2)}, u32[]{:S(2)}) collective-permute-start(bf16[48,192]{1,0:T(8,128)(2,1)S(1)} %get-tuple-element.100), channel_id=1, source_target_pairs={{0,12},{1,13},{2,4},{3,5},{4,2},{5,3},{6,0},{7,1},{8,14},{9,15},{1... | collective-permute-start | bytes 55304 | tf_op jit(solution)/shard_map/ppermute | solution.py:363
  43.8 0.9 %collective-permute-done.17.refs_2_ = bf16[48,192]{1,0:T(8,128)(2,1)S(1)} collective-permute-done((bf16[48,192]{1,0:T(8,128)(2,1)S(1)}, bf16[48,192]{1,0:T(8,128)(2,1)S(1)}, u32[]{:S(2)}, u32[]{:S(2)}) %collective-permute-start.17) | collective-permute-done | bytes 18464 | tf_op jit(solution)/shard_map/ppermute | solution.py:363
  44.7 1.1 %collective-permute-done.18.refs_3_ = bf16[48,192]{1,0:T(8,128)(2,1)S(1)} collective-permute-done((bf16[48,192]{1,0:T(8,128)(2,1)S(1)}, bf16[48,192]{1,0:T(8,128)(2,1)S(1)}, u32[]{:S(2)}, u32[]{:S(2)}) %collective-permute-start.18) | collective-permute-done | bytes 18464 | tf_op jit(solution)/shard_map/ppermute | solution.py:363
  (34 shorter events, 5.6 us)
Async XLA Ops:
  0.6 6.8 %copy-start = (bf16[96,1024]{1,0:T(8,128)(2,1)S(1)}, bf16[96,1024]{1,0:T(8,128)(2,1)}, u32[]{:S(2)}) copy-start(bf16[96,1024]{1,0:T(8,128)(2,1)} %states_ref.3) | copy-start | bytes 589828
  0.6 6.8 %copy-start.1 = (f32[1024]{0:T(1024)S(1)}, f32[1024]{0:T(1024)}, u32[]{:S(2)}) copy-start(f32[1024]{0:T(1024)} %param.7) | copy-start | bytes 12292
  1.5 5.9 %collective-permute-start = (bf16[112,128]{1,0:T(8,128)(2,1)S(1)}, bf16[112,128]{1,0:T(8,128)(2,1)S(1)}, u32[]{:S(2)}, u32[]{:S(2)}) collective-permute-start(bf16[112,128]{1,0:T(8,128)(2,1)S(1)} %get-tuple-element.53), channel_id=1, source_target_pairs={{0,1},{1,0},{2,3},{3,2},{4,5},{5,4},{6,7},{7,6},{8,9},{9,8},{10,11... | collective-permute-start | bytes 86024 | tf_op jit(solution)/shard_map/ppermute | solution.py:342
  2.1 5.3 %collective-permute-start.1 = (bf16[112,128]{1,0:T(8,128)(2,1)S(1)}, bf16[112,128]{1,0:T(8,128)(2,1)S(1)}, u32[]{:S(2)}, u32[]{:S(2)}) collective-permute-start(bf16[112,128]{1,0:T(8,128)(2,1)S(1)} %get-tuple-element.54), channel_id=1, source_target_pairs={{0,8},{1,2},{2,1},{3,4},{4,3},{5,6},{6,5},{7,15},{8,0},{9,10},{10,... | collective-permute-start | bytes 86024 | tf_op jit(solution)/shard_map/ppermute | solution.py:342
  8.3 3.9 %collective-permute-start.2 = (bf16[96,256]{1,0:T(8,128)(2,1)S(1)}, bf16[96,256]{1,0:T(8,128)(2,1)S(1)}, u32[]{:S(2)}, u32[]{:S(2)}) collective-permute-start(bf16[96,256]{1,0:T(8,128)(2,1)S(1)} %get-tuple-element.59), channel_id=1, source_target_pairs={{0,1},{1,0},{2,3},{3,2},{4,5},{5,4},{6,7},{7,6},{8,9},{9,8},{10,11... | collective-permute-start | bytes 147464 | tf_op jit(solution)/shard_map/ppermute | solution.py:342
  8.6 4.1 %collective-permute-start.3 = (bf16[96,256]{1,0:T(8,128)(2,1)S(1)}, bf16[96,256]{1,0:T(8,128)(2,1)S(1)}, u32[]{:S(2)}, u32[]{:S(2)}) collective-permute-start(bf16[96,256]{1,0:T(8,128)(2,1)S(1)} %get-tuple-element.60), channel_id=1, source_target_pairs={{0,8},{1,2},{2,1},{3,4},{4,3},{5,6},{6,5},{7,15},{8,0},{9,10},{10,... | collective-permute-start | bytes 147464 | tf_op jit(solution)/shard_map/ppermute | solution.py:342
  12.9 4.0 %collective-permute-start.4 = (bf16[96,256]{1,0:T(8,128)(2,1)S(1)}, bf16[96,256]{1,0:T(8,128)(2,1)S(1)}, u32[]{:S(2)}, u32[]{:S(2)}) collective-permute-start(bf16[96,256]{1,0:T(8,128)(2,1)S(1)} %get-tuple-element.70), channel_id=1, source_target_pairs={{0,1},{1,0},{2,3},{3,2},{4,5},{5,4},{6,7},{7,6},{8,9},{9,8},{10,11... | collective-permute-start | bytes 147464 | tf_op jit(solution)/shard_map/ppermute | solution.py:342
  13.0 4.1 %collective-permute-start.5 = (bf16[96,256]{1,0:T(8,128)(2,1)S(1)}, bf16[96,256]{1,0:T(8,128)(2,1)S(1)}, u32[]{:S(2)}, u32[]{:S(2)}) collective-permute-start(bf16[96,256]{1,0:T(8,128)(2,1)S(1)} %get-tuple-element.71), channel_id=1, source_target_pairs={{0,8},{1,2},{2,1},{3,4},{4,3},{5,6},{6,5},{7,15},{8,0},{9,10},{10,... | collective-permute-start | bytes 147464 | tf_op jit(solution)/shard_map/ppermute | solution.py:342
  17.4 2.6 %collective-permute-start.6 = (bf16[96,256]{1,0:T(8,128)(2,1)S(1)}, bf16[96,256]{1,0:T(8,128)(2,1)S(1)}, u32[]{:S(2)}, u32[]{:S(2)}) collective-permute-start(bf16[96,256]{1,0:T(8,128)(2,1)S(1)} %get-tuple-element.76), channel_id=1, source_target_pairs={{0,1},{1,0},{2,3},{3,2},{4,5},{5,4},{6,7},{7,6},{8,9},{9,8},{10,11... | collective-permute-start | bytes 147464 | tf_op jit(solution)/shard_map/ppermute | solution.py:342
  17.6 4.1 %collective-permute-start.7 = (bf16[96,256]{1,0:T(8,128)(2,1)S(1)}, bf16[96,256]{1,0:T(8,128)(2,1)S(1)}, u32[]{:S(2)}, u32[]{:S(2)}) collective-permute-start(bf16[96,256]{1,0:T(8,128)(2,1)S(1)} %get-tuple-element.77), channel_id=1, source_target_pairs={{0,8},{1,2},{2,1},{3,4},{4,3},{5,6},{6,5},{7,15},{8,0},{9,10},{10,... | collective-permute-start | bytes 147464 | tf_op jit(solution)/shard_map/ppermute | solution.py:342
  22.8 10.9 %collective-permute-start.10 = (bf16[96,768]{1,0:T(8,128)(2,1)S(1)}, bf16[96,768]{1,0:T(8,128)(2,1)S(1)}, u32[]{:S(2)}, u32[]{:S(2)}) collective-permute-start(bf16[96,768]{1,0:T(8,128)(2,1)S(1)} %get-tuple-element.88.inner_ref.refs_5_), channel_id=1, source_target_pairs={{0,8},{8,0},{16,24},{24,16},{1,9},{9,1},{17,25},{25,17},{2,10},{10... | collective-permute-start | bytes 442376 | tf_op jit(solution)/shard_map/ppermute | solution.py:352
  24.4 2.1 %collective-permute-start.8 = (bf16[96,256]{1,0:T(8,128)(2,1)S(1)}, bf16[96,256]{1,0:T(8,128)(2,1)S(1)}, u32[]{:S(2)}, u32[]{:S(2)}) collective-permute-start(bf16[96,256]{1,0:T(8,128)(2,1)S(1)} %get-tuple-element.84), channel_id=1, source_target_pairs={{0,1},{1,0},{2,3},{3,2},{4,5},{5,4},{6,7},{7,6},{8,9},{9,8},{10,11... | collective-permute-start | bytes 147464 | tf_op jit(solution)/shard_map/ppermute | solution.py:342
  24.4 4.9 %collective-permute-start.9 = (bf16[96,256]{1,0:T(8,128)(2,1)S(1)}, bf16[96,256]{1,0:T(8,128)(2,1)S(1)}, u32[]{:S(2)}, u32[]{:S(2)}) collective-permute-start(bf16[96,256]{1,0:T(8,128)(2,1)S(1)} %get-tuple-element.85), channel_id=1, source_target_pairs={{0,8},{1,2},{2,1},{3,4},{4,3},{5,6},{6,5},{7,15},{8,0},{9,10},{10,... | collective-permute-start | bytes 147464 | tf_op jit(solution)/shard_map/ppermute | solution.py:342
  24.9 9.3 %collective-permute-start.12 = (bf16[96,768]{1,0:T(8,128)(2,1)S(1)}, bf16[96,768]{1,0:T(8,128)(2,1)S(1)}, u32[]{:S(2)}, u32[]{:S(2)}) collective-permute-start(bf16[96,768]{1,0:T(8,128)(2,1)S(1)} %get-tuple-element.88.inner_ref.refs_5_), channel_id=1, source_target_pairs={{0,16},{8,24},{16,0},{24,8},{1,17},{9,25},{17,1},{25,9},{2,18},{10... | collective-permute-start | bytes 442376 | tf_op jit(solution)/shard_map/ppermute | solution.py:352
  29.4 4.8 %collective-permute-start.11 = (bf16[96,512]{1,0:T(8,128)(2,1)S(1)}, bf16[96,512]{1,0:T(8,128)(2,1)S(1)}, u32[]{:S(2)}, u32[]{:S(2)}) collective-permute-start(bf16[96,512]{1,0:T(8,128)(2,1)S(1)} %shard_map.76.zone_ref.refs_6_), channel_id=1, source_target_pairs={{0,8},{8,0},{16,24},{24,16},{1,9},{9,1},{17,25},{25,17},{2,10},{10... | collective-permute-start | bytes 294920 | tf_op jit(solution)/shard_map/ppermute | solution.py:352
  30.9 4.6 %collective-permute-start.13 = (bf16[96,512]{1,0:T(8,128)(2,1)S(1)}, bf16[96,512]{1,0:T(8,128)(2,1)S(1)}, u32[]{:S(2)}, u32[]{:S(2)}) collective-permute-start(bf16[96,512]{1,0:T(8,128)(2,1)S(1)} %shard_map.76.zone_ref.refs_6_), channel_id=1, source_target_pairs={{0,16},{8,24},{16,0},{24,8},{1,17},{9,25},{17,1},{25,9},{2,18},{10... | collective-permute-start | bytes 294920 | tf_op jit(solution)/shard_map/ppermute | solution.py:352
  36.5 1.4 %collective-permute-start.14 = (bf16[4,48,192]{2,1,0:T(8,128)(2,1)S(1)}, bf16[4,48,192]{2,1,0:T(8,128)(2,1)S(1)}, u32[]{:S(2)}, u32[]{:S(2)}) collective-permute-start(bf16[4,48,192]{2,1,0:T(8,128)(2,1)S(1)} %get-tuple-element.96), channel_id=1, source_target_pairs={{0,1},{1,0},{2,3},{3,2},{4,5},{5,4},{6,7},{7,6},{8,9},{9,8},{10,11... | collective-permute-start | bytes 221192 | tf_op jit(solution)/shard_map/ppermute | solution.py:342
  37.9 5.9 %collective-permute-start.15 = (bf16[48,192]{1,0:T(8,128)(2,1)S(1)}, bf16[48,192]{1,0:T(8,128)(2,1)S(1)}, u32[]{:S(2)}, u32[]{:S(2)}) collective-permute-start(bf16[48,192]{1,0:T(8,128)(2,1)S(1)} %get-tuple-element.97.mine_ref), channel_id=1, source_target_pairs={{0,10},{1,11},{2,8},{3,9},{4,14},{5,15},{6,12},{7,13},{8,2},{9,3},... | collective-permute-start | bytes 55304 | tf_op jit(solution)/shard_map/ppermute | solution.py:363
  37.9 5.8 %collective-permute-start.16 = (bf16[48,192]{1,0:T(8,128)(2,1)S(1)}, bf16[48,192]{1,0:T(8,128)(2,1)S(1)}, u32[]{:S(2)}, u32[]{:S(2)}) collective-permute-start(bf16[48,192]{1,0:T(8,128)(2,1)S(1)} %get-tuple-element.98), channel_id=1, source_target_pairs={{0,2},{1,3},{2,0},{3,1},{4,12},{5,13},{6,4},{7,5},{8,10},{9,11},{1... | collective-permute-start | bytes 55304 | tf_op jit(solution)/shard_map/ppermute | solution.py:363
  39.9 4.8 %collective-permute-start.17 = (bf16[48,192]{1,0:T(8,128)(2,1)S(1)}, bf16[48,192]{1,0:T(8,128)(2,1)S(1)}, u32[]{:S(2)}, u32[]{:S(2)}) collective-permute-start(bf16[48,192]{1,0:T(8,128)(2,1)S(1)} %get-tuple-element.99), channel_id=1, source_target_pairs={{0,4},{1,5},{2,12},{3,13},{4,0},{5,1},{6,2},{7,3},{8,6},{9,7},{10,... | collective-permute-start | bytes 55304 | tf_op jit(solution)/shard_map/ppermute | solution.py:363
  40.2 5.6 %collective-permute-start.18 = (bf16[48,192]{1,0:T(8,128)(2,1)S(1)}, bf16[48,192]{1,0:T(8,128)(2,1)S(1)}, u32[]{:S(2)}, u32[]{:S(2)}) collective-permute-start(bf16[48,192]{1,0:T(8,128)(2,1)S(1)} %get-tuple-element.100), channel_id=1, source_target_pairs={{0,12},{1,13},{2,4},{3,5},{4,2},{5,3},{6,0},{7,1},{8,14},{9,15},{1... | collective-permute-start | bytes 55304 | tf_op jit(solution)/shard_map/ppermute | solution.py:363

commit v2 on v1

--- a/solution.py
+++ b/solution.py
@@ -176,11 +176,11 @@
         zone_ref[:, here] = value.astype(BF16)
 
 
-def zone_sums(zone_ref, part_ref, border_ref, border_diagonal_ref):
+def zone_sums(zone_ref, part, border_ref, border_diagonal_ref):
     extent = border_ref.shape[0]
     width = zone_ref.shape[1] // 2
     sums = (
-        part_ref[...]
+        part
         + mm(zone_ref[:, :width], border_ref[:width, :])
         + mm(zone_ref[:, width:], border_ref[extent - width :, :])
         + border_diagonal_ref[...] * zone_ref[...].astype(F32)
@@ -192,7 +192,7 @@
     old_ref, rest = (rest[0], rest[1:]) if has_old else (None, rest)
     part_ref, border_ref, border_diagonal_ref, zone_ref, next_sums_ref, give_a_ref, give_b_ref = rest
     close_zones(sums_ref, got_a_ref, got_b_ref, shift_zone_ref, mid_ref, old_ref, scale, zone_ref)
-    low, high = zone_sums(zone_ref, part_ref, border_ref, border_diagonal_ref)
+    low, high = zone_sums(zone_ref, part_ref[...], border_ref, border_diagonal_ref)
     width = low.shape[1]
     next_sums_ref[:, :width] = low
     next_sums_ref[:, width:] = high
@@ -209,22 +209,34 @@
     )
 
 
-def inner_body(zone_ref, inner_ref, old_ref, shift_inner_ref, border_ref, square_ref, diagonal_ref, next_ref, part_ref):
+def inner_body(zone_ref, inner_ref, old_ref, shift_inner_ref, border_ref, square_ref, diagonal_ref,
+               next_ref, part_ref, *open_ref):
     sums = inner_sums(zone_ref, inner_ref, border_ref, square_ref, diagonal_ref)
     value = (sums + shift_inner_ref[...] * inner_ref[...].astype(F32)) * (2.0 / spectrum_half)
     next_ref[...] = (value - old_ref[...].astype(F32)).astype(BF16)
     width = zone_ref.shape[1] // 2
     part_ref[...] = mm(next_ref[...], border_ref[width : width + next_ref.shape[1], :])
+    for ref in open_ref:
+        line = diagonal_ref[...] + shift_inner_ref[...]
+        ref[...] = mm(next_ref[...], square_ref[...]) + line * next_ref[...].astype(F32)
+
+
+def last_inner_body(zone_ref, open_ref, old_ref, border_ref, next_ref):
+    width = zone_ref.shape[1] // 2
+    sums = open_ref[...] + mm_nt(zone_ref[...], border_ref[width : width + next_ref.shape[1], :])
+    value = sums * (2.0 / spectrum_half) - old_ref[...].astype(F32)
+    next_ref[...] = value.astype(BF16)
 
 
 def square_body(zone_ref, inner_ref, old_ref, shift_inner_ref, border_ref, hot_ref, wide_ref,
-                square_ref, diagonal_ref, next_ref, part_ref):
+                square_ref, diagonal_ref, next_ref, part_ref, *open_ref):
     size = square_ref.shape[0]
     width = (hot_ref.shape[0] - size) // 2
     for start in range(0, size, 256):
         rows = mm_nt(wide_ref[width + start : width + start + 256, :], hot_ref[width : width + size, :])
         take_diagonal(rows, start, square_ref, diagonal_ref, start)
-    inner_body(zone_ref, inner_ref, old_ref, shift_inner_ref, border_ref, square_ref, diagonal_ref, next_ref, part_ref)
+    inner_body(zone_ref, inner_ref, old_ref, shift_inner_ref, border_ref, square_ref, diagonal_ref,
+               next_ref, part_ref, *open_ref)
 
 
 def last_zone_body(sums_ref, got_a_ref, got_b_ref, shift_zone_ref, mid_ref, old_ref, zone_ref):
@@ -232,8 +244,8 @@
                 2.0 / spectrum_half, zone_ref)
 
 
-def zone_energy(zone_ref, part_ref, shift_zone_ref, border_ref, border_diagonal_ref, energy_ref):
-    low, high = zone_sums(zone_ref, part_ref, border_ref, border_diagonal_ref)
+def zone_energy(zone_ref, part, shift_zone_ref, border_ref, border_diagonal_ref, energy_ref):
+    low, high = zone_sums(zone_ref, part, border_ref, border_diagonal_ref)
     width = low.shape[1]
     rim = width // 2
     own = (shift_zone_ref[:, rim : width + rim] + spectrum_center) * zone_ref[:, rim : width + rim].astype(F32)
@@ -243,13 +255,14 @@
     energy_ref[:, width + rim :] = high[:, rim:].astype(energy_ref.dtype)
 
 
-def energy_body(zone_ref, inner_ref, part_ref, shift_inner_ref, shift_zone_ref,
+def energy_body(zone_ref, inner_ref, shift_inner_ref, shift_zone_ref,
                 border_ref, border_diagonal_ref, square_ref, diagonal_ref, energy_ref, energy_zone_ref, filtered_ref):
     sums = inner_sums(zone_ref, inner_ref, border_ref, square_ref, diagonal_ref)
     own = (shift_inner_ref[...] + spectrum_center) * inner_ref[...].astype(F32)
     energy_ref[...] = (sums + own).astype(BF16)
-    zone_energy(zone_ref, part_ref, shift_zone_ref, border_ref, border_diagonal_ref, energy_zone_ref)
     width = zone_ref.shape[1] // 2
+    part = mm(inner_ref[...], border_ref[width : width + inner_ref.shape[1], :])
+    zone_energy(zone_ref, part, shift_zone_ref, border_ref, border_diagonal_ref, energy_zone_ref)
     rim = width // 2
     owned = filtered_ref.shape[1]
     filtered_ref[:, :rim] = zone_ref[:, rim:width]
@@ -257,57 +270,67 @@
     filtered_ref[:, owned - rim :] = zone_ref[:, width : width + rim]
 
 
-def neighbour_body(inner_ref, shift_inner_ref, border_ref, square_ref, diagonal_ref, open_ref, part_ref):
-    inner = inner_ref[...]
+def neighbour_body(inner_ref, beside_ref, across_ref, energy_ref, shift_inner_ref, border_ref, square_ref, diagonal_ref,
+                   open_ref, part_ref, found_ref, other_ref):
+    beside = beside_ref[...]
     width = border_ref.shape[1] // 2
     line = diagonal_ref[...] + (shift_inner_ref[...] + spectrum_center)
-    open_ref[...] = mm(inner, square_ref[...]) + line * inner.astype(F32)
-    part_ref[...] = mm(inner, border_ref[width : width + inner.shape[1], :])
-
-
-def fill_pair(pair_ref, inner_ref, zone_ref):
-    count, inside = inner_ref.shape
+    open_ref[...] = mm(beside, square_ref[...]) + line * beside.astype(F32)
+    part_ref[...] = mm(beside, border_ref[width : width + beside.shape[1], :])
+    inner_found(found_ref, (inner_ref, beside_ref, across_ref), inner_ref, energy_ref)
+    other_ref[...] = mm_nt(across_ref[...], beside)
+
+
+def inner_found(found_ref, blocks, states_ref, energy_ref):
+    count = states_ref.shape[0]
+    for place, block in enumerate(blocks):
+        here = slice(place * count, (place + 1) * count)
+        found_ref[here, :count] = mm_nt(block[...], states_ref[...])
+        found_ref[here, count:] = mm_nt(block[...], energy_ref[...])
+
+
+def gram_body(*refs):
+    *blocks, energy_ref, found_ref = refs
+    inner_found(found_ref, blocks, blocks[0], energy_ref)
+
+
+def zone_found(block_ref, zone_ref, energy_zone_ref):
     rim = zone_ref.shape[1] // 4
-    none = jnp.zeros((count, rim), BF16)
-    pair_ref[:count, :inside] = inner_ref[...]
-    pair_ref[:count, inside : inside + rim] = none
-    pair_ref[:count, inside + rim : inside + 3 * rim] = zone_ref[:, rim : 3 * rim]
-    pair_ref[:count, inside + 3 * rim :] = none
-
-
-def project_body(square_of_four, scale, energy_ref, energy_zone_ref, *refs):
+    here = slice(rim, 3 * rim)
+    return mm_nt(block_ref[:, here], zone_ref[:, here]), mm_nt(block_ref[...], energy_zone_ref[...])
+
+
+def project_body(square_of_four, scale, energy_zone_ref, found_ref, *refs):
     if square_of_four:
-        (open_ref, part_ref, shift_zone_ref, border_ref, border_diagonal_ref), refs = refs[:5], refs[5:]
-        *blocks, out_ref, give_ref, stack_ref, pair_ref, other_ref, other_zone_ref = refs
+        (open_ref, part_ref, other_ref, across_ref, shift_zone_ref, border_ref, border_diagonal_ref), refs = refs[:7], refs[7:]
+        *zones, out_ref, give_ref, other_zone_ref = refs
     else:
-        *blocks, out_ref, give_ref, stack_ref, pair_ref = refs
-    count, inside = energy_ref.shape
+        *zones, out_ref, give_ref = refs
+    count = energy_zone_ref.shape[0]
+    columns = out_ref.shape[2] // 2
     group = lax.axis_index("state")
     odd = is_odd()
-    for place in range(len(blocks) // 2):
-        stack_ref[place * count : (place + 1) * count, :inside] = blocks[2 * place][...]
-        stack_ref[place * count : (place + 1) * count, inside:] = blocks[2 * place + 1][...]
-    fill_pair(pair_ref, blocks[0], blocks[1])
-    pair_ref[count:, :inside] = energy_ref[...]
-    pair_ref[count:, inside:] = energy_zone_ref[...]
-    both = mm_nt(stack_ref[...], pair_ref[...]) * scale
-    found = [(place, both[place * count : (place + 1) * count]) for place in range(len(blocks) // 2)]
+
+    def put(distance, states, energy):
+        at = group ^ distance
+        for block, there in ((states * scale, slice(0, columns)), (energy * scale, slice(columns, 2 * columns))):
+            parts = [block[:columns], block[columns:]]
+            for core in range(2):
+                out_ref[at, core, there] = parts[core].astype(BF16)
+            give_ref[at, there] = jnp.where(odd, parts[0], parts[1]).astype(BF16)
+
+    for distance, zone in enumerate(zones):
+        here = slice(distance * count, (distance + 1) * count)
+        states, energy = zone_found(zone, zones[0], energy_zone_ref)
+        put(distance, found_ref[here, :count] + states, found_ref[here, count:] + energy)
     if square_of_four:
-        beside, beside_zone = blocks[2], blocks[3]
+        beside_zone = zones[1]
         width = beside_zone.shape[1] // 2
-        fill_pair(other_ref, beside, beside_zone)
-        rest = mm_nt(beside_zone[...], border_ref[width : width + inside, :])
-        other_ref[count:, :inside] = (open_ref[...] + rest).astype(BF16)
-        zone_energy(beside_zone, part_ref, shift_zone_ref, border_ref, border_diagonal_ref, other_zone_ref)
-        other_ref[count:, inside:] = other_zone_ref[...]
-        found.append((3, mm_nt(stack_ref[2 * count :, :], other_ref[...]) * scale))
-    columns = out_ref.shape[2]
-    for distance, block in found:
-        at = group ^ distance
-        parts = [block[:columns], block[columns:]]
-        for core in range(2):
-            out_ref[at, core] = parts[core].astype(BF16)
-        give_ref[at] = jnp.where(odd, parts[0], parts[1]).astype(BF16)
+        rest = mm_nt(beside_zone[...], border_ref[width : width + open_ref.shape[1], :])
+        energy_inner = (open_ref[...] + rest).astype(BF16)
+        zone_energy(beside_zone, part_ref[...], shift_zone_ref, border_ref, border_diagonal_ref, other_zone_ref)
+        states, energy = zone_found(zones[2], beside_zone, other_zone_ref)
+        put(3, other_ref[...] + states, mm_nt(across_ref[...], energy_inner) + energy)
 
 
 def halve_body(mine_ref, got_ref, *pieces):
@@ -317,7 +340,7 @@
         piece_ref[...] = total.astype(BF16)
 
 
-def final_body(square_of_four, count, mine_ref, *refs):
+def final_body(square_of_four, mine_ref, *refs):
     parts, (first_ref, second_ref) = refs[:-2], refs[-2:]
     total = mine_ref[...].astype(F32)
     if square_of_four:
@@ -326,8 +349,9 @@
         parts = parts[1:]
     for part in parts:
         total = total + part[...].astype(F32)
-    first_ref[...] = total[:, :count]
-    second_ref[...] = total[:, count:]
+    columns = first_ref.shape[0]
+    first_ref[...] = total[:columns]
+    second_ref[...] = total[columns:]
 
 
 def swap(block, n_state, n_space, lead):
@@ -417,13 +441,18 @@
         zones.append(zone_k)
         got = exchange(*gave, n_state, n_space)
         ins = (zone_k, inners[-1], inners[-2], shift_inner, border)
+        outs = (inner, sums_of)
+        if k == DEGREE - 2:
+            outs += (SHAPE((count, inside), F32),)
         if k == 1:
-            square, diagonal, inner_k, partial = call(
-                square_body, (SHAPE((inside, inside), BF16), line, inner, sums_of), (*ins, hot, wide),
+            square, diagonal, inner_k, partial, *opened = call(
+                square_body, (SHAPE((inside, inside), BF16), line, *outs), (*ins, hot, wide),
                 2 * inside * inside * cells * nodes,
             )
+        elif k < DEGREE - 1:
+            inner_k, partial, *opened = call(inner_body, outs, (*ins, square, diagonal), work)
         else:
-            inner_k, partial = call(inner_body, (inner, sums_of), (*ins, square, diagonal), work)
+            inner_k = call(last_inner_body, inner, (zone_k, *opened, inners[-2], border), work // 4)
         inners.append(inner_k)
     square_of_four = four(n_state, n_space)
     distances = (1, 2) if square_of_four else range(1, n_state)
@@ -434,32 +463,34 @@
     zone_blocks = [zone_k] + [across(zone_k, "state", d) for d in distances]
     energy, energy_zone, filtered = call(
         energy_body, (inner, zone, SHAPE((count, owned), BF16)),
-        (zone_k, inner_k, partial, shift_inner, shift_zone, border, border_diagonal, square, diagonal), work,
-    )
-    blocks = [b for pair in zip(inner_blocks, zone_blocks) for b in pair]
-    extra = ()
-    scratch = [pltpu.VMEM((len(inner_blocks) * count, extent), BF16), pltpu.VMEM((2 * count, extent), BF16)]
+        (zone_k, inner_k, shift_inner, shift_zone, border, border_diagonal, square, diagonal), work,
+    )
+    extra, scratch = (), []
+    found_of = SHAPE((len(inner_blocks) * count, 2 * count), F32)
     if square_of_four:
-        opened, part_x = call(
-            neighbour_body, (SHAPE((count, inside), F32), sums_of),
-            (inner_blocks[1], shift_inner, border, square, diagonal), work // 2,
+        opened, part_x, found, other = call(
+            neighbour_body,
+            (SHAPE((count, inside), F32), sums_of, found_of, SHAPE((count, count), F32)),
+            (*inner_blocks, energy, shift_inner, border, square, diagonal), work // 2,
         )
-        extra = (opened, part_x, shift_zone, border, border_diagonal)
-        scratch += [pltpu.VMEM((2 * count, extent), BF16), pltpu.VMEM((count, 4 * rim), BF16)]
+        extra = (opened, part_x, other, inner_blocks[2], shift_zone, border, border_diagonal)
+        scratch = [pltpu.VMEM((count, 4 * rim), BF16)]
+    else:
+        found = call(gram_body, found_of, (*inner_blocks, energy), work)
     columns = count * n_state // n_space
     chips = n_space // 2
     mine, give_half = call(
         functools.partial(project_body, square_of_four, 1.0 / (owned * n_space)),
-        (SHAPE((chips, 2, columns, 2 * count), BF16), SHAPE((chips, columns, 2 * count), BF16)),
-        (energy, energy_zone, *extra, *blocks), 4 * count * n_state * count * owned, scratch=scratch,
+        (SHAPE((chips, 2, 2 * columns, count), BF16), SHAPE((chips, 2 * columns, count), BF16)),
+        (energy_zone, found, *extra, *zone_blocks), work // 4, scratch=scratch,
     )
     got_half = swap(give_half, n_state, n_space, 0)
-    piece = SHAPE((columns, 2 * count), BF16)
+    piece = SHAPE((2 * columns, count), BF16)
     pieces = call(halve_body, (piece,) * chips, (mine, got_half), 0)
     shares = [share_out(p, d, n_state, n_space, square_of_four) for d, p in enumerate(pieces) if d or square_of_four]
     turned = SHAPE((columns, count), F32)
     intersection, projected = call(
-        functools.partial(final_body, square_of_four, count), (turned, turned), (pieces[0], *shares), 0
+        functools.partial(final_body, square_of_four), (turned, turned), (pieces[0], *shares), 0
     )
     return filtered, intersection.T, projected.T
 

time: 46.7 us -> 47 us (level)
  waiting for transfers between devices: 9.88 us -> 10.6 us
  starting transfers between devices: 20.9 us -> 20.2 us
    ppermute x4, waiting for transfers between devices: 2.06 us -> 2.98 us  [share_out(): return lax.ppermute(block, ('state', 'space'), route)]
    ppermute x4, starting transfers between devices: 6.17 us -> 5.44 us  [across(): lax.ppermute(block, axis, [(i, i ^ distance) for i in range(lax.axis_size...]
  transfers between devices with their start and end apart: 19 -> 19, of which waited for: 8 -> 10; matrix products, arithmetic and copies ran while one was open for 0% -> 0% of each run, Pallas kernels for 21% -> 23%
where the time goes in v2:
time: 47 us; the launch traced here: 46.9 us
  starting transfers between devices  20.2 us (43%)
  Pallas kernels  15.3 us (33%)
  waiting for transfers between devices  10.6 us (23%)
  between operations  0.8 us (2%)
    pallas_call x16, Pallas kernels, call(): pl.pallas_call(body, out_shape=outs, in_specs=where, out_specs=jax.tree.m...  15.3 us
    ppermute x11, starting transfers between devices, swap(): return lax.ppermute(block, ('state', 'space'), route)  8.81 us
    ppermute x11, waiting for transfers between devices, swap(): return lax.ppermute(block, ('state', 'space'), route)  6.63 us
    ppermute x4, starting transfers between devices, share_out(): return lax.ppermute(block, ('state', 'space'), route)  5.91 us
    ppermute x4, starting transfers between devices, across(): lax.ppermute(block, axis, [(i, i ^ distance) for i in range(lax.axis_size...  5.44 us
    ppermute x4, waiting for transfers between devices, share_out(): return lax.ppermute(block, ('state', 'space'), route)  2.98 us
    ppermute x4, waiting for transfers between devices, across(): lax.ppermute(block, axis, [(i, i ^ distance) for i in range(lax.axis_size...  1 us
  transfers between devices with their start and end apart: 19, of which 10 were waited for; matrix products, arithmetic and copies ran while one was open for 0% of the time, Pallas kernels for 23%

profile of v2, /device:TPU:0, one launch (start us, length us, event | category | flops | bytes accessed | tf_op | source)
XLA Modules:
  0.0 46.9 jit_solution(8341579543536935070)
XLA Ops:
  0.7 0.9 %shard_map.67 = (bf16[112,128]{1,0:T(8,128)(2,1)S(1)}, bf16[112,128]{1,0:T(8,128)(2,1)S(1)}, s32[2,512]{1,0:T(2,128)S(1)}) custom-call(bf16[96,1024]{1,0:T(8,128)(2,1)} %states_ref.3, f32[1,1024]{1,0:T(1,128)} %bitcast.3, s32[2,512]{1,0:T(2,128)} %index_ref.1), custom_call_target="tpu_custom_call" | custom-call | bytes 4194304 | tf_op jit(solution)/shard_map/pallas_call | solution.py:26
  2.1 2.6 %collective-permute-start.1 = (bf16[112,128]{1,0:T(8,128)(2,1)S(1)}, bf16[112,128]{1,0:T(8,128)(2,1)S(1)}, u32[]{:S(2)}, u32[]{:S(2)}) collective-permute-start(bf16[112,128]{1,0:T(8,128)(2,1)S(1)} %get-tuple-element.54), channel_id=1, source_target_pairs={{0,8},{1,2},{2,1},{3,4},{4,3},{5,6},{6,5},{7,15},{8,0},{9,10},{10,... | collective-permute-start | bytes 86024 | tf_op jit(solution)/shard_map/ppermute | solution.py:366
  4.6 2.8 %shard_map.68 = (bf16[1280,1024]{1,0:T(8,128)(2,1)S(1)}, bf16[1280,1024]{1,0:T(8,128)(2,1)S(1)}) custom-call(s32[2,512]{1,0:T(2,128)S(1)} %get-tuple-element.55.index_ref, bf16[2,512,512]{2,1,0:T(8,128)(2,1)} %cells_ref.1), custom_call_target="tpu_custom_call" | custom-call | flops 1342177280 | bytes 4194304 | tf_op jit(solution)/shard_map/pallas_call | solution.py:26
  7.4 0.9 %shard_map.69 = (bf16[96,768]{1,0:T(8,128)(2,1)S(1)}, bf16[96,512]{1,0:T(8,128)(2,1)S(1)}, f32[1,768]{1,0:T(1,128)S(1)}, f32[1,512]{1,0:T(1,128)S(1)}, bf16[96,1...) custom-call(bf16[96,1024]{1,0:T(8,128)(2,1)S(1)} %copy-done, ...), custom_call_target="tpu_custom_call" | custom-call | flops 314572800 | bytes 4194304 | tf_op jit(solution)/shard_map/pallas_call | solution.py:26
  8.6 1.5 %collective-permute-start.3 = (bf16[96,256]{1,0:T(8,128)(2,1)S(1)}, bf16[96,256]{1,0:T(8,128)(2,1)S(1)}, u32[]{:S(2)}, u32[]{:S(2)}) collective-permute-start(bf16[96,256]{1,0:T(8,128)(2,1)S(1)} %get-tuple-element.60), channel_id=1, source_target_pairs={{0,8},{1,2},{2,1},{3,4},{4,3},{5,6},{6,5},{7,15},{8,0},{9,10},{10,... | collective-permute-start | bytes 147464 | tf_op jit(solution)/shard_map/ppermute | solution.py:366
  10.1 2.1 %shard_map.70 = (bf16[96,768]{1,0:T(8,128)(2,1)S(1)}, bf16[1280,512]{1,0:T(8,128)(2,1)S(1)}, f32[1,512]{1,0:T(1,128)S(1)}, f32[96,512]{1,0:T(8,128)S(1)}) custom-call(bf16[96,768]{1,0:T(8,128)(2,1)S(1)} %get-tuple-element.63.inner_ref.old_ref, bf16[96,1024]{1,0:T(8,128)(2,1)S(1)} %get-tuple-element.64.picked_ref, ...), custom_call_target="tpu_custom_call" | custom-call | flops 1342177280 | bytes 4194304 | tf_op jit(solution)/shard_map/pallas_call | solution.py:26
  13.0 1.5 %collective-permute-start.5 = (bf16[96,256]{1,0:T(8,128)(2,1)S(1)}, bf16[96,256]{1,0:T(8,128)(2,1)S(1)}, u32[]{:S(2)}, u32[]{:S(2)}) collective-permute-start(bf16[96,256]{1,0:T(8,128)(2,1)S(1)} %get-tuple-element.71), channel_id=1, source_target_pairs={{0,8},{1,2},{2,1},{3,4},{4,3},{5,6},{6,5},{7,15},{8,0},{9,10},{10,... | collective-permute-start | bytes 147464 | tf_op jit(solution)/shard_map/ppermute | solution.py:366
  14.6 2.4 %shard_map.72 = (bf16[768,768]{1,0:T(8,128)(2,1)S(1)}, f32[1,768]{1,0:T(1,128)S(1)}, bf16[96,768]{1,0:T(8,128)(2,1)S(1)}, f32[96,512]{1,0:T(8,128)S(1)}) custom-call(bf16[96,512]{1,0:T(8,128)(2,1)S(1)} %get-tuple-element.72.zone_ref.mid_ref.rest_0_, bf16[96,768]{1,0:T(8,128)(2,1)S(1)} %get-tuple-element.73.inner_ref.old_ref, ...), custom_call_target="tpu_custom_call" | custom-call | flops 1207959552 | bytes 4194304 | tf_op jit(solution)/shard_map/pallas_call | solution.py:26
  17.6 1.5 %collective-permute-start.7 = (bf16[96,256]{1,0:T(8,128)(2,1)S(1)}, bf16[96,256]{1,0:T(8,128)(2,1)S(1)}, u32[]{:S(2)}, u32[]{:S(2)}) collective-permute-start(bf16[96,256]{1,0:T(8,128)(2,1)S(1)} %get-tuple-element.77), channel_id=1, source_target_pairs={{0,8},{1,2},{2,1},{3,4},{4,3},{5,6},{6,5},{7,15},{8,0},{9,10},{10,... | collective-permute-start | bytes 147464 | tf_op jit(solution)/shard_map/ppermute | solution.py:366
  19.1 1.4 %shard_map.74 = (bf16[96,768]{1,0:T(8,128)(2,1)}, f32[96,512]{1,0:T(8,128)S(1)}, f32[96,768]{1,0:T(8,128)S(1)}) custom-call(bf16[96,512]{1,0:T(8,128)(2,1)S(1)} %get-tuple-element.78.zone_ref.mid_ref.old_ref, bf16[96,768]{1,0:T(8,128)(2,1)S(1)} %get-tuple-element.79.inner_ref.old_ref, bf16[96,768]{1,0:T(8,128)(2,1)S(1)} %get-tuple-element.73.inner_ref.old_ref, ...), custom_call_target="tpu_custom_call" | custom-call | flops 314572800 | bytes 4194304 | tf_op jit(solution)/shard_map/pallas_call | solution.py:26
  20.5 1.2 %collective-permute-done.7.got_b_ref = bf16[96,256]{1,0:T(8,128)(2,1)S(1)} collective-permute-done((bf16[96,256]{1,0:T(8,128)(2,1)S(1)}, bf16[96,256]{1,0:T(8,128)(2,1)S(1)}, u32[]{:S(2)}, u32[]{:S(2)}) %collective-permute-start.7) | collective-permute-done | bytes 49184 | tf_op jit(solution)/shard_map/ppermute | solution.py:366
  22.3 1.6 %collective-permute-start.10 = (bf16[96,768]{1,0:T(8,128)(2,1)S(1)}, bf16[96,768]{1,0:T(8,128)(2,1)S(1)}, u32[]{:S(2)}, u32[]{:S(2)}) collective-permute-start(bf16[96,768]{1,0:T(8,128)(2,1)S(1)} %shard_map.77.inner_ref), channel_id=1, source_target_pairs={{0,8},{8,0},{16,24},{24,16},{1,9},{9,1},{17,25},{25,17},{2,10},{10... | collective-permute-start | bytes 442376 | tf_op jit(solution)/shard_map/ppermute | solution.py:376
  23.9 1.5 %collective-permute-start.11 = (bf16[96,768]{1,0:T(8,128)(2,1)S(1)}, bf16[96,768]{1,0:T(8,128)(2,1)S(1)}, u32[]{:S(2)}, u32[]{:S(2)}) collective-permute-start(bf16[96,768]{1,0:T(8,128)(2,1)S(1)} %shard_map.77.inner_ref), channel_id=1, source_target_pairs={{0,16},{8,24},{16,0},{24,8},{1,17},{9,25},{17,1},{25,9},{2,18},{10... | collective-permute-start | bytes 442376 | tf_op jit(solution)/shard_map/ppermute | solution.py:376
  26.6 2.9 %collective-permute-done.9.got_b_ref = bf16[96,256]{1,0:T(8,128)(2,1)S(1)} collective-permute-done((bf16[96,256]{1,0:T(8,128)(2,1)S(1)}, bf16[96,256]{1,0:T(8,128)(2,1)S(1)}, u32[]{:S(2)}, u32[]{:S(2)}) %collective-permute-start.9) | collective-permute-done | bytes 49184 | tf_op jit(solution)/shard_map/ppermute | solution.py:366
  29.6 0.9 %collective-permute-start.12 = (bf16[96,512]{1,0:T(8,128)(2,1)S(1)}, bf16[96,512]{1,0:T(8,128)(2,1)S(1)}, u32[]{:S(2)}, u32[]{:S(2)}) collective-permute-start(bf16[96,512]{1,0:T(8,128)(2,1)S(1)} %shard_map.76.zone_ref.refs_7_), channel_id=1, source_target_pairs={{0,8},{8,0},{16,24},{24,16},{1,9},{9,1},{17,25},{25,17},{2,10},{10... | collective-permute-start | bytes 294920 | tf_op jit(solution)/shard_map/ppermute | solution.py:376
  30.4 1.5 %collective-permute-start.13 = (bf16[96,512]{1,0:T(8,128)(2,1)S(1)}, bf16[96,512]{1,0:T(8,128)(2,1)S(1)}, u32[]{:S(2)}, u32[]{:S(2)}) collective-permute-start(bf16[96,512]{1,0:T(8,128)(2,1)S(1)} %shard_map.76.zone_ref.refs_7_), channel_id=1, source_target_pairs={{0,16},{8,24},{16,0},{24,8},{1,17},{9,25},{17,1},{25,9},{2,18},{10... | collective-permute-start | bytes 294920 | tf_op jit(solution)/shard_map/ppermute | solution.py:376
  31.9 1.3 %shard_map.78 = (bf16[96,768]{1,0:T(8,128)(2,1)S(1)}, bf16[96,512]{1,0:T(8,128)(2,1)S(1)}, bf16[96,1024]{1,0:T(8,128)(2,1)}) custom-call(bf16[96,512]{1,0:T(8,128)(2,1)S(1)} %shard_map.76.zone_ref.refs_7_, bf16[96,768]{1,0:T(8,128)(2,1)S(1)} %shard_map.77.inner_ref, f32[1,768]{1,0:T(1,128)S(1)} %get-tuple-element.65.shift_inner_ref, ...), custom_call_target="tpu_custom_call" | custom-call | flops 314572800 | bytes 4194304 | tf_op jit(solution)/shard_map/pallas_call | solution.py:26
  35.0 0.9 %shard_map.80 = (bf16[4,2,96,96]{3,2,1,0:T(8,128)(2,1)S(1)}, bf16[4,96,96]{2,1,0:T(8,128)(2,1)S(1)}) custom-call(bf16[96,512]{1,0:T(8,128)(2,1)S(1)} %get-tuple-element.89.energy_zone_ref, f32[288,192]{1,0:T(8,128)S(1)} %get-tuple-element.91.found_ref, f32[96,768]{1,0:T(8,128)S(1)} %get-tuple-element.92.refs_0_, f32[96,512]{1,0:T(8,128)S(1)} %get-tuple-element.93.refs_1_, ...), custom_call_target="tpu_custom_call" | custom-call | flops 78643200 | bytes 4194304 | tf_op jit(solution)/shard_map/pallas_call | solution.py:26
  36.0 1.3 %collective-permute-done.14.got_ref = bf16[4,96,96]{2,1,0:T(8,128)(2,1)S(1)} collective-permute-done((bf16[4,96,96]{2,1,0:T(8,128)(2,1)S(1)}, bf16[4,96,96]{2,1,0:T(8,128)(2,1)S(1)}, u32[]{:S(2)}, u32[]{:S(2)}) %collective-permute-start.14) | collective-permute-done | bytes 73760 | tf_op jit(solution)/shard_map/ppermute | solution.py:366
  37.3 1.0 %collective-permute-start.15 = (bf16[96,96]{1,0:T(8,128)(2,1)S(1)}, bf16[96,96]{1,0:T(8,128)(2,1)S(1)}, u32[]{:S(2)}, u32[]{:S(2)}) collective-permute-start(bf16[96,96]{1,0:T(8,128)(2,1)S(1)} %get-tuple-element.97.mine_ref), channel_id=1, source_target_pairs={{0,10},{1,11},{2,8},{3,9},{4,14},{5,15},{6,12},{7,13},{8,2},{9,3},... | collective-permute-start | bytes 55304 | tf_op jit(solution)/shard_map/ppermute | solution.py:387
  38.4 1.7 %collective-permute-start.16 = (bf16[96,96]{1,0:T(8,128)(2,1)S(1)}, bf16[96,96]{1,0:T(8,128)(2,1)S(1)}, u32[]{:S(2)}, u32[]{:S(2)}) collective-permute-start(bf16[96,96]{1,0:T(8,128)(2,1)S(1)} %get-tuple-element.98), channel_id=1, source_target_pairs={{0,2},{1,3},{2,0},{3,1},{4,12},{5,13},{6,4},{7,5},{8,10},{9,11},{1... | collective-permute-start | bytes 55304 | tf_op jit(solution)/shard_map/ppermute | solution.py:387
  40.6 2.6 %collective-permute-start.18 = (bf16[96,96]{1,0:T(8,128)(2,1)S(1)}, bf16[96,96]{1,0:T(8,128)(2,1)S(1)}, u32[]{:S(2)}, u32[]{:S(2)}) collective-permute-start(bf16[96,96]{1,0:T(8,128)(2,1)S(1)} %get-tuple-element.100), channel_id=1, source_target_pairs={{0,12},{1,13},{2,4},{3,5},{4,2},{5,3},{6,0},{7,1},{8,14},{9,15},{1... | collective-permute-start | bytes 55304 | tf_op jit(solution)/shard_map/ppermute | solution.py:387
  43.3 1.8 %collective-permute-done.17.refs_2_ = bf16[96,96]{1,0:T(8,128)(2,1)S(1)} collective-permute-done((bf16[96,96]{1,0:T(8,128)(2,1)S(1)}, bf16[96,96]{1,0:T(8,128)(2,1)S(1)}, u32[]{:S(2)}, u32[]{:S(2)}) %collective-permute-start.17) | collective-permute-done | bytes 18464 | tf_op jit(solution)/shard_map/ppermute | solution.py:387
  45.1 1.2 %collective-permute-done.18.refs_3_ = bf16[96,96]{1,0:T(8,128)(2,1)S(1)} collective-permute-done((bf16[96,96]{1,0:T(8,128)(2,1)S(1)}, bf16[96,96]{1,0:T(8,128)(2,1)S(1)}, u32[]{:S(2)}, u32[]{:S(2)}) %collective-permute-start.18) | collective-permute-done | bytes 18464 | tf_op jit(solution)/shard_map/ppermute | solution.py:387
  (34 shorter events, 7.2 us)
Async XLA Ops:
  0.6 6.8 %copy-start = (bf16[96,1024]{1,0:T(8,128)(2,1)S(1)}, bf16[96,1024]{1,0:T(8,128)(2,1)}, u32[]{:S(2)}) copy-start(bf16[96,1024]{1,0:T(8,128)(2,1)} %states_ref.3) | copy-start | bytes 589828
  0.6 6.8 %copy-start.1 = (f32[1024]{0:T(1024)S(1)}, f32[1024]{0:T(1024)}, u32[]{:S(2)}) copy-start(f32[1024]{0:T(1024)} %param.7) | copy-start | bytes 12292
  1.5 5.9 %collective-permute-start = (bf16[112,128]{1,0:T(8,128)(2,1)S(1)}, bf16[112,128]{1,0:T(8,128)(2,1)S(1)}, u32[]{:S(2)}, u32[]{:S(2)}) collective-permute-start(bf16[112,128]{1,0:T(8,128)(2,1)S(1)} %get-tuple-element.53), channel_id=1, source_target_pairs={{0,1},{1,0},{2,3},{3,2},{4,5},{5,4},{6,7},{7,6},{8,9},{9,8},{10,11... | collective-permute-start | bytes 86024 | tf_op jit(solution)/shard_map/ppermute | solution.py:366
  2.1 5.3 %collective-permute-start.1 = (bf16[112,128]{1,0:T(8,128)(2,1)S(1)}, bf16[112,128]{1,0:T(8,128)(2,1)S(1)}, u32[]{:S(2)}, u32[]{:S(2)}) collective-permute-start(bf16[112,128]{1,0:T(8,128)(2,1)S(1)} %get-tuple-element.54), channel_id=1, source_target_pairs={{0,8},{1,2},{2,1},{3,4},{4,3},{5,6},{6,5},{7,15},{8,0},{9,10},{10,... | collective-permute-start | bytes 86024 | tf_op jit(solution)/shard_map/ppermute | solution.py:366
  8.3 3.9 %collective-permute-start.2 = (bf16[96,256]{1,0:T(8,128)(2,1)S(1)}, bf16[96,256]{1,0:T(8,128)(2,1)S(1)}, u32[]{:S(2)}, u32[]{:S(2)}) collective-permute-start(bf16[96,256]{1,0:T(8,128)(2,1)S(1)} %get-tuple-element.59), channel_id=1, source_target_pairs={{0,1},{1,0},{2,3},{3,2},{4,5},{5,4},{6,7},{7,6},{8,9},{9,8},{10,11... | collective-permute-start | bytes 147464 | tf_op jit(solution)/shard_map/ppermute | solution.py:366
  8.6 4.1 %collective-permute-start.3 = (bf16[96,256]{1,0:T(8,128)(2,1)S(1)}, bf16[96,256]{1,0:T(8,128)(2,1)S(1)}, u32[]{:S(2)}, u32[]{:S(2)}) collective-permute-start(bf16[96,256]{1,0:T(8,128)(2,1)S(1)} %get-tuple-element.60), channel_id=1, source_target_pairs={{0,8},{1,2},{2,1},{3,4},{4,3},{5,6},{6,5},{7,15},{8,0},{9,10},{10,... | collective-permute-start | bytes 147464 | tf_op jit(solution)/shard_map/ppermute | solution.py:366
  12.9 4.0 %collective-permute-start.4 = (bf16[96,256]{1,0:T(8,128)(2,1)S(1)}, bf16[96,256]{1,0:T(8,128)(2,1)S(1)}, u32[]{:S(2)}, u32[]{:S(2)}) collective-permute-start(bf16[96,256]{1,0:T(8,128)(2,1)S(1)} %get-tuple-element.70), channel_id=1, source_target_pairs={{0,1},{1,0},{2,3},{3,2},{4,5},{5,4},{6,7},{7,6},{8,9},{9,8},{10,11... | collective-permute-start | bytes 147464 | tf_op jit(solution)/shard_map/ppermute | solution.py:366
  13.0 4.1 %collective-permute-start.5 = (bf16[96,256]{1,0:T(8,128)(2,1)S(1)}, bf16[96,256]{1,0:T(8,128)(2,1)S(1)}, u32[]{:S(2)}, u32[]{:S(2)}) collective-permute-start(bf16[96,256]{1,0:T(8,128)(2,1)S(1)} %get-tuple-element.71), channel_id=1, source_target_pairs={{0,8},{1,2},{2,1},{3,4},{4,3},{5,6},{6,5},{7,15},{8,0},{9,10},{10,... | collective-permute-start | bytes 147464 | tf_op jit(solution)/shard_map/ppermute | solution.py:366
  17.4 3.1 %collective-permute-start.6 = (bf16[96,256]{1,0:T(8,128)(2,1)S(1)}, bf16[96,256]{1,0:T(8,128)(2,1)S(1)}, u32[]{:S(2)}, u32[]{:S(2)}) collective-permute-start(bf16[96,256]{1,0:T(8,128)(2,1)S(1)} %get-tuple-element.76), channel_id=1, source_target_pairs={{0,1},{1,0},{2,3},{3,2},{4,5},{5,4},{6,7},{7,6},{8,9},{9,8},{10,11... | collective-permute-start | bytes 147464 | tf_op jit(solution)/shard_map/ppermute | solution.py:366
  17.6 4.1 %collective-permute-start.7 = (bf16[96,256]{1,0:T(8,128)(2,1)S(1)}, bf16[96,256]{1,0:T(8,128)(2,1)S(1)}, u32[]{:S(2)}, u32[]{:S(2)}) collective-permute-start(bf16[96,256]{1,0:T(8,128)(2,1)S(1)} %get-tuple-element.77), channel_id=1, source_target_pairs={{0,8},{1,2},{2,1},{3,4},{4,3},{5,6},{6,5},{7,15},{8,0},{9,10},{10,... | collective-permute-start | bytes 147464 | tf_op jit(solution)/shard_map/ppermute | solution.py:366
  22.3 10.9 %collective-permute-start.10 = (bf16[96,768]{1,0:T(8,128)(2,1)S(1)}, bf16[96,768]{1,0:T(8,128)(2,1)S(1)}, u32[]{:S(2)}, u32[]{:S(2)}) collective-permute-start(bf16[96,768]{1,0:T(8,128)(2,1)S(1)} %shard_map.77.inner_ref), channel_id=1, source_target_pairs={{0,8},{8,0},{16,24},{24,16},{1,9},{9,1},{17,25},{25,17},{2,10},{10... | collective-permute-start | bytes 442376 | tf_op jit(solution)/shard_map/ppermute | solution.py:376
  23.9 9.4 %collective-permute-start.11 = (bf16[96,768]{1,0:T(8,128)(2,1)S(1)}, bf16[96,768]{1,0:T(8,128)(2,1)S(1)}, u32[]{:S(2)}, u32[]{:S(2)}) collective-permute-start(bf16[96,768]{1,0:T(8,128)(2,1)S(1)} %shard_map.77.inner_ref), channel_id=1, source_target_pairs={{0,16},{8,24},{16,0},{24,8},{1,17},{9,25},{17,1},{25,9},{2,18},{10... | collective-permute-start | bytes 442376 | tf_op jit(solution)/shard_map/ppermute | solution.py:376
  25.4 1.2 %collective-permute-start.8 = (bf16[96,256]{1,0:T(8,128)(2,1)S(1)}, bf16[96,256]{1,0:T(8,128)(2,1)S(1)}, u32[]{:S(2)}, u32[]{:S(2)}) collective-permute-start(bf16[96,256]{1,0:T(8,128)(2,1)S(1)} %get-tuple-element.84), channel_id=1, source_target_pairs={{0,1},{1,0},{2,3},{3,2},{4,5},{5,4},{6,7},{7,6},{8,9},{9,8},{10,11... | collective-permute-start | bytes 147464 | tf_op jit(solution)/shard_map/ppermute | solution.py:366
  25.4 4.1 %collective-permute-start.9 = (bf16[96,256]{1,0:T(8,128)(2,1)S(1)}, bf16[96,256]{1,0:T(8,128)(2,1)S(1)}, u32[]{:S(2)}, u32[]{:S(2)}) collective-permute-start(bf16[96,256]{1,0:T(8,128)(2,1)S(1)} %get-tuple-element.85), channel_id=1, source_target_pairs={{0,8},{1,2},{2,1},{3,4},{4,3},{5,6},{6,5},{7,15},{8,0},{9,10},{10,... | collective-permute-start | bytes 147464 | tf_op jit(solution)/shard_map/ppermute | solution.py:366
  29.6 4.9 %collective-permute-start.12 = (bf16[96,512]{1,0:T(8,128)(2,1)S(1)}, bf16[96,512]{1,0:T(8,128)(2,1)S(1)}, u32[]{:S(2)}, u32[]{:S(2)}) collective-permute-start(bf16[96,512]{1,0:T(8,128)(2,1)S(1)} %shard_map.76.zone_ref.refs_7_), channel_id=1, source_target_pairs={{0,8},{8,0},{16,24},{24,16},{1,9},{9,1},{17,25},{25,17},{2,10},{10... | collective-permute-start | bytes 294920 | tf_op jit(solution)/shard_map/ppermute | solution.py:376
  30.4 4.6 %collective-permute-start.13 = (bf16[96,512]{1,0:T(8,128)(2,1)S(1)}, bf16[96,512]{1,0:T(8,128)(2,1)S(1)}, u32[]{:S(2)}, u32[]{:S(2)}) collective-permute-start(bf16[96,512]{1,0:T(8,128)(2,1)S(1)} %shard_map.76.zone_ref.refs_7_), channel_id=1, source_target_pairs={{0,16},{8,24},{16,0},{24,8},{1,17},{9,25},{17,1},{25,9},{2,18},{10... | collective-permute-start | bytes 294920 | tf_op jit(solution)/shard_map/ppermute | solution.py:376
  35.9 1.4 %collective-permute-start.14 = (bf16[4,96,96]{2,1,0:T(8,128)(2,1)S(1)}, bf16[4,96,96]{2,1,0:T(8,128)(2,1)S(1)}, u32[]{:S(2)}, u32[]{:S(2)}) collective-permute-start(bf16[4,96,96]{2,1,0:T(8,128)(2,1)S(1)} %get-tuple-element.96), channel_id=1, source_target_pairs={{0,1},{1,0},{2,3},{3,2},{4,5},{5,4},{6,7},{7,6},{8,9},{9,8},{10,11... | collective-permute-start | bytes 221192 | tf_op jit(solution)/shard_map/ppermute | solution.py:366
  37.3 5.9 %collective-permute-start.15 = (bf16[96,96]{1,0:T(8,128)(2,1)S(1)}, bf16[96,96]{1,0:T(8,128)(2,1)S(1)}, u32[]{:S(2)}, u32[]{:S(2)}) collective-permute-start(bf16[96,96]{1,0:T(8,128)(2,1)S(1)} %get-tuple-element.97.mine_ref), channel_id=1, source_target_pairs={{0,10},{1,11},{2,8},{3,9},{4,14},{5,15},{6,12},{7,13},{8,2},{9,3},... | collective-permute-start | bytes 55304 | tf_op jit(solution)/shard_map/ppermute | solution.py:387
  38.4 4.9 %collective-permute-start.16 = (bf16[96,96]{1,0:T(8,128)(2,1)S(1)}, bf16[96,96]{1,0:T(8,128)(2,1)S(1)}, u32[]{:S(2)}, u32[]{:S(2)}) collective-permute-start(bf16[96,96]{1,0:T(8,128)(2,1)S(1)} %get-tuple-element.98), channel_id=1, source_target_pairs={{0,2},{1,3},{2,0},{3,1},{4,12},{5,13},{6,4},{7,5},{8,10},{9,11},{1... | collective-permute-start | bytes 55304 | tf_op jit(solution)/shard_map/ppermute | solution.py:387
  40.1 5.0 %collective-permute-start.17 = (bf16[96,96]{1,0:T(8,128)(2,1)S(1)}, bf16[96,96]{1,0:T(8,128)(2,1)S(1)}, u32[]{:S(2)}, u32[]{:S(2)}) collective-permute-start(bf16[96,96]{1,0:T(8,128)(2,1)S(1)} %get-tuple-element.99), channel_id=1, source_target_pairs={{0,4},{1,5},{2,12},{3,13},{4,0},{5,1},{6,2},{7,3},{8,6},{9,7},{10,... | collective-permute-start | bytes 55304 | tf_op jit(solution)/shard_map/ppermute | solution.py:387
  40.6 5.6 %collective-permute-start.18 = (bf16[96,96]{1,0:T(8,128)(2,1)S(1)}, bf16[96,96]{1,0:T(8,128)(2,1)S(1)}, u32[]{:S(2)}, u32[]{:S(2)}) collective-permute-start(bf16[96,96]{1,0:T(8,128)(2,1)S(1)} %get-tuple-element.100), channel_id=1, source_target_pairs={{0,12},{1,13},{2,4},{3,5},{4,2},{5,3},{6,0},{7,1},{8,14},{9,15},{1... | collective-permute-start | bytes 55304 | tf_op jit(solution)/shard_map/ppermute | solution.py:387

commit v3 on v2

--- a/solution.py
+++ b/solution.py
@@ -271,14 +271,17 @@
 
 
 def neighbour_body(inner_ref, beside_ref, across_ref, energy_ref, shift_inner_ref, border_ref, square_ref, diagonal_ref,
-                   open_ref, part_ref, found_ref, other_ref):
-    beside = beside_ref[...]
+                   part_ref, found_ref, other_ref, other_energy_ref, toward_ref):
+    beside, across = beside_ref[...], across_ref[...]
     width = border_ref.shape[1] // 2
+    inside = border_ref[width : width + beside.shape[1], :]
     line = diagonal_ref[...] + (shift_inner_ref[...] + spectrum_center)
-    open_ref[...] = mm(beside, square_ref[...]) + line * beside.astype(F32)
-    part_ref[...] = mm(beside, border_ref[width : width + beside.shape[1], :])
+    energy = (mm(beside, square_ref[...]) + line * beside.astype(F32)).astype(BF16)
+    part_ref[...] = mm(beside, inside)
+    toward_ref[...] = mm(across, inside).astype(BF16)
     inner_found(found_ref, (inner_ref, beside_ref, across_ref), inner_ref, energy_ref)
-    other_ref[...] = mm_nt(across_ref[...], beside)
+    other_ref[...] = mm_nt(across, beside)
+    other_energy_ref[...] = mm_nt(across, energy)
 
 
 def inner_found(found_ref, blocks, states_ref, energy_ref):
@@ -302,7 +305,7 @@
 
 def project_body(square_of_four, scale, energy_zone_ref, found_ref, *refs):
     if square_of_four:
-        (open_ref, part_ref, other_ref, across_ref, shift_zone_ref, border_ref, border_diagonal_ref), refs = refs[:7], refs[7:]
+        (part_ref, other_ref, other_energy_ref, toward_ref, shift_zone_ref, border_ref, border_diagonal_ref), refs = refs[:7], refs[7:]
         *zones, out_ref, give_ref, other_zone_ref = refs
     else:
         *zones, out_ref, give_ref = refs
@@ -319,18 +322,16 @@
                 out_ref[at, core, there] = parts[core].astype(BF16)
             give_ref[at, there] = jnp.where(odd, parts[0], parts[1]).astype(BF16)
 
+    if square_of_four:
+        zone_energy(zones[1], part_ref[...], shift_zone_ref, border_ref, border_diagonal_ref, other_zone_ref)
     for distance, zone in enumerate(zones):
         here = slice(distance * count, (distance + 1) * count)
         states, energy = zone_found(zone, zones[0], energy_zone_ref)
         put(distance, found_ref[here, :count] + states, found_ref[here, count:] + energy)
     if square_of_four:
-        beside_zone = zones[1]
-        width = beside_zone.shape[1] // 2
-        rest = mm_nt(beside_zone[...], border_ref[width : width + open_ref.shape[1], :])
-        energy_inner = (open_ref[...] + rest).astype(BF16)
-        zone_energy(beside_zone, part_ref[...], shift_zone_ref, border_ref, border_diagonal_ref, other_zone_ref)
-        states, energy = zone_found(zones[2], beside_zone, other_zone_ref)
-        put(3, other_ref[...] + states, mm_nt(across_ref[...], energy_inner) + energy)
+        states, energy = zone_found(zones[2], zones[1], other_zone_ref)
+        energy = energy + mm_nt(toward_ref[...], zones[1][...])
+        put(3, other_ref[...] + states, other_energy_ref[...] + energy)
 
 
 def halve_body(mine_ref, got_ref, *pieces):
@@ -466,14 +467,14 @@
         (zone_k, inner_k, shift_inner, shift_zone, border, border_diagonal, square, diagonal), work,
     )
     extra, scratch = (), []
+    pair_of = SHAPE((count, count), F32)
     found_of = SHAPE((len(inner_blocks) * count, 2 * count), F32)
     if square_of_four:
-        opened, part_x, found, other = call(
-            neighbour_body,
-            (SHAPE((count, inside), F32), sums_of, found_of, SHAPE((count, count), F32)),
+        part_x, found, *other = call(
+            neighbour_body, (sums_of, found_of, pair_of, pair_of, zone),
             (*inner_blocks, energy, shift_inner, border, square, diagonal), work // 2,
         )
-        extra = (opened, part_x, other, inner_blocks[2], shift_zone, border, border_diagonal)
+        extra = (part_x, *other, shift_zone, border, border_diagonal)
         scratch = [pltpu.VMEM((count, 4 * rim), BF16)]
     else:
         found = call(gram_body, found_of, (*inner_blocks, energy), work)

time: 47 us -> 46.7 us (level)
  transfers between devices with their start and end apart: 19 -> 19, of which waited for: 10 -> 10; matrix products, arithmetic and copies ran while one was open for 0% -> 0% of each run, Pallas kernels for 23% -> 24%
where the time goes in v3:
time: 46.7 us; the launch traced here: 46.5 us
  starting transfers between devices  20.2 us (43%)
  Pallas kernels  15 us (32%)
  waiting for transfers between devices  10.5 us (22%)
  between operations  0.8 us (2%)
    pallas_call x16, Pallas kernels, call(): pl.pallas_call(body, out_shape=outs, in_specs=where, out_specs=jax.tree.m...  15 us
    ppermute x11, starting transfers between devices, swap(): return lax.ppermute(block, ('state', 'space'), route)  8.8 us
    ppermute x11, waiting for transfers between devices, swap(): return lax.ppermute(block, ('state', 'space'), route)  6.64 us
    ppermute x4, starting transfers between devices, share_out(): return lax.ppermute(block, ('state', 'space'), route)  5.91 us
    ppermute x4, starting transfers between devices, across(): lax.ppermute(block, axis, [(i, i ^ distance) for i in range(lax.axis_size...  5.45 us
    ppermute x4, waiting for transfers between devices, share_out(): return lax.ppermute(block, ('state', 'space'), route)  2.97 us
  transfers between devices with their start and end apart: 19, of which 10 were waited for; matrix products, arithmetic and copies ran while one was open for 0% of the time, Pallas kernels for 24%

profile of v3, /device:TPU:0, one launch (start us, length us, event | category | flops | bytes accessed | tf_op | source)
XLA Modules:
  0.0 46.5 jit_solution(6986609183547934892)
XLA Ops:
  0.7 0.9 %shard_map.67 = (bf16[112,128]{1,0:T(8,128)(2,1)S(1)}, bf16[112,128]{1,0:T(8,128)(2,1)S(1)}, s32[2,512]{1,0:T(2,128)S(1)}) custom-call(bf16[96,1024]{1,0:T(8,128)(2,1)} %states_ref.3, f32[1,1024]{1,0:T(1,128)} %bitcast.3, s32[2,512]{1,0:T(2,128)} %index_ref.1), custom_call_target="tpu_custom_call" | custom-call | bytes 4194304 | tf_op jit(solution)/shard_map/pallas_call | solution.py:26
  2.1 2.6 %collective-permute-start.1 = (bf16[112,128]{1,0:T(8,128)(2,1)S(1)}, bf16[112,128]{1,0:T(8,128)(2,1)S(1)}, u32[]{:S(2)}, u32[]{:S(2)}) collective-permute-start(bf16[112,128]{1,0:T(8,128)(2,1)S(1)} %get-tuple-element.55), channel_id=1, source_target_pairs={{0,8},{1,2},{2,1},{3,4},{4,3},{5,6},{6,5},{7,15},{8,0},{9,10},{10,... | collective-permute-start | bytes 86024 | tf_op jit(solution)/shard_map/ppermute | solution.py:367
  4.6 2.8 %shard_map.68 = (bf16[1280,1024]{1,0:T(8,128)(2,1)S(1)}, bf16[1280,1024]{1,0:T(8,128)(2,1)S(1)}) custom-call(s32[2,512]{1,0:T(2,128)S(1)} %get-tuple-element.56.index_ref, bf16[2,512,512]{2,1,0:T(8,128)(2,1)} %cells_ref.1), custom_call_target="tpu_custom_call" | custom-call | flops 1342177280 | bytes 4194304 | tf_op jit(solution)/shard_map/pallas_call | solution.py:26
  7.4 0.9 %shard_map.69 = (bf16[96,768]{1,0:T(8,128)(2,1)S(1)}, bf16[96,512]{1,0:T(8,128)(2,1)S(1)}, f32[1,768]{1,0:T(1,128)S(1)}, f32[1,512]{1,0:T(1,128)S(1)}, bf16[96,1...) custom-call(bf16[96,1024]{1,0:T(8,128)(2,1)S(1)} %copy-done, ...), custom_call_target="tpu_custom_call" | custom-call | flops 314572800 | bytes 4194304 | tf_op jit(solution)/shard_map/pallas_call | solution.py:26
  8.6 1.5 %collective-permute-start.3 = (bf16[96,256]{1,0:T(8,128)(2,1)S(1)}, bf16[96,256]{1,0:T(8,128)(2,1)S(1)}, u32[]{:S(2)}, u32[]{:S(2)}) collective-permute-start(bf16[96,256]{1,0:T(8,128)(2,1)S(1)} %get-tuple-element.61), channel_id=1, source_target_pairs={{0,8},{1,2},{2,1},{3,4},{4,3},{5,6},{6,5},{7,15},{8,0},{9,10},{10,... | collective-permute-start | bytes 147464 | tf_op jit(solution)/shard_map/ppermute | solution.py:367
  10.1 2.1 %shard_map.70 = (bf16[96,768]{1,0:T(8,128)(2,1)S(1)}, bf16[1280,512]{1,0:T(8,128)(2,1)S(1)}, f32[1,512]{1,0:T(1,128)S(1)}, f32[96,512]{1,0:T(8,128)S(1)}) custom-call(bf16[96,768]{1,0:T(8,128)(2,1)S(1)} %get-tuple-element.64.inner_ref.old_ref, bf16[96,1024]{1,0:T(8,128)(2,1)S(1)} %get-tuple-element.65.picked_ref, ...), custom_call_target="tpu_custom_call" | custom-call | flops 1342177280 | bytes 4194304 | tf_op jit(solution)/shard_map/pallas_call | solution.py:26
  13.0 1.5 %collective-permute-start.5 = (bf16[96,256]{1,0:T(8,128)(2,1)S(1)}, bf16[96,256]{1,0:T(8,128)(2,1)S(1)}, u32[]{:S(2)}, u32[]{:S(2)}) collective-permute-start(bf16[96,256]{1,0:T(8,128)(2,1)S(1)} %get-tuple-element.72), channel_id=1, source_target_pairs={{0,8},{1,2},{2,1},{3,4},{4,3},{5,6},{6,5},{7,15},{8,0},{9,10},{10,... | collective-permute-start | bytes 147464 | tf_op jit(solution)/shard_map/ppermute | solution.py:367
  14.6 2.4 %shard_map.72 = (bf16[768,768]{1,0:T(8,128)(2,1)S(1)}, f32[1,768]{1,0:T(1,128)S(1)}, bf16[96,768]{1,0:T(8,128)(2,1)S(1)}, f32[96,512]{1,0:T(8,128)S(1)}) custom-call(bf16[96,512]{1,0:T(8,128)(2,1)S(1)} %get-tuple-element.73.zone_ref.mid_ref.rest_0_, bf16[96,768]{1,0:T(8,128)(2,1)S(1)} %get-tuple-element.74.inner_ref.old_ref, ...), custom_call_target="tpu_custom_call" | custom-call | flops 1207959552 | bytes 4194304 | tf_op jit(solution)/shard_map/pallas_call | solution.py:26
  17.6 1.5 %collective-permute-start.7 = (bf16[96,256]{1,0:T(8,128)(2,1)S(1)}, bf16[96,256]{1,0:T(8,128)(2,1)S(1)}, u32[]{:S(2)}, u32[]{:S(2)}) collective-permute-start(bf16[96,256]{1,0:T(8,128)(2,1)S(1)} %get-tuple-element.78), channel_id=1, source_target_pairs={{0,8},{1,2},{2,1},{3,4},{4,3},{5,6},{6,5},{7,15},{8,0},{9,10},{10,... | collective-permute-start | bytes 147464 | tf_op jit(solution)/shard_map/ppermute | solution.py:367
  19.1 1.4 %shard_map.74 = (bf16[96,768]{1,0:T(8,128)(2,1)}, f32[96,512]{1,0:T(8,128)S(1)}, f32[96,768]{1,0:T(8,128)S(1)}) custom-call(bf16[96,512]{1,0:T(8,128)(2,1)S(1)} %get-tuple-element.79.zone_ref.mid_ref.old_ref, bf16[96,768]{1,0:T(8,128)(2,1)S(1)} %get-tuple-element.80.inner_ref.old_ref, bf16[96,768]{1,0:T(8,128)(2,1)S(1)} %get-tuple-element.74.inner_ref.old_ref, ...), custom_call_target="tpu_custom_call" | custom-call | flops 314572800 | bytes 4194304 | tf_op jit(solution)/shard_map/pallas_call | solution.py:26
  20.5 1.2 %collective-permute-done.7.got_b_ref = bf16[96,256]{1,0:T(8,128)(2,1)S(1)} collective-permute-done((bf16[96,256]{1,0:T(8,128)(2,1)S(1)}, bf16[96,256]{1,0:T(8,128)(2,1)S(1)}, u32[]{:S(2)}, u32[]{:S(2)}) %collective-permute-start.7) | collective-permute-done | bytes 49184 | tf_op jit(solution)/shard_map/ppermute | solution.py:367
  22.3 1.6 %collective-permute-start.10 = (bf16[96,768]{1,0:T(8,128)(2,1)S(1)}, bf16[96,768]{1,0:T(8,128)(2,1)S(1)}, u32[]{:S(2)}, u32[]{:S(2)}) collective-permute-start(bf16[96,768]{1,0:T(8,128)(2,1)S(1)} %shard_map.77.inner_ref), channel_id=1, source_target_pairs={{0,8},{8,0},{16,24},{24,16},{1,9},{9,1},{17,25},{25,17},{2,10},{10... | collective-permute-start | bytes 442376 | tf_op jit(solution)/shard_map/ppermute | solution.py:377
  23.9 1.5 %collective-permute-start.11 = (bf16[96,768]{1,0:T(8,128)(2,1)S(1)}, bf16[96,768]{1,0:T(8,128)(2,1)S(1)}, u32[]{:S(2)}, u32[]{:S(2)}) collective-permute-start(bf16[96,768]{1,0:T(8,128)(2,1)S(1)} %shard_map.77.inner_ref), channel_id=1, source_target_pairs={{0,16},{8,24},{16,0},{24,8},{1,17},{9,25},{17,1},{25,9},{2,18},{10... | collective-permute-start | bytes 442376 | tf_op jit(solution)/shard_map/ppermute | solution.py:377
  26.6 2.9 %collective-permute-done.9.got_b_ref = bf16[96,256]{1,0:T(8,128)(2,1)S(1)} collective-permute-done((bf16[96,256]{1,0:T(8,128)(2,1)S(1)}, bf16[96,256]{1,0:T(8,128)(2,1)S(1)}, u32[]{:S(2)}, u32[]{:S(2)}) %collective-permute-start.9) | collective-permute-done | bytes 49184 | tf_op jit(solution)/shard_map/ppermute | solution.py:367
  29.6 0.8 %collective-permute-start.12 = (bf16[96,512]{1,0:T(8,128)(2,1)S(1)}, bf16[96,512]{1,0:T(8,128)(2,1)S(1)}, u32[]{:S(2)}, u32[]{:S(2)}) collective-permute-start(bf16[96,512]{1,0:T(8,128)(2,1)S(1)} %shard_map.76.zone_ref.refs_7_), channel_id=1, source_target_pairs={{0,8},{8,0},{16,24},{24,16},{1,9},{9,1},{17,25},{25,17},{2,10},{10... | collective-permute-start | bytes 294920 | tf_op jit(solution)/shard_map/ppermute | solution.py:377
  30.4 1.5 %collective-permute-start.13 = (bf16[96,512]{1,0:T(8,128)(2,1)S(1)}, bf16[96,512]{1,0:T(8,128)(2,1)S(1)}, u32[]{:S(2)}, u32[]{:S(2)}) collective-permute-start(bf16[96,512]{1,0:T(8,128)(2,1)S(1)} %shard_map.76.zone_ref.refs_7_), channel_id=1, source_target_pairs={{0,16},{8,24},{16,0},{24,8},{1,17},{9,25},{17,1},{25,9},{2,18},{10... | collective-permute-start | bytes 294920 | tf_op jit(solution)/shard_map/ppermute | solution.py:377
  31.9 1.3 %shard_map.78 = (bf16[96,768]{1,0:T(8,128)(2,1)S(1)}, bf16[96,512]{1,0:T(8,128)(2,1)S(1)}, bf16[96,1024]{1,0:T(8,128)(2,1)}) custom-call(bf16[96,512]{1,0:T(8,128)(2,1)S(1)} %shard_map.76.zone_ref.refs_7_, bf16[96,768]{1,0:T(8,128)(2,1)S(1)} %shard_map.77.inner_ref, f32[1,768]{1,0:T(1,128)S(1)} %get-tuple-element.66.shift_inner_ref, ...), custom_call_target="tpu_custom_call" | custom-call | flops 314572800 | bytes 4194304 | tf_op jit(solution)/shard_map/pallas_call | solution.py:26
  33.2 0.9 %shard_map.79 = (f32[96,512]{1,0:T(8,128)S(1)}, f32[288,192]{1,0:T(8,128)S(1)}, f32[96,96]{1,0:T(8,128)S(1)}, f32[96,96]{1,0:T(8,128)S(1)}, bf16[96,512]{1,0:T(8,128)(2,1)S(1)}) custom-call(bf16[96,768]{1,0:T(8,128)(2,1)S(1)} %shard_map.77.inner_ref, bf16[96,768]{1,0:T(8,128)(2,1)S(1)} %collective-permute-done.10.beside_ref, ...), custom_call_target="tpu_custom_call" | custom-call | flops 157286400 | bytes 4194304 | tf_op jit(solution)/shard_map/pallas_call | solution.py:26
  35.6 1.3 %collective-permute-done.14.got_ref = bf16[4,96,96]{2,1,0:T(8,128)(2,1)S(1)} collective-permute-done((bf16[4,96,96]{2,1,0:T(8,128)(2,1)S(1)}, bf16[4,96,96]{2,1,0:T(8,128)(2,1)S(1)}, u32[]{:S(2)}, u32[]{:S(2)}) %collective-permute-start.14) | collective-permute-done | bytes 73760 | tf_op jit(solution)/shard_map/ppermute | solution.py:367
  37.0 1.0 %collective-permute-start.15 = (bf16[96,96]{1,0:T(8,128)(2,1)S(1)}, bf16[96,96]{1,0:T(8,128)(2,1)S(1)}, u32[]{:S(2)}, u32[]{:S(2)}) collective-permute-start(bf16[96,96]{1,0:T(8,128)(2,1)S(1)} %get-tuple-element.99.mine_ref), channel_id=1, source_target_pairs={{0,10},{1,11},{2,8},{3,9},{4,14},{5,15},{6,12},{7,13},{8,2},{9,3},... | collective-permute-start | bytes 55304 | tf_op jit(solution)/shard_map/ppermute | solution.py:388
  38.0 1.8 %collective-permute-start.16 = (bf16[96,96]{1,0:T(8,128)(2,1)S(1)}, bf16[96,96]{1,0:T(8,128)(2,1)S(1)}, u32[]{:S(2)}, u32[]{:S(2)}) collective-permute-start(bf16[96,96]{1,0:T(8,128)(2,1)S(1)} %get-tuple-element.100), channel_id=1, source_target_pairs={{0,2},{1,3},{2,0},{3,1},{4,12},{5,13},{6,4},{7,5},{8,10},{9,11},{1... | collective-permute-start | bytes 55304 | tf_op jit(solution)/shard_map/ppermute | solution.py:388
  40.2 2.7 %collective-permute-start.18 = (bf16[96,96]{1,0:T(8,128)(2,1)S(1)}, bf16[96,96]{1,0:T(8,128)(2,1)S(1)}, u32[]{:S(2)}, u32[]{:S(2)}) collective-permute-start(bf16[96,96]{1,0:T(8,128)(2,1)S(1)} %get-tuple-element.102), channel_id=1, source_target_pairs={{0,12},{1,13},{2,4},{3,5},{4,2},{5,3},{6,0},{7,1},{8,14},{9,15},{1... | collective-permute-start | bytes 55304 | tf_op jit(solution)/shard_map/ppermute | solution.py:388
  42.9 1.8 %collective-permute-done.17.refs_2_ = bf16[96,96]{1,0:T(8,128)(2,1)S(1)} collective-permute-done((bf16[96,96]{1,0:T(8,128)(2,1)S(1)}, bf16[96,96]{1,0:T(8,128)(2,1)S(1)}, u32[]{:S(2)}, u32[]{:S(2)}) %collective-permute-start.17) | collective-permute-done | bytes 18464 | tf_op jit(solution)/shard_map/ppermute | solution.py:388
  44.7 1.2 %collective-permute-done.18.refs_3_ = bf16[96,96]{1,0:T(8,128)(2,1)S(1)} collective-permute-done((bf16[96,96]{1,0:T(8,128)(2,1)S(1)}, bf16[96,96]{1,0:T(8,128)(2,1)S(1)}, u32[]{:S(2)}, u32[]{:S(2)}) %collective-permute-start.18) | collective-permute-done | bytes 18464 | tf_op jit(solution)/shard_map/ppermute | solution.py:388
  (34 shorter events, 6.8 us)
Async XLA Ops:
  0.6 6.8 %copy-start = (bf16[96,1024]{1,0:T(8,128)(2,1)S(1)}, bf16[96,1024]{1,0:T(8,128)(2,1)}, u32[]{:S(2)}) copy-start(bf16[96,1024]{1,0:T(8,128)(2,1)} %states_ref.3) | copy-start | bytes 589828
  0.6 6.8 %copy-start.1 = (f32[1024]{0:T(1024)S(1)}, f32[1024]{0:T(1024)}, u32[]{:S(2)}) copy-start(f32[1024]{0:T(1024)} %param.7) | copy-start | bytes 12292
  1.5 5.9 %collective-permute-start = (bf16[112,128]{1,0:T(8,128)(2,1)S(1)}, bf16[112,128]{1,0:T(8,128)(2,1)S(1)}, u32[]{:S(2)}, u32[]{:S(2)}) collective-permute-start(bf16[112,128]{1,0:T(8,128)(2,1)S(1)} %get-tuple-element.54), channel_id=1, source_target_pairs={{0,1},{1,0},{2,3},{3,2},{4,5},{5,4},{6,7},{7,6},{8,9},{9,8},{10,11... | collective-permute-start | bytes 86024 | tf_op jit(solution)/shard_map/ppermute | solution.py:367
  2.1 5.3 %collective-permute-start.1 = (bf16[112,128]{1,0:T(8,128)(2,1)S(1)}, bf16[112,128]{1,0:T(8,128)(2,1)S(1)}, u32[]{:S(2)}, u32[]{:S(2)}) collective-permute-start(bf16[112,128]{1,0:T(8,128)(2,1)S(1)} %get-tuple-element.55), channel_id=1, source_target_pairs={{0,8},{1,2},{2,1},{3,4},{4,3},{5,6},{6,5},{7,15},{8,0},{9,10},{10,... | collective-permute-start | bytes 86024 | tf_op jit(solution)/shard_map/ppermute | solution.py:367
  8.3 3.9 %collective-permute-start.2 = (bf16[96,256]{1,0:T(8,128)(2,1)S(1)}, bf16[96,256]{1,0:T(8,128)(2,1)S(1)}, u32[]{:S(2)}, u32[]{:S(2)}) collective-permute-start(bf16[96,256]{1,0:T(8,128)(2,1)S(1)} %get-tuple-element.60), channel_id=1, source_target_pairs={{0,1},{1,0},{2,3},{3,2},{4,5},{5,4},{6,7},{7,6},{8,9},{9,8},{10,11... | collective-permute-start | bytes 147464 | tf_op jit(solution)/shard_map/ppermute | solution.py:367
  8.6 4.1 %collective-permute-start.3 = (bf16[96,256]{1,0:T(8,128)(2,1)S(1)}, bf16[96,256]{1,0:T(8,128)(2,1)S(1)}, u32[]{:S(2)}, u32[]{:S(2)}) collective-permute-start(bf16[96,256]{1,0:T(8,128)(2,1)S(1)} %get-tuple-element.61), channel_id=1, source_target_pairs={{0,8},{1,2},{2,1},{3,4},{4,3},{5,6},{6,5},{7,15},{8,0},{9,10},{10,... | collective-permute-start | bytes 147464 | tf_op jit(solution)/shard_map/ppermute | solution.py:367
  12.9 4.0 %collective-permute-start.4 = (bf16[96,256]{1,0:T(8,128)(2,1)S(1)}, bf16[96,256]{1,0:T(8,128)(2,1)S(1)}, u32[]{:S(2)}, u32[]{:S(2)}) collective-permute-start(bf16[96,256]{1,0:T(8,128)(2,1)S(1)} %get-tuple-element.71), channel_id=1, source_target_pairs={{0,1},{1,0},{2,3},{3,2},{4,5},{5,4},{6,7},{7,6},{8,9},{9,8},{10,11... | collective-permute-start | bytes 147464 | tf_op jit(solution)/shard_map/ppermute | solution.py:367
  13.0 4.1 %collective-permute-start.5 = (bf16[96,256]{1,0:T(8,128)(2,1)S(1)}, bf16[96,256]{1,0:T(8,128)(2,1)S(1)}, u32[]{:S(2)}, u32[]{:S(2)}) collective-permute-start(bf16[96,256]{1,0:T(8,128)(2,1)S(1)} %get-tuple-element.72), channel_id=1, source_target_pairs={{0,8},{1,2},{2,1},{3,4},{4,3},{5,6},{6,5},{7,15},{8,0},{9,10},{10,... | collective-permute-start | bytes 147464 | tf_op jit(solution)/shard_map/ppermute | solution.py:367
  17.4 3.1 %collective-permute-start.6 = (bf16[96,256]{1,0:T(8,128)(2,1)S(1)}, bf16[96,256]{1,0:T(8,128)(2,1)S(1)}, u32[]{:S(2)}, u32[]{:S(2)}) collective-permute-start(bf16[96,256]{1,0:T(8,128)(2,1)S(1)} %get-tuple-element.77), channel_id=1, source_target_pairs={{0,1},{1,0},{2,3},{3,2},{4,5},{5,4},{6,7},{7,6},{8,9},{9,8},{10,11... | collective-permute-start | bytes 147464 | tf_op jit(solution)/shard_map/ppermute | solution.py:367
  17.6 4.1 %collective-permute-start.7 = (bf16[96,256]{1,0:T(8,128)(2,1)S(1)}, bf16[96,256]{1,0:T(8,128)(2,1)S(1)}, u32[]{:S(2)}, u32[]{:S(2)}) collective-permute-start(bf16[96,256]{1,0:T(8,128)(2,1)S(1)} %get-tuple-element.78), channel_id=1, source_target_pairs={{0,8},{1,2},{2,1},{3,4},{4,3},{5,6},{6,5},{7,15},{8,0},{9,10},{10,... | collective-permute-start | bytes 147464 | tf_op jit(solution)/shard_map/ppermute | solution.py:367
  22.3 10.9 %collective-permute-start.10 = (bf16[96,768]{1,0:T(8,128)(2,1)S(1)}, bf16[96,768]{1,0:T(8,128)(2,1)S(1)}, u32[]{:S(2)}, u32[]{:S(2)}) collective-permute-start(bf16[96,768]{1,0:T(8,128)(2,1)S(1)} %shard_map.77.inner_ref), channel_id=1, source_target_pairs={{0,8},{8,0},{16,24},{24,16},{1,9},{9,1},{17,25},{25,17},{2,10},{10... | collective-permute-start | bytes 442376 | tf_op jit(solution)/shard_map/ppermute | solution.py:377
  23.9 9.4 %collective-permute-start.11 = (bf16[96,768]{1,0:T(8,128)(2,1)S(1)}, bf16[96,768]{1,0:T(8,128)(2,1)S(1)}, u32[]{:S(2)}, u32[]{:S(2)}) collective-permute-start(bf16[96,768]{1,0:T(8,128)(2,1)S(1)} %shard_map.77.inner_ref), channel_id=1, source_target_pairs={{0,16},{8,24},{16,0},{24,8},{1,17},{9,25},{17,1},{25,9},{2,18},{10... | collective-permute-start | bytes 442376 | tf_op jit(solution)/shard_map/ppermute | solution.py:377
  25.4 1.2 %collective-permute-start.8 = (bf16[96,256]{1,0:T(8,128)(2,1)S(1)}, bf16[96,256]{1,0:T(8,128)(2,1)S(1)}, u32[]{:S(2)}, u32[]{:S(2)}) collective-permute-start(bf16[96,256]{1,0:T(8,128)(2,1)S(1)} %get-tuple-element.85), channel_id=1, source_target_pairs={{0,1},{1,0},{2,3},{3,2},{4,5},{5,4},{6,7},{7,6},{8,9},{9,8},{10,11... | collective-permute-start | bytes 147464 | tf_op jit(solution)/shard_map/ppermute | solution.py:367
  25.4 4.1 %collective-permute-start.9 = (bf16[96,256]{1,0:T(8,128)(2,1)S(1)}, bf16[96,256]{1,0:T(8,128)(2,1)S(1)}, u32[]{:S(2)}, u32[]{:S(2)}) collective-permute-start(bf16[96,256]{1,0:T(8,128)(2,1)S(1)} %get-tuple-element.86), channel_id=1, source_target_pairs={{0,8},{1,2},{2,1},{3,4},{4,3},{5,6},{6,5},{7,15},{8,0},{9,10},{10,... | collective-permute-start | bytes 147464 | tf_op jit(solution)/shard_map/ppermute | solution.py:367
  29.6 4.9 %collective-permute-start.12 = (bf16[96,512]{1,0:T(8,128)(2,1)S(1)}, bf16[96,512]{1,0:T(8,128)(2,1)S(1)}, u32[]{:S(2)}, u32[]{:S(2)}) collective-permute-start(bf16[96,512]{1,0:T(8,128)(2,1)S(1)} %shard_map.76.zone_ref.refs_7_), channel_id=1, source_target_pairs={{0,8},{8,0},{16,24},{24,16},{1,9},{9,1},{17,25},{25,17},{2,10},{10... | collective-permute-start | bytes 294920 | tf_op jit(solution)/shard_map/ppermute | solution.py:377
  30.4 4.6 %collective-permute-start.13 = (bf16[96,512]{1,0:T(8,128)(2,1)S(1)}, bf16[96,512]{1,0:T(8,128)(2,1)S(1)}, u32[]{:S(2)}, u32[]{:S(2)}) collective-permute-start(bf16[96,512]{1,0:T(8,128)(2,1)S(1)} %shard_map.76.zone_ref.refs_7_), channel_id=1, source_target_pairs={{0,16},{8,24},{16,0},{24,8},{1,17},{9,25},{17,1},{25,9},{2,18},{10... | collective-permute-start | bytes 294920 | tf_op jit(solution)/shard_map/ppermute | solution.py:377
  35.6 1.4 %collective-permute-start.14 = (bf16[4,96,96]{2,1,0:T(8,128)(2,1)S(1)}, bf16[4,96,96]{2,1,0:T(8,128)(2,1)S(1)}, u32[]{:S(2)}, u32[]{:S(2)}) collective-permute-start(bf16[4,96,96]{2,1,0:T(8,128)(2,1)S(1)} %get-tuple-element.98), channel_id=1, source_target_pairs={{0,1},{1,0},{2,3},{3,2},{4,5},{5,4},{6,7},{7,6},{8,9},{9,8},{10,11... | collective-permute-start | bytes 221192 | tf_op jit(solution)/shard_map/ppermute | solution.py:367
  37.0 5.9 %collective-permute-start.15 = (bf16[96,96]{1,0:T(8,128)(2,1)S(1)}, bf16[96,96]{1,0:T(8,128)(2,1)S(1)}, u32[]{:S(2)}, u32[]{:S(2)}) collective-permute-start(bf16[96,96]{1,0:T(8,128)(2,1)S(1)} %get-tuple-element.99.mine_ref), channel_id=1, source_target_pairs={{0,10},{1,11},{2,8},{3,9},{4,14},{5,15},{6,12},{7,13},{8,2},{9,3},... | collective-permute-start | bytes 55304 | tf_op jit(solution)/shard_map/ppermute | solution.py:388
  38.0 4.9 %collective-permute-start.16 = (bf16[96,96]{1,0:T(8,128)(2,1)S(1)}, bf16[96,96]{1,0:T(8,128)(2,1)S(1)}, u32[]{:S(2)}, u32[]{:S(2)}) collective-permute-start(bf16[96,96]{1,0:T(8,128)(2,1)S(1)} %get-tuple-element.100), channel_id=1, source_target_pairs={{0,2},{1,3},{2,0},{3,1},{4,12},{5,13},{6,4},{7,5},{8,10},{9,11},{1... | collective-permute-start | bytes 55304 | tf_op jit(solution)/shard_map/ppermute | solution.py:388
  39.7 5.0 %collective-permute-start.17 = (bf16[96,96]{1,0:T(8,128)(2,1)S(1)}, bf16[96,96]{1,0:T(8,128)(2,1)S(1)}, u32[]{:S(2)}, u32[]{:S(2)}) collective-permute-start(bf16[96,96]{1,0:T(8,128)(2,1)S(1)} %get-tuple-element.101), channel_id=1, source_target_pairs={{0,4},{1,5},{2,12},{3,13},{4,0},{5,1},{6,2},{7,3},{8,6},{9,7},{10,... | collective-permute-start | bytes 55304 | tf_op jit(solution)/shard_map/ppermute | solution.py:388
  40.2 5.6 %collective-permute-start.18 = (bf16[96,96]{1,0:T(8,128)(2,1)S(1)}, bf16[96,96]{1,0:T(8,128)(2,1)S(1)}, u32[]{:S(2)}, u32[]{:S(2)}) collective-permute-start(bf16[96,96]{1,0:T(8,128)(2,1)S(1)} %get-tuple-element.102), channel_id=1, source_target_pairs={{0,12},{1,13},{2,4},{3,5},{4,2},{5,3},{6,0},{7,1},{8,14},{9,15},{1... | collective-permute-start | bytes 55304 | tf_op jit(solution)/shard_map/ppermute | solution.py:388

commit v4 on v3

--- a/solution.py
+++ b/solution.py
@@ -61,7 +61,7 @@
 
 
 def halo_body(states_ref, potential_ref, index_ref,
-              give_a_ref, give_b_ref, local_ref, low_ref, high_ref, row_ref, sem):
+              give_a_ref, give_b_ref, row_ref, local_ref, low_ref, high_ref, sem):
     count, owned = states_ref.shape
     rim = low_ref.shape[1]
     copies = [
@@ -90,24 +90,30 @@
         ).astype(BF16)
 
 
-def spread_body(index_ref, cells_ref, hot_ref, wide_ref, cells, sem):
-    copy = pltpu.make_async_copy(cells_ref, cells, sem)
-    copy.start()
+def spread_body(index_ref, states_ref, cells_ref, hot_ref, wide_ref, picked_ref, here_ref, cells_out_ref, sem):
+    states_copy = pltpu.make_async_copy(states_ref, here_ref, sem.at[0])
+    cells_copy = pltpu.make_async_copy(cells_ref, cells_out_ref, sem.at[1])
+    states_copy.start()
+    cells_copy.start()
     number, nodes, _ = cells_ref.shape
     extent = hot_ref.shape[0]
     rim = nodes // 4
-    offset = lax.axis_index("space") * (extent - 2 * rim) - rim
+    width = 2 * rim
+    offset = lax.axis_index("space") * (extent - width) - rim
     for c in range(number):
         index = index_ref[c : c + 1, :] - offset
         hot = lax.broadcasted_iota(jnp.int32, (extent, nodes), 0) == index
         hot_ref[:, c * nodes : (c + 1) * nodes] = hot.astype(BF16)
-    copy.wait()
+    states_copy.wait()
+    picked_ref[...] = mm(here_ref[...], hot_ref[rim : extent - rim, :]).astype(BF16)
+    cells_copy.wait()
     for c in range(number):
         here = slice(c * nodes, (c + 1) * nodes)
-        wide_ref[:, here] = mm(hot_ref[:, here], cells[c]).astype(BF16)
-
-
-def first_zone_body(states_ref, halo_a_ref, halo_b_ref, potential_ref, hot_ref, wide_ref,
+        wide_ref[:width, here] = mm(hot_ref[:width, here], cells_out_ref[c]).astype(BF16)
+        wide_ref[width:, here] = mm(hot_ref[extent - width :, here], cells_out_ref[c]).astype(BF16)
+
+
+def first_zone_body(states_ref, halo_a_ref, halo_b_ref, potential_ref, hot_ref, wide_ref, owned_ref,
                     inner_ref, zone_ref, shift_inner_ref, shift_zone_ref, picked_ref, sums_ref, give_a_ref, give_b_ref):
     count, owned = states_ref.shape
     rim = halo_a_ref.shape[1]
@@ -126,15 +132,14 @@
         part = got[count : count + 8]
         shift_zone_ref[:, at : at + rim] = (part[0:1] + part[1:2] + part[2:3]) - spectrum_center
     picked = (
-        mm(inner_ref[...], hot_ref[width : extent - width, :])
-        + mm(zone_ref[:, :width], hot_ref[:width, :])
-        + mm(zone_ref[:, width:], hot_ref[extent - width :, :])
+        owned_ref[...].astype(F32)
+        + mm(zone_ref[:, :rim], hot_ref[:rim, :])
+        + mm(zone_ref[:, width + rim :], hot_ref[extent - rim :, :])
     ).astype(BF16)
     picked_ref[...] = picked
-    low, high = mm_nt(picked, wide_ref[:width, :]), mm_nt(picked, wide_ref[extent - width :, :])
-    sums_ref[:, :width] = low
-    sums_ref[:, width:] = high
-    hand_out(low, high, give_a_ref, give_b_ref)
+    sums = mm_nt(picked, wide_ref[...])
+    sums_ref[...] = sums
+    hand_out(sums[:, :width], sums[:, width:], give_a_ref, give_b_ref)
 
 
 def take_diagonal(rows, start, matrix_ref, diagonal_ref, at):
@@ -148,21 +153,24 @@
     matrix_ref[start : start + size, at : at + size] = jnp.where(same, 0.0, square).astype(BF16)
 
 
-def first_inner_body(inner_ref, picked_ref, shift_inner_ref, hot_ref, wide_ref,
-                     next_ref, border_ref, diagonal_ref, part_ref, columns_ref):
-    extent = border_ref.shape[0]
+def first_inner_body(inner_ref, picked_ref, shift_inner_ref, hot_ref, wide_ref, cells_ref,
+                     next_ref, wide_inner_ref, border_ref, diagonal_ref, part_ref, next_picked_ref, columns_ref):
+    extent = hot_ref.shape[0]
     width = border_ref.shape[1] // 2
     inside = slice(width, extent - width)
-    value = mm_nt(picked_ref[...], wide_ref[inside, :]) + shift_inner_ref[...] * inner_ref[...].astype(F32)
-    following = (value * (1.0 / spectrum_half)).astype(BF16)
-    next_ref[...] = following
+    number, nodes, _ = cells_ref.shape
+    for c in range(number):
+        here = slice(c * nodes, (c + 1) * nodes)
+        wide_inner_ref[:, here] = mm(hot_ref[inside, here], cells_ref[c]).astype(BF16)
+    value = mm_nt(picked_ref[...], wide_inner_ref[...]) + shift_inner_ref[...] * inner_ref[...].astype(F32)
+    next_ref[...] = (value * (1.0 / spectrum_half)).astype(BF16)
     columns_ref[:width, :] = hot_ref[:width, :]
     columns_ref[width:, :] = hot_ref[extent - width :, :]
-    border_ref[inside, :] = mm_nt(wide_ref[inside, :], columns_ref[...]).astype(BF16)
-    for start, at in ((0, 0), (extent - width, width)):
-        rows = mm_nt(wide_ref[start : start + width, :], columns_ref[...])
-        take_diagonal(rows, start, border_ref, diagonal_ref, at)
-    part_ref[...] = mm(following, border_ref[inside, :])
+    for at in (0, width):
+        rows = mm_nt(wide_ref[at : at + width, :], columns_ref[...])
+        take_diagonal(rows, at, border_ref, diagonal_ref, at)
+    next_picked_ref[...] = mm(next_ref[...], hot_ref[inside, :]).astype(BF16)
+    part_ref[...] = mm_nt(next_picked_ref[...], wide_ref[...])
 
 
 def close_zones(sums_ref, got_a_ref, got_b_ref, shift_zone_ref, mid_ref, old_ref, scale, zone_ref):
@@ -177,14 +185,8 @@
 
 
 def zone_sums(zone_ref, part, border_ref, border_diagonal_ref):
-    extent = border_ref.shape[0]
     width = zone_ref.shape[1] // 2
-    sums = (
-        part
-        + mm(zone_ref[:, :width], border_ref[:width, :])
-        + mm(zone_ref[:, width:], border_ref[extent - width :, :])
-        + border_diagonal_ref[...] * zone_ref[...].astype(F32)
-    )
+    sums = part + mm(zone_ref[...], border_ref[...]) + border_diagonal_ref[...] * zone_ref[...].astype(F32)
     return sums[:, :width], sums[:, width:]
 
 
@@ -199,44 +201,55 @@
     hand_out(low, high, give_a_ref, give_b_ref)
 
 
-def inner_sums(zone_ref, inner_ref, border_ref, square_ref, diagonal_ref):
-    width = zone_ref.shape[1] // 2
-    inside = slice(width, width + square_ref.shape[0])
+def inner_sums(zone_ref, inner_ref, columns_ref, square_ref, diagonal_ref):
     return (
-        mm_nt(zone_ref[...], border_ref[inside, :])
+        mm_nt(zone_ref[...], columns_ref[...])
         + mm(inner_ref[...], square_ref[...])
         + diagonal_ref[...] * inner_ref[...].astype(F32)
     )
 
 
-def inner_body(zone_ref, inner_ref, old_ref, shift_inner_ref, border_ref, square_ref, diagonal_ref,
-               next_ref, part_ref, *open_ref):
-    sums = inner_sums(zone_ref, inner_ref, border_ref, square_ref, diagonal_ref)
+def second_inner_body(zone_ref, inner_ref, old_ref, shift_inner_ref, picked_ref, hot_ref, wide_inner_ref,
+                      next_ref, part_ref, columns_ref, square_ref, diagonal_ref, zone_hot_ref):
+    extent = hot_ref.shape[0]
+    width = zone_ref.shape[1] // 2
+    zone_hot_ref[:width, :] = hot_ref[:width, :]
+    zone_hot_ref[width:, :] = hot_ref[extent - width :, :]
+    columns_ref[...] = mm_nt(wide_inner_ref[...], zone_hot_ref[...]).astype(BF16)
+    picked = (picked_ref[...].astype(F32) + mm(zone_ref[...], zone_hot_ref[...])).astype(BF16)
+    sums = mm_nt(picked, wide_inner_ref[...])
     value = (sums + shift_inner_ref[...] * inner_ref[...].astype(F32)) * (2.0 / spectrum_half)
     next_ref[...] = (value - old_ref[...].astype(F32)).astype(BF16)
-    width = zone_ref.shape[1] // 2
-    part_ref[...] = mm(next_ref[...], border_ref[width : width + next_ref.shape[1], :])
-    for ref in open_ref:
-        line = diagonal_ref[...] + shift_inner_ref[...]
-        ref[...] = mm(next_ref[...], square_ref[...]) + line * next_ref[...].astype(F32)
-
-
-def last_inner_body(zone_ref, open_ref, old_ref, border_ref, next_ref):
-    width = zone_ref.shape[1] // 2
-    sums = open_ref[...] + mm_nt(zone_ref[...], border_ref[width : width + next_ref.shape[1], :])
+    part_ref[...] = mm(next_ref[...], columns_ref[...])
+    rows = mm_nt(wide_inner_ref[: square_ref.shape[0], :], hot_ref[width : extent - width, :])
+    diagonal_ref[...] = jnp.zeros_like(diagonal_ref)
+    take_diagonal(rows, 0, square_ref, diagonal_ref, 0)
+
+
+def third_inner_body(zone_ref, inner_ref, old_ref, shift_inner_ref, columns_ref, begun_ref, begun_diagonal_ref,
+                     hot_ref, wide_inner_ref, square_ref, diagonal_ref, next_ref, part_ref, open_ref):
+    size, step = square_ref.shape[0], begun_ref.shape[0]
+    width = (hot_ref.shape[0] - size) // 2
+    square_ref[:step, :] = begun_ref[...]
+    diagonal_ref[...] = begun_diagonal_ref[...]
+    for start in range(step, size, step):
+        rows = mm_nt(wide_inner_ref[start : start + step, :], hot_ref[width : width + size, :])
+        take_diagonal(rows, start, square_ref, diagonal_ref, start)
+    line = diagonal_ref[...] + shift_inner_ref[...]
+    sums = (
+        mm_nt(zone_ref[...], columns_ref[...])
+        + mm(inner_ref[...], square_ref[...])
+        + line * inner_ref[...].astype(F32)
+    )
+    next_ref[...] = (sums * (2.0 / spectrum_half) - old_ref[...].astype(F32)).astype(BF16)
+    part_ref[...] = mm(next_ref[...], columns_ref[...])
+    open_ref[...] = mm(next_ref[...], square_ref[...]) + line * next_ref[...].astype(F32)
+
+
+def last_inner_body(zone_ref, open_ref, old_ref, columns_ref, next_ref):
+    sums = open_ref[...] + mm_nt(zone_ref[...], columns_ref[...])
     value = sums * (2.0 / spectrum_half) - old_ref[...].astype(F32)
     next_ref[...] = value.astype(BF16)
-
-
-def square_body(zone_ref, inner_ref, old_ref, shift_inner_ref, border_ref, hot_ref, wide_ref,
-                square_ref, diagonal_ref, next_ref, part_ref, *open_ref):
-    size = square_ref.shape[0]
-    width = (hot_ref.shape[0] - size) // 2
-    for start in range(0, size, 256):
-        rows = mm_nt(wide_ref[width + start : width + start + 256, :], hot_ref[width : width + size, :])
-        take_diagonal(rows, start, square_ref, diagonal_ref, start)
-    inner_body(zone_ref, inner_ref, old_ref, shift_inner_ref, border_ref, square_ref, diagonal_ref,
-               next_ref, part_ref, *open_ref)
 
 
 def last_zone_body(sums_ref, got_a_ref, got_b_ref, shift_zone_ref, mid_ref, old_ref, zone_ref):
@@ -256,12 +269,12 @@
 
 
 def energy_body(zone_ref, inner_ref, shift_inner_ref, shift_zone_ref,
-                border_ref, border_diagonal_ref, square_ref, diagonal_ref, energy_ref, energy_zone_ref, filtered_ref):
-    sums = inner_sums(zone_ref, inner_ref, border_ref, square_ref, diagonal_ref)
+                border_ref, border_diagonal_ref, columns_ref, square_ref, diagonal_ref, energy_ref, energy_zone_ref, filtered_ref):
+    sums = inner_sums(zone_ref, inner_ref, columns_ref, square_ref, diagonal_ref)
     own = (shift_inner_ref[...] + spectrum_center) * inner_ref[...].astype(F32)
     energy_ref[...] = (sums + own).astype(BF16)
     width = zone_ref.shape[1] // 2
-    part = mm(inner_ref[...], border_ref[width : width + inner_ref.shape[1], :])
+    part = mm(inner_ref[...], columns_ref[...])
     zone_energy(zone_ref, part, shift_zone_ref, border_ref, border_diagonal_ref, energy_zone_ref)
     rim = width // 2
     owned = filtered_ref.shape[1]
@@ -270,15 +283,13 @@
     filtered_ref[:, owned - rim :] = zone_ref[:, width : width + rim]
 
 
-def neighbour_body(inner_ref, beside_ref, across_ref, energy_ref, shift_inner_ref, border_ref, square_ref, diagonal_ref,
+def neighbour_body(inner_ref, beside_ref, across_ref, energy_ref, shift_inner_ref, columns_ref, square_ref, diagonal_ref,
                    part_ref, found_ref, other_ref, other_energy_ref, toward_ref):
     beside, across = beside_ref[...], across_ref[...]
-    width = border_ref.shape[1] // 2
-    inside = border_ref[width : width + beside.shape[1], :]
     line = diagonal_ref[...] + (shift_inner_ref[...] + spectrum_center)
     energy = (mm(beside, square_ref[...]) + line * beside.astype(F32)).astype(BF16)
-    part_ref[...] = mm(beside, inside)
-    toward_ref[...] = mm(across, inside).astype(BF16)
+    part_ref[...] = mm(beside, columns_ref[...])
+    toward_ref[...] = mm(across, columns_ref[...]).astype(BF16)
     inner_found(found_ref, (inner_ref, beside_ref, across_ref), inner_ref, energy_ref)
     other_ref[...] = mm_nt(across, beside)
     other_energy_ref[...] = mm_nt(across, energy)
@@ -401,33 +412,34 @@
     give = SHAPE((count, 2 * rim), BF16)
 
     halo = SHAPE((count + 16, rim), BF16)
-    *gave, local = call(
-        halo_body, (halo, halo, SHAPE(connectivity.shape, connectivity.dtype)),
+    *gave, row, local = call(
+        halo_body,
+        (halo, halo, SHAPE(row.shape, F32), SHAPE(connectivity.shape, connectivity.dtype)),
         (states_in, row, connectivity), 0, raw=(0, 1, 2),
         scratch=[
-            pltpu.VMEM((count, rim), BF16), pltpu.VMEM((count, rim), BF16),
-            pltpu.VMEM((1, owned), F32), pltpu.SemaphoreType.DMA((4,)),
+            pltpu.VMEM((count, rim), BF16), pltpu.VMEM((count, rim), BF16), pltpu.SemaphoreType.DMA((4,)),
         ],
     )
     got = exchange(*gave, n_state, n_space)
     table = SHAPE((extent, cells * nodes), BF16)
-    hot, wide = call(
-        spread_body, (table, table), (local, cell_matrices),
-        2 * extent * cells * nodes * nodes, raw=(1,),
-        scratch=[pltpu.VMEM(cell_matrices.shape, BF16), pltpu.SemaphoreType.DMA],
-    )
+    hot, wide, picked, states_here, cells_here = call(
+        spread_body,
+        (table, SHAPE((4 * rim, cells * nodes), BF16), SHAPE((count, cells * nodes), BF16),
+         SHAPE(states_in.shape, BF16), SHAPE(cell_matrices.shape, BF16)),
+        (local, states_in, cell_matrices), work, raw=(1, 2), scratch=[pltpu.SemaphoreType.DMA((2,))],
+    )
+    border_line, line = SHAPE((1, 4 * rim), F32), SHAPE((1, inside), F32)
     inner_0, zone_0, shift_inner, shift_zone, picked, sums, *gave = call(
         first_zone_body,
-        (inner, zone, SHAPE((1, inside), F32), SHAPE((1, 4 * rim), F32),
-         SHAPE((count, cells * nodes), BF16), sums_of, give, give),
-        (states_in, *got, row, hot, wide), work,
+        (inner, zone, line, border_line, SHAPE((count, cells * nodes), BF16), sums_of, give, give),
+        (states_here, *got, row, hot, wide, picked), work,
     )
     got = exchange(*gave, n_state, n_space)
-    border_line, line = SHAPE((1, 4 * rim), F32), SHAPE((1, inside), F32)
-    inner_1, border, border_diagonal, partial = call(
+    inner_1, wide_inner, border, border_diagonal, partial, picked = call(
         first_inner_body,
-        (inner, SHAPE((extent, 4 * rim), BF16), border_line, sums_of),
-        (inner_0, picked, shift_inner, hot, wide), 8 * extent * rim * cells * nodes,
+        (inner, SHAPE((inside, cells * nodes), BF16), SHAPE((4 * rim, 4 * rim), BF16), border_line, sums_of,
+         SHAPE((count, cells * nodes), BF16)),
+        (inner_0, picked, shift_inner, hot, wide, cells_here), 8 * extent * rim * cells * nodes,
         scratch=[pltpu.VMEM((4 * rim, cells * nodes), BF16)],
     )
     inners, zones = [inner_0, inner_1], [zone_0]
@@ -441,19 +453,22 @@
         )
         zones.append(zone_k)
         got = exchange(*gave, n_state, n_space)
-        ins = (zone_k, inners[-1], inners[-2], shift_inner, border)
-        outs = (inner, sums_of)
-        if k == DEGREE - 2:
-            outs += (SHAPE((count, inside), F32),)
+        ins = (zone_k, inners[-1], inners[-2], shift_inner)
         if k == 1:
-            square, diagonal, inner_k, partial, *opened = call(
-                square_body, (SHAPE((inside, inside), BF16), line, *outs), (*ins, hot, wide),
-                2 * inside * inside * cells * nodes,
+            inner_k, partial, columns, begun, begun_diagonal = call(
+                second_inner_body,
+                (inner, sums_of, SHAPE((inside, 4 * rim), BF16), SHAPE((2 * rim, inside), BF16), line),
+                (*ins, picked, hot, wide_inner), 4 * extent * rim * cells * nodes,
+                scratch=[pltpu.VMEM((4 * rim, cells * nodes), BF16)],
             )
-        elif k < DEGREE - 1:
-            inner_k, partial, *opened = call(inner_body, outs, (*ins, square, diagonal), work)
+        elif k == 2:
+            square, diagonal, inner_k, partial, opened = call(
+                third_inner_body,
+                (SHAPE((inside, inside), BF16), line, inner, sums_of, SHAPE((count, inside), F32)),
+                (*ins, columns, begun, begun_diagonal, hot, wide_inner), 4 * extent * rim * cells * nodes,
+            )
         else:
-            inner_k = call(last_inner_body, inner, (zone_k, *opened, inners[-2], border), work // 4)
+            inner_k = call(last_inner_body, inner, (zone_k, opened, inners[-2], columns), work // 4)
         inners.append(inner_k)
     square_of_four = four(n_state, n_space)
     distances = (1, 2) if square_of_four else range(1, n_state)
@@ -464,7 +479,7 @@
     zone_blocks = [zone_k] + [across(zone_k, "state", d) for d in distances]
     energy, energy_zone, filtered = call(
         energy_body, (inner, zone, SHAPE((count, owned), BF16)),
-        (zone_k, inner_k, shift_inner, shift_zone, border, border_diagonal, square, diagonal), work,
+        (zone_k, inner_k, shift_inner, shift_zone, border, border_diagonal, columns, square, diagonal), work,
     )
     extra, scratch = (), []
     pair_of = SHAPE((count, count), F32)
@@ -472,24 +487,24 @@
     if square_of_four:
         part_x, found, *other = call(
             neighbour_body, (sums_of, found_of, pair_of, pair_of, zone),
-            (*inner_blocks, energy, shift_inner, border, square, diagonal), work // 2,
+            (*inner_blocks, energy, shift_inner, columns, square, diagonal), work // 2,
         )
         extra = (part_x, *other, shift_zone, border, border_diagonal)
         scratch = [pltpu.VMEM((count, 4 * rim), BF16)]
     else:
         found = call(gram_body, found_of, (*inner_blocks, energy), work)
-    columns = count * n_state // n_space
+    share = count * n_state // n_space
     chips = n_space // 2
     mine, give_half = call(
         functools.partial(project_body, square_of_four, 1.0 / (owned * n_space)),
-        (SHAPE((chips, 2, 2 * columns, count), BF16), SHAPE((chips, 2 * columns, count), BF16)),
+        (SHAPE((chips, 2, 2 * share, count), BF16), SHAPE((chips, 2 * share, count), BF16)),
         (energy_zone, found, *extra, *zone_blocks), work // 4, scratch=scratch,
     )
     got_half = swap(give_half, n_state, n_space, 0)
-    piece = SHAPE((2 * columns, count), BF16)
+    piece = SHAPE((2 * share, count), BF16)
     pieces = call(halve_body, (piece,) * chips, (mine, got_half), 0)
     shares = [share_out(p, d, n_state, n_space, square_of_four) for d, p in enumerate(pieces) if d or square_of_four]
-    turned = SHAPE((columns, count), F32)
+    turned = SHAPE((share, count), F32)
     intersection, projected = call(
         functools.partial(final_body, square_of_four), (turned, turned), (pieces[0], *shares), 0
     )

time: 46.7 us -> 46 us (0.985)
  waiting for transfers between devices: 10.5 us -> 8.98 us
  Pallas kernels: 15 us -> 15.9 us
    ppermute x11, waiting for transfers between devices: 6.64 us -> 5 us  [swap(): return lax.ppermute(block, ('state', 'space'), route)]
    pallas_call x16, Pallas kernels: 15 us -> 15.9 us  [call(): pl.pallas_call(body, out_shape=outs, in_specs=where, out_specs=jax.tree.m...]
  transfers between devices with their start and end apart: 19 -> 19, of which waited for: 10 -> 8; matrix products, arithmetic and copies ran while one was open for 0% -> 0% of each run, Pallas kernels for 24% -> 27%
where the time goes in v4:
time: 46 us; the launch traced here: 45.8 us
  starting transfers between devices  20.2 us (44%)
  Pallas kernels  15.9 us (35%)
  waiting for transfers between devices  8.98 us (20%)
  between operations  0.79 us (2%)
    pallas_call x16, Pallas kernels, call(): pl.pallas_call(body, out_shape=outs, in_specs=where, out_specs=jax.tree.m...  15.9 us
    ppermute x11, starting transfers between devices, swap(): return lax.ppermute(block, ('state', 'space'), route)  8.98 us
    ppermute x4, starting transfers between devices, share_out(): return lax.ppermute(block, ('state', 'space'), route)  5.91 us
    ppermute x4, starting transfers between devices, across(): lax.ppermute(block, axis, [(i, i ^ distance) for i in range(lax.axis_size...  5.27 us
    ppermute x11, waiting for transfers between devices, swap(): return lax.ppermute(block, ('state', 'space'), route)  5 us
    ppermute x4, waiting for transfers between devices, share_out(): return lax.ppermute(block, ('state', 'space'), route)  3.11 us
  transfers between devices with their start and end apart: 19, of which 8 were waited for; matrix products, arithmetic and copies ran while one was open for 0% of the time, Pallas kernels for 27%

profile of v4, /device:TPU:0, one launch (start us, length us, event | category | flops | bytes accessed | tf_op | source)
XLA Modules:
  0.0 45.8 jit_solution(17501258189414356736)
XLA Ops:
  0.6 0.8 %shard_map.67 = (bf16[112,128]{1,0:T(8,128)(2,1)S(1)}, bf16[112,128]{1,0:T(8,128)(2,1)S(1)}, f32[1,1024]{1,0:T(1,128)S(1)}, s32[2,512]{1,0:T(2,128)S(1)}) custom-call(bf16[96,1024]{1,0:T(8,128)(2,1)} %states_ref.3, f32[1,1024]{1,0:T(1,128)} %bitcast.3, s32[2,512]{1,0:T(2,128)} %index_ref.1), custom_call_target="tpu_custom_call" | custom-call | bytes 4194304 | tf_op jit(solution)/shard_map/pallas_call | solution.py:26
  2.0 2.6 %collective-permute-start.1 = (bf16[112,128]{1,0:T(8,128)(2,1)S(1)}, bf16[112,128]{1,0:T(8,128)(2,1)S(1)}, u32[]{:S(2)}, u32[]{:S(2)}) collective-permute-start(bf16[112,128]{1,0:T(8,128)(2,1)S(1)} %get-tuple-element.66), channel_id=1, source_target_pairs={{0,8},{1,2},{2,1},{3,4},{4,3},{5,6},{6,5},{7,15},{8,0},{9,10},{10,... | collective-permute-start | bytes 86024 | tf_op jit(solution)/shard_map/ppermute | solution.py:378
  4.6 2.2 %shard_map.68 = (bf16[1280,1024]{1,0:T(8,128)(2,1)S(1)}, bf16[512,1024]{1,0:T(8,128)(2,1)S(1)}, bf16[96,1024]{1,0:T(8,128)(2,1)S(1)}, bf16[96,1024]{1,0:T(8,128)(2,1)S(1)}, bf16[2,512,512]{2,1,0:T(8,128)(2,1)S(1)}) custom-call(s32[2,512]{1,0:T(2,128)S(1)} %get-tuple-element.63.index_ref, bf16[96,1024]{1,0:T(8,128)(2,1)} %states_ref.3, ...), custom_call_target="tpu_custom_call" | custom-call | flops 314572800 | bytes 4194304 | tf_op jit(solution)/shard_map/pallas_call | solution.py:26
  7.7 1.6 %collective-permute-start.3 = (bf16[96,256]{1,0:T(8,128)(2,1)S(1)}, bf16[96,256]{1,0:T(8,128)(2,1)S(1)}, u32[]{:S(2)}, u32[]{:S(2)}) collective-permute-start(bf16[96,256]{1,0:T(8,128)(2,1)S(1)} %get-tuple-element.73), channel_id=1, source_target_pairs={{0,8},{1,2},{2,1},{3,4},{4,3},{5,6},{6,5},{7,15},{8,0},{9,10},{10,... | collective-permute-start | bytes 147464 | tf_op jit(solution)/shard_map/ppermute | solution.py:378
  9.2 2.6 %shard_map.70 = (bf16[96,768]{1,0:T(8,128)(2,1)S(1)}, bf16[768,1024]{1,0:T(8,128)(2,1)S(1)}, bf16[512,512]{1,0:T(8,128)(2,1)S(1)}, f32[1,512]{1,0:T(1,128)S(1)},...) custom-call(bf16[96,768]{1,0:T(8,128)(2,1)S(1)} %get-tuple-element.76.inner_ref.old_ref, ...), custom_call_target="tpu_custom_call" | custom-call | flops 1342177280 | bytes 4194304 | tf_op jit(solution)/shard_map/pallas_call | solution.py:26
  12.3 1.5 %collective-permute-start.5 = (bf16[96,256]{1,0:T(8,128)(2,1)S(1)}, bf16[96,256]{1,0:T(8,128)(2,1)S(1)}, u32[]{:S(2)}, u32[]{:S(2)}) collective-permute-start(bf16[96,256]{1,0:T(8,128)(2,1)S(1)} %get-tuple-element.85), channel_id=1, source_target_pairs={{0,8},{1,2},{2,1},{3,4},{4,3},{5,6},{6,5},{7,15},{8,0},{9,10},{10,... | collective-permute-start | bytes 147464 | tf_op jit(solution)/shard_map/ppermute | solution.py:378
  13.8 2.7 %shard_map.72 = (bf16[96,768]{1,0:T(8,128)(2,1)S(1)}, f32[96,512]{1,0:T(8,128)S(1)}, bf16[768,512]{1,0:T(8,128)(2,1)S(1)}, bf16[256,768]{1,0:T(8,128)(2,1)S(1)}, f32[1,768]{1,0:T(1,128)S(1)}) custom-call(bf16[96,512]{1,0:T(8,128)(2,1)S(1)} %get-tuple-element.86.zone_ref.mid_ref.rest_0_, bf16[96,768]{1,0:T(8,128)(2,1)S(1)} %get-tuple-element.87.inner_ref.old_ref, ...), custom_call_target="tpu_custom_call" | custom-call | flops 671088640 | bytes 4194304 | tf_op jit(solution)/shard_map/pallas_call | solution.py:26
  17.0 1.5 %collective-permute-start.7 = (bf16[96,256]{1,0:T(8,128)(2,1)S(1)}, bf16[96,256]{1,0:T(8,128)(2,1)S(1)}, u32[]{:S(2)}, u32[]{:S(2)}) collective-permute-start(bf16[96,256]{1,0:T(8,128)(2,1)S(1)} %get-tuple-element.93), channel_id=1, source_target_pairs={{0,8},{1,2},{2,1},{3,4},{4,3},{5,6},{6,5},{7,15},{8,0},{9,10},{10,... | collective-permute-start | bytes 147464 | tf_op jit(solution)/shard_map/ppermute | solution.py:378
  18.5 2.5 %shard_map.74 = (bf16[768,768]{1,0:T(8,128)(2,1)S(1)}, f32[1,768]{1,0:T(1,128)S(1)}, bf16[96,768]{1,0:T(8,128)(2,1)}, f32[96,512]{1,0:T(8,128)S(1)}, f32[96,768]{1,0:T(8,128)S(1)}) custom-call(bf16[96,512]{1,0:T(8,128)(2,1)S(1)} %get-tuple-element.94.zone_ref.mid_ref.old_ref, bf16[96,768]{1,0:T(8,128)(2,1)S(1)} %get-tuple-element.95.inner_ref.old_ref, ...), custom_call_target="tpu_custom_call" | custom-call | flops 671088640 | bytes 4194304 | tf_op jit(solution)/shard_map/pallas_call | solution.py:26
  21.7 1.6 %collective-permute-start.10 = (bf16[96,768]{1,0:T(8,128)(2,1)S(1)}, bf16[96,768]{1,0:T(8,128)(2,1)S(1)}, u32[]{:S(2)}, u32[]{:S(2)}) collective-permute-start(bf16[96,768]{1,0:T(8,128)(2,1)S(1)} %shard_map.77.inner_ref), channel_id=1, source_target_pairs={{0,8},{8,0},{16,24},{24,16},{1,9},{9,1},{17,25},{25,17},{2,10},{10... | collective-permute-start | bytes 442376 | tf_op jit(solution)/shard_map/ppermute | solution.py:388
  23.2 1.5 %collective-permute-start.11 = (bf16[96,768]{1,0:T(8,128)(2,1)S(1)}, bf16[96,768]{1,0:T(8,128)(2,1)S(1)}, u32[]{:S(2)}, u32[]{:S(2)}) collective-permute-start(bf16[96,768]{1,0:T(8,128)(2,1)S(1)} %shard_map.77.inner_ref), channel_id=1, source_target_pairs={{0,16},{8,24},{16,0},{24,8},{1,17},{9,25},{17,1},{25,9},{2,18},{10... | collective-permute-start | bytes 442376 | tf_op jit(solution)/shard_map/ppermute | solution.py:388
  25.3 0.7 %collective-permute-done.8.got_a_ref = bf16[96,256]{1,0:T(8,128)(2,1)S(1)} collective-permute-done((bf16[96,256]{1,0:T(8,128)(2,1)S(1)}, bf16[96,256]{1,0:T(8,128)(2,1)S(1)}, u32[]{:S(2)}, u32[]{:S(2)}) %collective-permute-start.8) | collective-permute-done | bytes 49184 | tf_op jit(solution)/shard_map/ppermute | solution.py:378
  26.0 2.9 %collective-permute-done.9.got_b_ref = bf16[96,256]{1,0:T(8,128)(2,1)S(1)} collective-permute-done((bf16[96,256]{1,0:T(8,128)(2,1)S(1)}, bf16[96,256]{1,0:T(8,128)(2,1)S(1)}, u32[]{:S(2)}, u32[]{:S(2)}) %collective-permute-start.9) | collective-permute-done | bytes 49184 | tf_op jit(solution)/shard_map/ppermute | solution.py:378
  28.9 0.7 %collective-permute-start.12 = (bf16[96,512]{1,0:T(8,128)(2,1)S(1)}, bf16[96,512]{1,0:T(8,128)(2,1)S(1)}, u32[]{:S(2)}, u32[]{:S(2)}) collective-permute-start(bf16[96,512]{1,0:T(8,128)(2,1)S(1)} %shard_map.76.zone_ref.refs_7_), channel_id=1, source_target_pairs={{0,8},{8,0},{16,24},{24,16},{1,9},{9,1},{17,25},{25,17},{2,10},{10... | collective-permute-start | bytes 294920 | tf_op jit(solution)/shard_map/ppermute | solution.py:388
  29.6 1.5 %collective-permute-start.13 = (bf16[96,512]{1,0:T(8,128)(2,1)S(1)}, bf16[96,512]{1,0:T(8,128)(2,1)S(1)}, u32[]{:S(2)}, u32[]{:S(2)}) collective-permute-start(bf16[96,512]{1,0:T(8,128)(2,1)S(1)} %shard_map.76.zone_ref.refs_7_), channel_id=1, source_target_pairs={{0,16},{8,24},{16,0},{24,8},{1,17},{9,25},{17,1},{25,9},{2,18},{10... | collective-permute-start | bytes 294920 | tf_op jit(solution)/shard_map/ppermute | solution.py:388
  31.1 1.3 %shard_map.78 = (bf16[96,768]{1,0:T(8,128)(2,1)S(1)}, bf16[96,512]{1,0:T(8,128)(2,1)S(1)}, bf16[96,1024]{1,0:T(8,128)(2,1)}) custom-call(bf16[96,512]{1,0:T(8,128)(2,1)S(1)} %shard_map.76.zone_ref.refs_7_, bf16[96,768]{1,0:T(8,128)(2,1)S(1)} %shard_map.77.inner_ref, f32[1,768]{1,0:T(1,128)S(1)} %get-tuple-element.78.shift_inner_ref, ...), custom_call_target="tpu_custom_call" | custom-call | flops 314572800 | bytes 4194304 | tf_op jit(solution)/shard_map/pallas_call | solution.py:26
  32.5 0.9 %shard_map.79 = (f32[96,512]{1,0:T(8,128)S(1)}, f32[288,192]{1,0:T(8,128)S(1)}, f32[96,96]{1,0:T(8,128)S(1)}, f32[96,96]{1,0:T(8,128)S(1)}, bf16[96,512]{1,0:T(8,128)(2,1)S(1)}) custom-call(bf16[96,768]{1,0:T(8,128)(2,1)S(1)} %shard_map.77.inner_ref, bf16[96,768]{1,0:T(8,128)(2,1)S(1)} %collective-permute-done.10.beside_ref, ...), custom_call_target="tpu_custom_call" | custom-call | flops 157286400 | bytes 4194304 | tf_op jit(solution)/shard_map/pallas_call | solution.py:26
  34.8 1.3 %collective-permute-done.14.got_ref = bf16[4,96,96]{2,1,0:T(8,128)(2,1)S(1)} collective-permute-done((bf16[4,96,96]{2,1,0:T(8,128)(2,1)S(1)}, bf16[4,96,96]{2,1,0:T(8,128)(2,1)S(1)}, u32[]{:S(2)}, u32[]{:S(2)}) %collective-permute-start.14) | collective-permute-done | bytes 73760 | tf_op jit(solution)/shard_map/ppermute | solution.py:378
  36.2 1.3 %collective-permute-start.15 = (bf16[96,96]{1,0:T(8,128)(2,1)S(1)}, bf16[96,96]{1,0:T(8,128)(2,1)S(1)}, u32[]{:S(2)}, u32[]{:S(2)}) collective-permute-start(bf16[96,96]{1,0:T(8,128)(2,1)S(1)} %get-tuple-element.117.mine_ref), channel_id=1, source_target_pairs={{0,10},{1,11},{2,8},{3,9},{4,14},{5,15},{6,12},{7,13},{8,2},{9,3},... | collective-permute-start | bytes 55304 | tf_op jit(solution)/shard_map/ppermute | solution.py:399
  37.5 1.6 %collective-permute-start.16 = (bf16[96,96]{1,0:T(8,128)(2,1)S(1)}, bf16[96,96]{1,0:T(8,128)(2,1)S(1)}, u32[]{:S(2)}, u32[]{:S(2)}) collective-permute-start(bf16[96,96]{1,0:T(8,128)(2,1)S(1)} %get-tuple-element.118), channel_id=1, source_target_pairs={{0,2},{1,3},{2,0},{3,1},{4,12},{5,13},{6,4},{7,5},{8,10},{9,11},{1... | collective-permute-start | bytes 55304 | tf_op jit(solution)/shard_map/ppermute | solution.py:399
  39.6 2.5 %collective-permute-start.18 = (bf16[96,96]{1,0:T(8,128)(2,1)S(1)}, bf16[96,96]{1,0:T(8,128)(2,1)S(1)}, u32[]{:S(2)}, u32[]{:S(2)}) collective-permute-start(bf16[96,96]{1,0:T(8,128)(2,1)S(1)} %get-tuple-element.120), channel_id=1, source_target_pairs={{0,12},{1,13},{2,4},{3,5},{4,2},{5,3},{6,0},{7,1},{8,14},{9,15},{1... | collective-permute-start | bytes 55304 | tf_op jit(solution)/shard_map/ppermute | solution.py:399
  42.1 2.0 %collective-permute-done.17.refs_2_ = bf16[96,96]{1,0:T(8,128)(2,1)S(1)} collective-permute-done((bf16[96,96]{1,0:T(8,128)(2,1)S(1)}, bf16[96,96]{1,0:T(8,128)(2,1)S(1)}, u32[]{:S(2)}, u32[]{:S(2)}) %collective-permute-start.17) | collective-permute-done | bytes 18464 | tf_op jit(solution)/shard_map/ppermute | solution.py:399
  44.1 1.1 %collective-permute-done.18.refs_3_ = bf16[96,96]{1,0:T(8,128)(2,1)S(1)} collective-permute-done((bf16[96,96]{1,0:T(8,128)(2,1)S(1)}, bf16[96,96]{1,0:T(8,128)(2,1)S(1)}, u32[]{:S(2)}, u32[]{:S(2)}) %collective-permute-start.18) | collective-permute-done | bytes 18464 | tf_op jit(solution)/shard_map/ppermute | solution.py:399
  45.2 0.6 %shard_map.82 = (f32[48,96]{1,0:T(8,128)}, f32[48,96]{1,0:T(8,128)}) custom-call(bf16[96,96]{1,0:T(8,128)(2,1)S(1)} %get-tuple-element.117.mine_ref, bf16[96,96]{1,0:T(8,128)(2,1)S(1)} %collective-permute-done.15.refs_0_, bf16[96,96]{1,0:T(8,128)(2,1)S(1)} %collective-permute-done.16.refs_1_, bf16[96,96]{1,0:T(8,128)(2,1)S(1)} %collective-permute-done.17.refs_2_, ...), custom_call_target="tpu_custom_call" | custom-call | bytes 4194304 | tf_op jit(solution)/shard_map/pallas_call | solution.py:26
  (30 shorter events, 5.7 us)
Async XLA Ops:
  1.5 5.3 %collective-permute-start = (bf16[112,128]{1,0:T(8,128)(2,1)S(1)}, bf16[112,128]{1,0:T(8,128)(2,1)S(1)}, u32[]{:S(2)}, u32[]{:S(2)}) collective-permute-start(bf16[112,128]{1,0:T(8,128)(2,1)S(1)} %get-tuple-element.65), channel_id=1, source_target_pairs={{0,1},{1,0},{2,3},{3,2},{4,5},{5,4},{6,7},{7,6},{8,9},{9,8},{10,11... | collective-permute-start | bytes 86024 | tf_op jit(solution)/shard_map/ppermute | solution.py:378
  2.0 4.7 %collective-permute-start.1 = (bf16[112,128]{1,0:T(8,128)(2,1)S(1)}, bf16[112,128]{1,0:T(8,128)(2,1)S(1)}, u32[]{:S(2)}, u32[]{:S(2)}) collective-permute-start(bf16[112,128]{1,0:T(8,128)(2,1)S(1)} %get-tuple-element.66), channel_id=1, source_target_pairs={{0,8},{1,2},{2,1},{3,4},{4,3},{5,6},{6,5},{7,15},{8,0},{9,10},{10,... | collective-permute-start | bytes 86024 | tf_op jit(solution)/shard_map/ppermute | solution.py:378
  7.4 4.5 %collective-permute-start.2 = (bf16[96,256]{1,0:T(8,128)(2,1)S(1)}, bf16[96,256]{1,0:T(8,128)(2,1)S(1)}, u32[]{:S(2)}, u32[]{:S(2)}) collective-permute-start(bf16[96,256]{1,0:T(8,128)(2,1)S(1)} %get-tuple-element.72), channel_id=1, source_target_pairs={{0,1},{1,0},{2,3},{3,2},{4,5},{5,4},{6,7},{7,6},{8,9},{9,8},{10,11... | collective-permute-start | bytes 147464 | tf_op jit(solution)/shard_map/ppermute | solution.py:378
  7.7 4.2 %collective-permute-start.3 = (bf16[96,256]{1,0:T(8,128)(2,1)S(1)}, bf16[96,256]{1,0:T(8,128)(2,1)S(1)}, u32[]{:S(2)}, u32[]{:S(2)}) collective-permute-start(bf16[96,256]{1,0:T(8,128)(2,1)S(1)} %get-tuple-element.73), channel_id=1, source_target_pairs={{0,8},{1,2},{2,1},{3,4},{4,3},{5,6},{6,5},{7,15},{8,0},{9,10},{10,... | collective-permute-start | bytes 147464 | tf_op jit(solution)/shard_map/ppermute | solution.py:378
  12.1 4.3 %collective-permute-start.4 = (bf16[96,256]{1,0:T(8,128)(2,1)S(1)}, bf16[96,256]{1,0:T(8,128)(2,1)S(1)}, u32[]{:S(2)}, u32[]{:S(2)}) collective-permute-start(bf16[96,256]{1,0:T(8,128)(2,1)S(1)} %get-tuple-element.84), channel_id=1, source_target_pairs={{0,1},{1,0},{2,3},{3,2},{4,5},{5,4},{6,7},{7,6},{8,9},{9,8},{10,11... | collective-permute-start | bytes 147464 | tf_op jit(solution)/shard_map/ppermute | solution.py:378
  12.3 4.2 %collective-permute-start.5 = (bf16[96,256]{1,0:T(8,128)(2,1)S(1)}, bf16[96,256]{1,0:T(8,128)(2,1)S(1)}, u32[]{:S(2)}, u32[]{:S(2)}) collective-permute-start(bf16[96,256]{1,0:T(8,128)(2,1)S(1)} %get-tuple-element.85), channel_id=1, source_target_pairs={{0,8},{1,2},{2,1},{3,4},{4,3},{5,6},{6,5},{7,15},{8,0},{9,10},{10,... | collective-permute-start | bytes 147464 | tf_op jit(solution)/shard_map/ppermute | solution.py:378
  16.7 4.2 %collective-permute-start.6 = (bf16[96,256]{1,0:T(8,128)(2,1)S(1)}, bf16[96,256]{1,0:T(8,128)(2,1)S(1)}, u32[]{:S(2)}, u32[]{:S(2)}) collective-permute-start(bf16[96,256]{1,0:T(8,128)(2,1)S(1)} %get-tuple-element.92), channel_id=1, source_target_pairs={{0,1},{1,0},{2,3},{3,2},{4,5},{5,4},{6,7},{7,6},{8,9},{9,8},{10,11... | collective-permute-start | bytes 147464 | tf_op jit(solution)/shard_map/ppermute | solution.py:378
  17.0 4.1 %collective-permute-start.7 = (bf16[96,256]{1,0:T(8,128)(2,1)S(1)}, bf16[96,256]{1,0:T(8,128)(2,1)S(1)}, u32[]{:S(2)}, u32[]{:S(2)}) collective-permute-start(bf16[96,256]{1,0:T(8,128)(2,1)S(1)} %get-tuple-element.93), channel_id=1, source_target_pairs={{0,8},{1,2},{2,1},{3,4},{4,3},{5,6},{6,5},{7,15},{8,0},{9,10},{10,... | collective-permute-start | bytes 147464 | tf_op jit(solution)/shard_map/ppermute | solution.py:378
  21.7 10.8 %collective-permute-start.10 = (bf16[96,768]{1,0:T(8,128)(2,1)S(1)}, bf16[96,768]{1,0:T(8,128)(2,1)S(1)}, u32[]{:S(2)}, u32[]{:S(2)}) collective-permute-start(bf16[96,768]{1,0:T(8,128)(2,1)S(1)} %shard_map.77.inner_ref), channel_id=1, source_target_pairs={{0,8},{8,0},{16,24},{24,16},{1,9},{9,1},{17,25},{25,17},{2,10},{10... | collective-permute-start | bytes 442376 | tf_op jit(solution)/shard_map/ppermute | solution.py:388
  23.2 9.2 %collective-permute-start.11 = (bf16[96,768]{1,0:T(8,128)(2,1)S(1)}, bf16[96,768]{1,0:T(8,128)(2,1)S(1)}, u32[]{:S(2)}, u32[]{:S(2)}) collective-permute-start(bf16[96,768]{1,0:T(8,128)(2,1)S(1)} %shard_map.77.inner_ref), channel_id=1, source_target_pairs={{0,16},{8,24},{16,0},{24,8},{1,17},{9,25},{17,1},{25,9},{2,18},{10... | collective-permute-start | bytes 442376 | tf_op jit(solution)/shard_map/ppermute | solution.py:388
  24.8 1.2 %collective-permute-start.8 = (bf16[96,256]{1,0:T(8,128)(2,1)S(1)}, bf16[96,256]{1,0:T(8,128)(2,1)S(1)}, u32[]{:S(2)}, u32[]{:S(2)}) collective-permute-start(bf16[96,256]{1,0:T(8,128)(2,1)S(1)} %get-tuple-element.101), channel_id=1, source_target_pairs={{0,1},{1,0},{2,3},{3,2},{4,5},{5,4},{6,7},{7,6},{8,9},{9,8},{10,11... | collective-permute-start | bytes 147464 | tf_op jit(solution)/shard_map/ppermute | solution.py:378
  24.8 4.1 %collective-permute-start.9 = (bf16[96,256]{1,0:T(8,128)(2,1)S(1)}, bf16[96,256]{1,0:T(8,128)(2,1)S(1)}, u32[]{:S(2)}, u32[]{:S(2)}) collective-permute-start(bf16[96,256]{1,0:T(8,128)(2,1)S(1)} %get-tuple-element.102), channel_id=1, source_target_pairs={{0,8},{1,2},{2,1},{3,4},{4,3},{5,6},{6,5},{7,15},{8,0},{9,10},{10,... | collective-permute-start | bytes 147464 | tf_op jit(solution)/shard_map/ppermute | solution.py:378
  28.9 4.9 %collective-permute-start.12 = (bf16[96,512]{1,0:T(8,128)(2,1)S(1)}, bf16[96,512]{1,0:T(8,128)(2,1)S(1)}, u32[]{:S(2)}, u32[]{:S(2)}) collective-permute-start(bf16[96,512]{1,0:T(8,128)(2,1)S(1)} %shard_map.76.zone_ref.refs_7_), channel_id=1, source_target_pairs={{0,8},{8,0},{16,24},{24,16},{1,9},{9,1},{17,25},{25,17},{2,10},{10... | collective-permute-start | bytes 294920 | tf_op jit(solution)/shard_map/ppermute | solution.py:388
  29.6 4.6 %collective-permute-start.13 = (bf16[96,512]{1,0:T(8,128)(2,1)S(1)}, bf16[96,512]{1,0:T(8,128)(2,1)S(1)}, u32[]{:S(2)}, u32[]{:S(2)}) collective-permute-start(bf16[96,512]{1,0:T(8,128)(2,1)S(1)} %shard_map.76.zone_ref.refs_7_), channel_id=1, source_target_pairs={{0,16},{8,24},{16,0},{24,8},{1,17},{9,25},{17,1},{25,9},{2,18},{10... | collective-permute-start | bytes 294920 | tf_op jit(solution)/shard_map/ppermute | solution.py:388
  34.8 1.4 %collective-permute-start.14 = (bf16[4,96,96]{2,1,0:T(8,128)(2,1)S(1)}, bf16[4,96,96]{2,1,0:T(8,128)(2,1)S(1)}, u32[]{:S(2)}, u32[]{:S(2)}) collective-permute-start(bf16[4,96,96]{2,1,0:T(8,128)(2,1)S(1)} %get-tuple-element.116), channel_id=1, source_target_pairs={{0,1},{1,0},{2,3},{3,2},{4,5},{5,4},{6,7},{7,6},{8,9},{9,8},{10,11... | collective-permute-start | bytes 221192 | tf_op jit(solution)/shard_map/ppermute | solution.py:378
  36.2 5.9 %collective-permute-start.15 = (bf16[96,96]{1,0:T(8,128)(2,1)S(1)}, bf16[96,96]{1,0:T(8,128)(2,1)S(1)}, u32[]{:S(2)}, u32[]{:S(2)}) collective-permute-start(bf16[96,96]{1,0:T(8,128)(2,1)S(1)} %get-tuple-element.117.mine_ref), channel_id=1, source_target_pairs={{0,10},{1,11},{2,8},{3,9},{4,14},{5,15},{6,12},{7,13},{8,2},{9,3},... | collective-permute-start | bytes 55304 | tf_op jit(solution)/shard_map/ppermute | solution.py:399
  37.5 4.6 %collective-permute-start.16 = (bf16[96,96]{1,0:T(8,128)(2,1)S(1)}, bf16[96,96]{1,0:T(8,128)(2,1)S(1)}, u32[]{:S(2)}, u32[]{:S(2)}) collective-permute-start(bf16[96,96]{1,0:T(8,128)(2,1)S(1)} %get-tuple-element.118), channel_id=1, source_target_pairs={{0,2},{1,3},{2,0},{3,1},{4,12},{5,13},{6,4},{7,5},{8,10},{9,11},{1... | collective-permute-start | bytes 55304 | tf_op jit(solution)/shard_map/ppermute | solution.py:399
  39.1 5.0 %collective-permute-start.17 = (bf16[96,96]{1,0:T(8,128)(2,1)S(1)}, bf16[96,96]{1,0:T(8,128)(2,1)S(1)}, u32[]{:S(2)}, u32[]{:S(2)}) collective-permute-start(bf16[96,96]{1,0:T(8,128)(2,1)S(1)} %get-tuple-element.119), channel_id=1, source_target_pairs={{0,4},{1,5},{2,12},{3,13},{4,0},{5,1},{6,2},{7,3},{8,6},{9,7},{10,... | collective-permute-start | bytes 55304 | tf_op jit(solution)/shard_map/ppermute | solution.py:399
  39.6 5.6 %collective-permute-start.18 = (bf16[96,96]{1,0:T(8,128)(2,1)S(1)}, bf16[96,96]{1,0:T(8,128)(2,1)S(1)}, u32[]{:S(2)}, u32[]{:S(2)}) collective-permute-start(bf16[96,96]{1,0:T(8,128)(2,1)S(1)} %get-tuple-element.120), channel_id=1, source_target_pairs={{0,12},{1,13},{2,4},{3,5},{4,2},{5,3},{6,0},{7,1},{8,14},{9,15},{1... | collective-permute-start | bytes 55304 | tf_op jit(solution)/shard_map/ppermute | solution.py:399

commit v5 on v4

--- a/solution.py
+++ b/solution.py
@@ -90,7 +90,8 @@
         ).astype(BF16)
 
 
-def spread_body(index_ref, states_ref, cells_ref, hot_ref, wide_ref, picked_ref, here_ref, cells_out_ref, sem):
+def spread_body(index_ref, states_ref, cells_ref,
+                hot_ref, outer_ref, wide_ref, picked_ref, here_ref, cells_out_ref, sem):
     states_copy = pltpu.make_async_copy(states_ref, here_ref, sem.at[0])
     cells_copy = pltpu.make_async_copy(cells_ref, cells_out_ref, sem.at[1])
     states_copy.start()
@@ -104,6 +105,8 @@
         index = index_ref[c : c + 1, :] - offset
         hot = lax.broadcasted_iota(jnp.int32, (extent, nodes), 0) == index
         hot_ref[:, c * nodes : (c + 1) * nodes] = hot.astype(BF16)
+    outer_ref[:rim, :] = hot_ref[:rim, :]
+    outer_ref[rim:, :] = hot_ref[extent - rim :, :]
     states_copy.wait()
     picked_ref[...] = mm(here_ref[...], hot_ref[rim : extent - rim, :]).astype(BF16)
     cells_copy.wait()
@@ -113,11 +116,11 @@
         wide_ref[width:, here] = mm(hot_ref[extent - width :, here], cells_out_ref[c]).astype(BF16)
 
 
-def first_zone_body(states_ref, halo_a_ref, halo_b_ref, potential_ref, hot_ref, wide_ref, owned_ref,
+def first_zone_body(states_ref, halo_a_ref, halo_b_ref, potential_ref, outer_ref, wide_ref, owned_ref,
                     inner_ref, zone_ref, shift_inner_ref, shift_zone_ref, picked_ref, sums_ref, give_a_ref, give_b_ref):
     count, owned = states_ref.shape
     rim = halo_a_ref.shape[1]
-    width, extent = 2 * rim, owned + 2 * rim
+    width = 2 * rim
     low, high = sort_out(halo_a_ref[...], halo_b_ref[...])
     zone_ref[:, :rim] = low[:count].astype(BF16)
     zone_ref[:, rim:width] = states_ref[:, :rim]
@@ -133,8 +136,7 @@
         shift_zone_ref[:, at : at + rim] = (part[0:1] + part[1:2] + part[2:3]) - spectrum_center
     picked = (
         owned_ref[...].astype(F32)
-        + mm(zone_ref[:, :rim], hot_ref[:rim, :])
-        + mm(zone_ref[:, width + rim :], hot_ref[extent - rim :, :])
+        + mm(jnp.concatenate([zone_ref[:, :rim], zone_ref[:, width + rim :]], axis=1), outer_ref[...])
     ).astype(BF16)
     picked_ref[...] = picked
     sums = mm_nt(picked, wide_ref[...])
@@ -283,14 +285,19 @@
     filtered_ref[:, owned - rim :] = zone_ref[:, width : width + rim]
 
 
-def neighbour_body(inner_ref, beside_ref, across_ref, energy_ref, shift_inner_ref, columns_ref, square_ref, diagonal_ref,
+def by_core(first_ref, second_ref):
+    odd, first, second = is_odd(), first_ref[...], second_ref[...]
+    return jnp.where(odd, second, first), jnp.where(odd, first, second)
+
+
+def neighbour_body(inner_ref, first_ref, second_ref, energy_ref, shift_inner_ref, columns_ref, square_ref, diagonal_ref,
                    part_ref, found_ref, other_ref, other_energy_ref, toward_ref):
-    beside, across = beside_ref[...], across_ref[...]
+    beside, across = by_core(first_ref, second_ref)
     line = diagonal_ref[...] + (shift_inner_ref[...] + spectrum_center)
     energy = (mm(beside, square_ref[...]) + line * beside.astype(F32)).astype(BF16)
     part_ref[...] = mm(beside, columns_ref[...])
     toward_ref[...] = mm(across, columns_ref[...]).astype(BF16)
-    inner_found(found_ref, (inner_ref, beside_ref, across_ref), inner_ref, energy_ref)
+    inner_found(found_ref, (inner_ref[...], beside, across), inner_ref, energy_ref)
     other_ref[...] = mm_nt(across, beside)
     other_energy_ref[...] = mm_nt(across, energy)
 
@@ -299,13 +306,13 @@
     count = states_ref.shape[0]
     for place, block in enumerate(blocks):
         here = slice(place * count, (place + 1) * count)
-        found_ref[here, :count] = mm_nt(block[...], states_ref[...])
-        found_ref[here, count:] = mm_nt(block[...], energy_ref[...])
+        found_ref[here, :count] = mm_nt(block, states_ref[...])
+        found_ref[here, count:] = mm_nt(block, energy_ref[...])
 
 
 def gram_body(*refs):
     *blocks, energy_ref, found_ref = refs
-    inner_found(found_ref, blocks, blocks[0], energy_ref)
+    inner_found(found_ref, [block[...] for block in blocks], blocks[0], energy_ref)
 
 
 def zone_found(block_ref, zone_ref, energy_zone_ref):
@@ -317,7 +324,9 @@
 def project_body(square_of_four, scale, energy_zone_ref, found_ref, *refs):
     if square_of_four:
         (part_ref, other_ref, other_energy_ref, toward_ref, shift_zone_ref, border_ref, border_diagonal_ref), refs = refs[:7], refs[7:]
-        *zones, out_ref, give_ref, other_zone_ref = refs
+        *zones, out_ref, give_ref, other_zone_ref, beside_ref, across_ref = refs
+        beside_ref[...], across_ref[...] = by_core(zones[1], zones[2])
+        zones = [zones[0], beside_ref, across_ref]
     else:
         *zones, out_ref, give_ref = refs
     count = energy_zone_ref.shape[0]
@@ -331,7 +340,8 @@
             parts = [block[:columns], block[columns:]]
             for core in range(2):
                 out_ref[at, core, there] = parts[core].astype(BF16)
-            give_ref[at, there] = jnp.where(odd, parts[0], parts[1]).astype(BF16)
+            if not square_of_four:
+                give_ref[at, there] = jnp.where(odd, parts[0], parts[1]).astype(BF16)
 
     if square_of_four:
         zone_energy(zones[1], part_ref[...], shift_zone_ref, border_ref, border_diagonal_ref, other_zone_ref)
@@ -343,6 +353,38 @@
         states, energy = zone_found(zones[2], zones[1], other_zone_ref)
         energy = energy + mm_nt(toward_ref[...], zones[1][...])
         put(3, other_ref[...] + states, other_energy_ref[...] + energy)
+        for order, (even, uneven) in enumerate(CORE_WAYS):
+            give_ref[order] = out_ref[chip_at(jnp.where(odd, even, uneven))]
+
+
+CORE_WAYS = ((1, 3), (0, 2))
+
+
+def chip_at(distance):
+    return (lax.axis_index("space") >> 1) ^ distance
+
+
+def split_body(mine_ref, got_ref, *pieces):
+    odd = is_odd()
+    for order, (even, uneven) in enumerate(CORE_WAYS):
+        block = mine_ref[chip_at(jnp.where(odd, uneven, even))].astype(F32)
+        pieces[order][...] = (block + got_ref[order].astype(F32)).astype(BF16)
+
+
+def gather_body(mine_ref, first_ref, second_ref, keep_ref, give_ref):
+    odd = is_odd()
+    made_elsewhere = jnp.logical_or(odd, chip_at(0) == (lax.axis_index("state") ^ 3))
+    second = jnp.where(made_elsewhere, second_ref[...].astype(F32), mine_ref[...].astype(F32))
+    total = first_ref[...].astype(F32) + second
+    keep_ref[...] = jnp.where(odd, total[1], total[0])
+    give_ref[...] = jnp.where(odd, total[0], total[1]).astype(BF16)
+
+
+def join_body(keep_ref, got_ref, first_ref, second_ref):
+    total = keep_ref[...] + got_ref[...].astype(F32)
+    columns = first_ref.shape[0]
+    first_ref[...] = total[:columns]
+    second_ref[...] = total[columns:]
 
 
 def halve_body(mine_ref, got_ref, *pieces):
@@ -352,13 +394,9 @@
         piece_ref[...] = total.astype(BF16)
 
 
-def final_body(square_of_four, mine_ref, *refs):
+def final_body(mine_ref, *refs):
     parts, (first_ref, second_ref) = refs[:-2], refs[-2:]
     total = mine_ref[...].astype(F32)
-    if square_of_four:
-        made_elsewhere = (lax.axis_index("space") >> 1) == (lax.axis_index("state") ^ 3)
-        total = jnp.where(made_elsewhere, parts[0][...].astype(F32), total)
-        parts = parts[1:]
     for part in parts:
         total = total + part[...].astype(F32)
     columns = first_ref.shape[0]
@@ -388,12 +426,22 @@
     return lax.ppermute(block, axis, [(i, i ^ distance) for i in range(lax.axis_size(axis))])
 
 
-def share_out(block, distance, n_state, n_space, square_of_four):
+def beside(block, first, n_state, n_space):
     route = []
     for s in range(n_state):
         for i in range(n_space):
+            distance = 1 if first == (i & 1 == 0) else 2
+            route.append((s * n_space + i, (s ^ distance) * n_space + i))
+    return lax.ppermute(block, ("state", "space"), route)
+
+
+def share_out(block, order, n_state, n_space):
+    route = []
+    for s in range(n_state):
+        for i in range(n_space):
+            distance = CORE_WAYS[order][i & 1]
             to_group, to_chip = s, (i >> 1) ^ distance
-            if square_of_four and (distance == 0 or to_chip == s ^ 3):
+            if distance == 0 or to_chip == s ^ 3:
                 to_group, to_chip = s ^ 1, to_chip ^ 1
             route.append((s * n_space + i, to_group * n_space + 2 * to_chip + (i & 1)))
     return lax.ppermute(block, ("state", "space"), route)
@@ -422,17 +470,17 @@
     )
     got = exchange(*gave, n_state, n_space)
     table = SHAPE((extent, cells * nodes), BF16)
-    hot, wide, picked, states_here, cells_here = call(
+    hot, outer, wide, picked, states_here, cells_here = call(
         spread_body,
-        (table, SHAPE((4 * rim, cells * nodes), BF16), SHAPE((count, cells * nodes), BF16),
-         SHAPE(states_in.shape, BF16), SHAPE(cell_matrices.shape, BF16)),
+        (table, SHAPE((2 * rim, cells * nodes), BF16), SHAPE((4 * rim, cells * nodes), BF16),
+         SHAPE((count, cells * nodes), BF16), SHAPE(states_in.shape, BF16), SHAPE(cell_matrices.shape, BF16)),
         (local, states_in, cell_matrices), work, raw=(1, 2), scratch=[pltpu.SemaphoreType.DMA((2,))],
     )
     border_line, line = SHAPE((1, 4 * rim), F32), SHAPE((1, inside), F32)
     inner_0, zone_0, shift_inner, shift_zone, picked, sums, *gave = call(
         first_zone_body,
         (inner, zone, line, border_line, SHAPE((count, cells * nodes), BF16), sums_of, give, give),
-        (states_here, *got, row, hot, wide, picked), work,
+        (states_here, *got, row, outer, wide, picked), work,
     )
     got = exchange(*gave, n_state, n_space)
     inner_1, wide_inner, border, border_diagonal, partial, picked = call(
@@ -471,12 +519,17 @@
             inner_k = call(last_inner_body, inner, (zone_k, opened, inners[-2], columns), work // 4)
         inners.append(inner_k)
     square_of_four = four(n_state, n_space)
-    distances = (1, 2) if square_of_four else range(1, n_state)
-    inner_blocks = [inner_k] + [across(inner_k, "state", d) for d in distances]
+    if square_of_four:
+        inner_blocks = [inner_k] + [beside(inner_k, first, n_state, n_space) for first in (True, False)]
+    else:
+        inner_blocks = [inner_k] + [across(inner_k, "state", d) for d in range(1, n_state)]
     zone_k = call(
         last_zone_body, zone, (sums, *got, shift_zone, zones[-1], zones[-2]), 0
     )
-    zone_blocks = [zone_k] + [across(zone_k, "state", d) for d in distances]
+    if square_of_four:
+        zone_blocks = [zone_k] + [beside(zone_k, first, n_state, n_space) for first in (True, False)]
+    else:
+        zone_blocks = [zone_k] + [across(zone_k, "state", d) for d in range(1, n_state)]
     energy, energy_zone, filtered = call(
         energy_body, (inner, zone, SHAPE((count, owned), BF16)),
         (zone_k, inner_k, shift_inner, shift_zone, border, border_diagonal, columns, square, diagonal), work,
@@ -490,24 +543,33 @@
             (*inner_blocks, energy, shift_inner, columns, square, diagonal), work // 2,
         )
         extra = (part_x, *other, shift_zone, border, border_diagonal)
-        scratch = [pltpu.VMEM((count, 4 * rim), BF16)]
+        scratch = [pltpu.VMEM((count, 4 * rim), BF16)] * 3
     else:
         found = call(gram_body, found_of, (*inner_blocks, energy), work)
     share = count * n_state // n_space
     chips = n_space // 2
+    turned = SHAPE((share, count), F32)
+    piece = SHAPE((2 * share, count), BF16)
+    both_halves = SHAPE((2, 2 * share, count), BF16)
     mine, give_half = call(
         functools.partial(project_body, square_of_four, 1.0 / (owned * n_space)),
-        (SHAPE((chips, 2, 2 * share, count), BF16), SHAPE((chips, 2 * share, count), BF16)),
+        (SHAPE((chips, 2, 2 * share, count), BF16),
+         SHAPE((2, 2, 2 * share, count) if square_of_four else (chips, 2 * share, count), BF16)),
         (energy_zone, found, *extra, *zone_blocks), work // 4, scratch=scratch,
     )
     got_half = swap(give_half, n_state, n_space, 0)
-    piece = SHAPE((2 * share, count), BF16)
-    pieces = call(halve_body, (piece,) * chips, (mine, got_half), 0)
-    shares = [share_out(p, d, n_state, n_space, square_of_four) for d, p in enumerate(pieces) if d or square_of_four]
-    turned = SHAPE((share, count), F32)
-    intersection, projected = call(
-        functools.partial(final_body, square_of_four), (turned, turned), (pieces[0], *shares), 0
-    )
+    if square_of_four:
+        pieces = call(split_body, (both_halves,) * 2, (mine, got_half), 0)
+        shares = [share_out(p, order, n_state, n_space) for order, p in enumerate(pieces)]
+        keep, give_last = call(
+            gather_body, (SHAPE(piece.shape, F32), piece), (pieces[1], *shares), 0
+        )
+        got_last = swap(give_last, n_state, n_space, 0)
+        intersection, projected = call(join_body, (turned, turned), (keep, got_last), 0)
+    else:
+        pieces = call(halve_body, (piece,) * chips, (mine, got_half), 0)
+        shares = [across(p, "space", 2 * d) for d, p in enumerate(pieces) if d]
+        intersection, projected = call(final_body, (turned, turned), (pieces[0], *shares), 0)
     return filtered, intersection.T, projected.T
 
 

time: 46 us -> 45.2 us (0.983)
  starting transfers between devices: 20.2 us -> 16.4 us
  waiting for transfers between devices: 8.98 us -> 11.6 us
    ppermute x4 -> x2, starting transfers between devices: 5.91 us -> 2.04 us  [share_out(): return lax.ppermute(block, ('state', 'space'), route)]
    ppermute x11 -> x12, waiting for transfers between devices: 5 us -> 6.34 us  [swap(): return lax.ppermute(block, ('state', 'space'), route)]
    ppermute x4, waiting for transfers between devices: 0.86 us -> 1.66 us  [beside(): return lax.ppermute(block, ('state', 'space'), route)]
    ppermute x4 -> x2, waiting for transfers between devices: 3.11 us -> 3.64 us  [share_out(): return lax.ppermute(block, ('state', 'space'), route)]
    pallas_call x16 -> x17, Pallas kernels: 15.9 us -> 16.1 us  [call(): pl.pallas_call(body, out_shape=outs, in_specs=where, out_specs=jax.tree.m...]
    ppermute x11 -> x12, starting transfers between devices: 8.98 us -> 9.06 us  [swap(): return lax.ppermute(block, ('state', 'space'), route)]
  transfers between devices with their start and end apart: 19 -> 18, of which waited for: 8 -> 9; matrix products, arithmetic and copies ran while one was open for 0% -> 0% of each run, Pallas kernels for 27% -> 28%
where the time goes in v5:
time: 45.2 us; the launch traced here: 45 us
  starting transfers between devices  16.4 us (36%)
  Pallas kernels  16.1 us (36%)
  waiting for transfers between devices  11.6 us (26%)
  between operations  0.8 us (2%)
    pallas_call x17, Pallas kernels, call(): pl.pallas_call(body, out_shape=outs, in_specs=where, out_specs=jax.tree.m...  16.1 us
    ppermute x12, starting transfers between devices, swap(): return lax.ppermute(block, ('state', 'space'), route)  9.06 us
    ppermute x12, waiting for transfers between devices, swap(): return lax.ppermute(block, ('state', 'space'), route)  6.34 us
    ppermute x4, starting transfers between devices, beside(): return lax.ppermute(block, ('state', 'space'), route)  5.33 us
    ppermute x2, waiting for transfers between devices, share_out(): return lax.ppermute(block, ('state', 'space'), route)  3.64 us
    ppermute x2, starting transfers between devices, share_out(): return lax.ppermute(block, ('state', 'space'), route)  2.04 us
    ppermute x4, waiting for transfers between devices, beside(): return lax.ppermute(block, ('state', 'space'), route)  1.66 us
  transfers between devices with their start and end apart: 18, of which 9 were waited for; matrix products, arithmetic and copies ran while one was open for 0% of the time, Pallas kernels for 28%

profile of v5, /device:TPU:0, one launch (start us, length us, event | category | flops | bytes accessed | tf_op | source)
XLA Modules:
  0.0 45.0 jit_solution(14385276333378540475)
XLA Ops:
  0.6 0.8 %shard_map.67 = (bf16[112,128]{1,0:T(8,128)(2,1)S(1)}, bf16[112,128]{1,0:T(8,128)(2,1)S(1)}, f32[1,1024]{1,0:T(1,128)S(1)}, s32[2,512]{1,0:T(2,128)S(1)}) custom-call(bf16[96,1024]{1,0:T(8,128)(2,1)} %states_ref.3, f32[1,1024]{1,0:T(1,128)} %bitcast.3, s32[2,512]{1,0:T(2,128)} %index_ref.1), custom_call_target="tpu_custom_call" | custom-call | bytes 4194304 | tf_op jit(solution)/shard_map/pallas_call | solution.py:26
  2.0 2.6 %collective-permute-start.1 = (bf16[112,128]{1,0:T(8,128)(2,1)S(1)}, bf16[112,128]{1,0:T(8,128)(2,1)S(1)}, u32[]{:S(2)}, u32[]{:S(2)}) collective-permute-start(bf16[112,128]{1,0:T(8,128)(2,1)S(1)} %get-tuple-element.67), channel_id=1, source_target_pairs={{0,8},{1,2},{2,1},{3,4},{4,3},{5,6},{6,5},{7,15},{8,0},{9,10},{10,... | collective-permute-start | bytes 86024 | tf_op jit(solution)/shard_map/ppermute | solution.py:416
  4.6 2.4 %shard_map.68 = (bf16[1280,1024]{1,0:T(8,128)(2,1)S(1)}, bf16[256,1024]{1,0:T(8,128)(2,1)S(1)}, bf16[512,1024]{1,0:T(8,128)(2,1)S(1)}, bf16[96,1024]{1,0:T(8,128...) custom-call(s32[2,512]{1,0:T(2,128)S(1)} %get-tuple-element.64.index_ref, ...), custom_call_target="tpu_custom_call" | custom-call | flops 314572800 | bytes 4194304 | tf_op jit(solution)/shard_map/pallas_call | solution.py:26
  7.8 1.5 %collective-permute-start.3 = (bf16[96,256]{1,0:T(8,128)(2,1)S(1)}, bf16[96,256]{1,0:T(8,128)(2,1)S(1)}, u32[]{:S(2)}, u32[]{:S(2)}) collective-permute-start(bf16[96,256]{1,0:T(8,128)(2,1)S(1)} %get-tuple-element.74), channel_id=1, source_target_pairs={{0,8},{1,2},{2,1},{3,4},{4,3},{5,6},{6,5},{7,15},{8,0},{9,10},{10,... | collective-permute-start | bytes 147464 | tf_op jit(solution)/shard_map/ppermute | solution.py:416
  9.3 2.6 %shard_map.70 = (bf16[96,768]{1,0:T(8,128)(2,1)S(1)}, bf16[768,1024]{1,0:T(8,128)(2,1)S(1)}, bf16[512,512]{1,0:T(8,128)(2,1)S(1)}, f32[1,512]{1,0:T(1,128)S(1)},...) custom-call(bf16[96,768]{1,0:T(8,128)(2,1)S(1)} %get-tuple-element.77.inner_ref.old_ref, ...), custom_call_target="tpu_custom_call" | custom-call | flops 1342177280 | bytes 4194304 | tf_op jit(solution)/shard_map/pallas_call | solution.py:26
  12.4 1.5 %collective-permute-start.5 = (bf16[96,256]{1,0:T(8,128)(2,1)S(1)}, bf16[96,256]{1,0:T(8,128)(2,1)S(1)}, u32[]{:S(2)}, u32[]{:S(2)}) collective-permute-start(bf16[96,256]{1,0:T(8,128)(2,1)S(1)} %get-tuple-element.87), channel_id=1, source_target_pairs={{0,8},{1,2},{2,1},{3,4},{4,3},{5,6},{6,5},{7,15},{8,0},{9,10},{10,... | collective-permute-start | bytes 147464 | tf_op jit(solution)/shard_map/ppermute | solution.py:416
  13.9 2.7 %shard_map.72 = (bf16[96,768]{1,0:T(8,128)(2,1)S(1)}, f32[96,512]{1,0:T(8,128)S(1)}, bf16[768,512]{1,0:T(8,128)(2,1)S(1)}, bf16[256,768]{1,0:T(8,128)(2,1)S(1)}, f32[1,768]{1,0:T(1,128)S(1)}) custom-call(bf16[96,512]{1,0:T(8,128)(2,1)S(1)} %get-tuple-element.88.zone_ref.mid_ref.rest_0_, bf16[96,768]{1,0:T(8,128)(2,1)S(1)} %get-tuple-element.89.inner_ref.old_ref, ...), custom_call_target="tpu_custom_call" | custom-call | flops 671088640 | bytes 4194304 | tf_op jit(solution)/shard_map/pallas_call | solution.py:26
  17.2 1.5 %collective-permute-start.7 = (bf16[96,256]{1,0:T(8,128)(2,1)S(1)}, bf16[96,256]{1,0:T(8,128)(2,1)S(1)}, u32[]{:S(2)}, u32[]{:S(2)}) collective-permute-start(bf16[96,256]{1,0:T(8,128)(2,1)S(1)} %get-tuple-element.95), channel_id=1, source_target_pairs={{0,8},{1,2},{2,1},{3,4},{4,3},{5,6},{6,5},{7,15},{8,0},{9,10},{10,... | collective-permute-start | bytes 147464 | tf_op jit(solution)/shard_map/ppermute | solution.py:416
  18.6 2.5 %shard_map.74 = (bf16[768,768]{1,0:T(8,128)(2,1)S(1)}, f32[1,768]{1,0:T(1,128)S(1)}, bf16[96,768]{1,0:T(8,128)(2,1)}, f32[96,512]{1,0:T(8,128)S(1)}, f32[96,768]{1,0:T(8,128)S(1)}) custom-call(bf16[96,512]{1,0:T(8,128)(2,1)S(1)} %get-tuple-element.96.zone_ref.mid_ref.old_ref, bf16[96,768]{1,0:T(8,128)(2,1)S(1)} %get-tuple-element.97.inner_ref.old_ref, ...), custom_call_target="tpu_custom_call" | custom-call | flops 671088640 | bytes 4194304 | tf_op jit(solution)/shard_map/pallas_call | solution.py:26
  21.9 1.6 %collective-permute-start.10 = (bf16[96,768]{1,0:T(8,128)(2,1)S(1)}, bf16[96,768]{1,0:T(8,128)(2,1)S(1)}, u32[]{:S(2)}, u32[]{:S(2)}) collective-permute-start(bf16[96,768]{1,0:T(8,128)(2,1)S(1)} %shard_map.77.inner_ref), channel_id=1, source_target_pairs={{0,8},{1,17},{2,10},{3,19},{4,12},{5,21},{6,14},{7,23},{8,0},{9,25... | collective-permute-start | bytes 442376 | tf_op jit(solution)/shard_map/ppermute | solution.py:435
  23.4 1.5 %collective-permute-start.11 = (bf16[96,768]{1,0:T(8,128)(2,1)S(1)}, bf16[96,768]{1,0:T(8,128)(2,1)S(1)}, u32[]{:S(2)}, u32[]{:S(2)}) collective-permute-start(bf16[96,768]{1,0:T(8,128)(2,1)S(1)} %shard_map.77.inner_ref), channel_id=1, source_target_pairs={{0,16},{1,9},{2,18},{3,11},{4,20},{5,13},{6,22},{7,15},{8,24},{9,1... | collective-permute-start | bytes 442376 | tf_op jit(solution)/shard_map/ppermute | solution.py:435
  25.5 0.7 %collective-permute-done.8.got_a_ref = bf16[96,256]{1,0:T(8,128)(2,1)S(1)} collective-permute-done((bf16[96,256]{1,0:T(8,128)(2,1)S(1)}, bf16[96,256]{1,0:T(8,128)(2,1)S(1)}, u32[]{:S(2)}, u32[]{:S(2)}) %collective-permute-start.8) | collective-permute-done | bytes 49184 | tf_op jit(solution)/shard_map/ppermute | solution.py:416
  26.2 3.0 %collective-permute-done.9.got_b_ref = bf16[96,256]{1,0:T(8,128)(2,1)S(1)} collective-permute-done((bf16[96,256]{1,0:T(8,128)(2,1)S(1)}, bf16[96,256]{1,0:T(8,128)(2,1)S(1)}, u32[]{:S(2)}, u32[]{:S(2)}) %collective-permute-start.9) | collective-permute-done | bytes 49184 | tf_op jit(solution)/shard_map/ppermute | solution.py:416
  29.3 1.6 %collective-permute-start.12 = (bf16[96,512]{1,0:T(8,128)(2,1)S(1)}, bf16[96,512]{1,0:T(8,128)(2,1)S(1)}, u32[]{:S(2)}, u32[]{:S(2)}) collective-permute-start(bf16[96,512]{1,0:T(8,128)(2,1)S(1)} %shard_map.76.zone_ref.refs_7_), channel_id=1, source_target_pairs={{0,8},{1,17},{2,10},{3,19},{4,12},{5,21},{6,14},{7,23},{8,0},{9,25... | collective-permute-start | bytes 294920 | tf_op jit(solution)/shard_map/ppermute | solution.py:435
  30.8 0.7 %collective-permute-start.13 = (bf16[96,512]{1,0:T(8,128)(2,1)S(1)}, bf16[96,512]{1,0:T(8,128)(2,1)S(1)}, u32[]{:S(2)}, u32[]{:S(2)}) collective-permute-start(bf16[96,512]{1,0:T(8,128)(2,1)S(1)} %shard_map.76.zone_ref.refs_7_), channel_id=1, source_target_pairs={{0,16},{1,9},{2,18},{3,11},{4,20},{5,13},{6,22},{7,15},{8,24},{9,1... | collective-permute-start | bytes 294920 | tf_op jit(solution)/shard_map/ppermute | solution.py:435
  31.5 1.3 %shard_map.78 = (bf16[96,768]{1,0:T(8,128)(2,1)S(1)}, bf16[96,512]{1,0:T(8,128)(2,1)S(1)}, bf16[96,1024]{1,0:T(8,128)(2,1)}) custom-call(bf16[96,512]{1,0:T(8,128)(2,1)S(1)} %shard_map.76.zone_ref.refs_7_, bf16[96,768]{1,0:T(8,128)(2,1)S(1)} %shard_map.77.inner_ref, f32[1,768]{1,0:T(1,128)S(1)} %get-tuple-element.79.shift_inner_ref, ...), custom_call_target="tpu_custom_call" | custom-call | flops 314572800 | bytes 4194304 | tf_op jit(solution)/shard_map/pallas_call | solution.py:26
  32.9 0.9 %shard_map.79 = (f32[96,512]{1,0:T(8,128)S(1)}, f32[288,192]{1,0:T(8,128)S(1)}, f32[96,96]{1,0:T(8,128)S(1)}, f32[96,96]{1,0:T(8,128)S(1)}, bf16[96,512]{1,0:T(8,128)(2,1)S(1)}) custom-call(bf16[96,768]{1,0:T(8,128)(2,1)S(1)} %shard_map.77.inner_ref, bf16[96,768]{1,0:T(8,128)(2,1)S(1)} %collective-permute-done.10.first_ref, ...), custom_call_target="tpu_custom_call" | custom-call | flops 157286400 | bytes 4194304 | tf_op jit(solution)/shard_map/pallas_call | solution.py:26
  34.3 1.1 %collective-permute-done.13.refs_9_ = bf16[96,512]{1,0:T(8,128)(2,1)S(1)} collective-permute-done((bf16[96,512]{1,0:T(8,128)(2,1)S(1)}, bf16[96,512]{1,0:T(8,128)(2,1)S(1)}, u32[]{:S(2)}, u32[]{:S(2)}) %collective-permute-start.13) | collective-permute-done | bytes 98336 | tf_op jit(solution)/shard_map/ppermute | solution.py:435
  36.1 1.3 %collective-permute-done.14.got_ref = bf16[2,2,96,96]{3,2,1,0:T(8,128)(2,1)S(1)} collective-permute-done((bf16[2,2,96,96]{3,2,1,0:T(8,128)(2,1)S(1)}, bf16[2,2,96,96]{3,2,1,0:T(8,128)(2,1)S(1)}, u32[]{:S(2)}, u32[]{:S(2)}) %collective-permute-start.14) | collective-permute-done | bytes 73760 | tf_op jit(solution)/shard_map/ppermute | solution.py:416
  37.5 2.0 %collective-permute-start.16 = (bf16[2,96,96]{2,1,0:T(8,128)(2,1)S(1)}, bf16[2,96,96]{2,1,0:T(8,128)(2,1)S(1)}, u32[]{:S(2)}, u32[]{:S(2)}) collective-permute-start(bf16[2,96,96]{2,1,0:T(8,128)(2,1)S(1)} %get-tuple-element.119.mine_ref), channel_id=1, source_target_pairs={{0,10},{1,5},{2,8},{3,13},{4,14},{5,1},{6,12},{7,3},{8,2},{9,7},{1... | collective-permute-start | bytes 110600 | tf_op jit(solution)/shard_map/ppermute | solution.py:447
  39.4 2.7 %collective-permute-done.15.first_ref = bf16[2,96,96]{2,1,0:T(8,128)(2,1)S(1)} collective-permute-done((bf16[2,96,96]{2,1,0:T(8,128)(2,1)S(1)}, bf16[2,96,96]{2,1,0:T(8,128)(2,1)S(1)}, u32[]{:S(2)}, u32[]{:S(2)}) %collective-permute-start.15) | collective-permute-done | bytes 36896 | tf_op jit(solution)/shard_map/ppermute | solution.py:447
  42.1 1.0 %collective-permute-done.16.second_ref = bf16[2,96,96]{2,1,0:T(8,128)(2,1)S(1)} collective-permute-done((bf16[2,96,96]{2,1,0:T(8,128)(2,1)S(1)}, bf16[2,96,96]{2,1,0:T(8,128)(2,1)S(1)}, u32[]{:S(2)}, u32[]{:S(2)}) %collective-permute-start.16) | collective-permute-done | bytes 36896 | tf_op jit(solution)/shard_map/ppermute | solution.py:447
  43.2 1.2 %collective-permute-done.17.got_ref = bf16[96,96]{1,0:T(8,128)(2,1)S(1)} collective-permute-done((bf16[96,96]{1,0:T(8,128)(2,1)S(1)}, bf16[96,96]{1,0:T(8,128)(2,1)S(1)}, u32[]{:S(2)}, u32[]{:S(2)}) %collective-permute-start.17) | collective-permute-done | bytes 18464 | tf_op jit(solution)/shard_map/ppermute | solution.py:416
  44.4 0.6 %shard_map.83 = (f32[48,96]{1,0:T(8,128)}, f32[48,96]{1,0:T(8,128)}) custom-call(f32[96,96]{1,0:T(8,128)S(1)} %get-tuple-element.121.keep_ref, bf16[96,96]{1,0:T(8,128)(2,1)S(1)} %collective-permute-done.17.got_ref), custom_call_target="tpu_custom_call" | custom-call | bytes 4194304 | tf_op jit(solution)/shard_map/pallas_call | solution.py:26
  (29 shorter events, 5.2 us)
Async XLA Ops:
  1.5 5.5 %collective-permute-start = (bf16[112,128]{1,0:T(8,128)(2,1)S(1)}, bf16[112,128]{1,0:T(8,128)(2,1)S(1)}, u32[]{:S(2)}, u32[]{:S(2)}) collective-permute-start(bf16[112,128]{1,0:T(8,128)(2,1)S(1)} %get-tuple-element.66), channel_id=1, source_target_pairs={{0,1},{1,0},{2,3},{3,2},{4,5},{5,4},{6,7},{7,6},{8,9},{9,8},{10,11... | collective-permute-start | bytes 86024 | tf_op jit(solution)/shard_map/ppermute | solution.py:416
  2.0 5.0 %collective-permute-start.1 = (bf16[112,128]{1,0:T(8,128)(2,1)S(1)}, bf16[112,128]{1,0:T(8,128)(2,1)S(1)}, u32[]{:S(2)}, u32[]{:S(2)}) collective-permute-start(bf16[112,128]{1,0:T(8,128)(2,1)S(1)} %get-tuple-element.67), channel_id=1, source_target_pairs={{0,8},{1,2},{2,1},{3,4},{4,3},{5,6},{6,5},{7,15},{8,0},{9,10},{10,... | collective-permute-start | bytes 86024 | tf_op jit(solution)/shard_map/ppermute | solution.py:416
  7.6 4.3 %collective-permute-start.2 = (bf16[96,256]{1,0:T(8,128)(2,1)S(1)}, bf16[96,256]{1,0:T(8,128)(2,1)S(1)}, u32[]{:S(2)}, u32[]{:S(2)}) collective-permute-start(bf16[96,256]{1,0:T(8,128)(2,1)S(1)} %get-tuple-element.73), channel_id=1, source_target_pairs={{0,1},{1,0},{2,3},{3,2},{4,5},{5,4},{6,7},{7,6},{8,9},{9,8},{10,11... | collective-permute-start | bytes 147464 | tf_op jit(solution)/shard_map/ppermute | solution.py:416
  7.8 4.1 %collective-permute-start.3 = (bf16[96,256]{1,0:T(8,128)(2,1)S(1)}, bf16[96,256]{1,0:T(8,128)(2,1)S(1)}, u32[]{:S(2)}, u32[]{:S(2)}) collective-permute-start(bf16[96,256]{1,0:T(8,128)(2,1)S(1)} %get-tuple-element.74), channel_id=1, source_target_pairs={{0,8},{1,2},{2,1},{3,4},{4,3},{5,6},{6,5},{7,15},{8,0},{9,10},{10,... | collective-permute-start | bytes 147464 | tf_op jit(solution)/shard_map/ppermute | solution.py:416
  12.2 4.4 %collective-permute-start.4 = (bf16[96,256]{1,0:T(8,128)(2,1)S(1)}, bf16[96,256]{1,0:T(8,128)(2,1)S(1)}, u32[]{:S(2)}, u32[]{:S(2)}) collective-permute-start(bf16[96,256]{1,0:T(8,128)(2,1)S(1)} %get-tuple-element.86), channel_id=1, source_target_pairs={{0,1},{1,0},{2,3},{3,2},{4,5},{5,4},{6,7},{7,6},{8,9},{9,8},{10,11... | collective-permute-start | bytes 147464 | tf_op jit(solution)/shard_map/ppermute | solution.py:416
  12.4 4.2 %collective-permute-start.5 = (bf16[96,256]{1,0:T(8,128)(2,1)S(1)}, bf16[96,256]{1,0:T(8,128)(2,1)S(1)}, u32[]{:S(2)}, u32[]{:S(2)}) collective-permute-start(bf16[96,256]{1,0:T(8,128)(2,1)S(1)} %get-tuple-element.87), channel_id=1, source_target_pairs={{0,8},{1,2},{2,1},{3,4},{4,3},{5,6},{6,5},{7,15},{8,0},{9,10},{10,... | collective-permute-start | bytes 147464 | tf_op jit(solution)/shard_map/ppermute | solution.py:416
  16.9 4.2 %collective-permute-start.6 = (bf16[96,256]{1,0:T(8,128)(2,1)S(1)}, bf16[96,256]{1,0:T(8,128)(2,1)S(1)}, u32[]{:S(2)}, u32[]{:S(2)}) collective-permute-start(bf16[96,256]{1,0:T(8,128)(2,1)S(1)} %get-tuple-element.94), channel_id=1, source_target_pairs={{0,1},{1,0},{2,3},{3,2},{4,5},{5,4},{6,7},{7,6},{8,9},{9,8},{10,11... | collective-permute-start | bytes 147464 | tf_op jit(solution)/shard_map/ppermute | solution.py:416
  17.2 4.1 %collective-permute-start.7 = (bf16[96,256]{1,0:T(8,128)(2,1)S(1)}, bf16[96,256]{1,0:T(8,128)(2,1)S(1)}, u32[]{:S(2)}, u32[]{:S(2)}) collective-permute-start(bf16[96,256]{1,0:T(8,128)(2,1)S(1)} %get-tuple-element.95), channel_id=1, source_target_pairs={{0,8},{1,2},{2,1},{3,4},{4,3},{5,6},{6,5},{7,15},{8,0},{9,10},{10,... | collective-permute-start | bytes 147464 | tf_op jit(solution)/shard_map/ppermute | solution.py:416
  21.9 11.0 %collective-permute-start.10 = (bf16[96,768]{1,0:T(8,128)(2,1)S(1)}, bf16[96,768]{1,0:T(8,128)(2,1)S(1)}, u32[]{:S(2)}, u32[]{:S(2)}) collective-permute-start(bf16[96,768]{1,0:T(8,128)(2,1)S(1)} %shard_map.77.inner_ref), channel_id=1, source_target_pairs={{0,8},{1,17},{2,10},{3,19},{4,12},{5,21},{6,14},{7,23},{8,0},{9,25... | collective-permute-start | bytes 442376 | tf_op jit(solution)/shard_map/ppermute | solution.py:435
  23.4 9.5 %collective-permute-start.11 = (bf16[96,768]{1,0:T(8,128)(2,1)S(1)}, bf16[96,768]{1,0:T(8,128)(2,1)S(1)}, u32[]{:S(2)}, u32[]{:S(2)}) collective-permute-start(bf16[96,768]{1,0:T(8,128)(2,1)S(1)} %shard_map.77.inner_ref), channel_id=1, source_target_pairs={{0,16},{1,9},{2,18},{3,11},{4,20},{5,13},{6,22},{7,15},{8,24},{9,1... | collective-permute-start | bytes 442376 | tf_op jit(solution)/shard_map/ppermute | solution.py:435
  24.9 1.2 %collective-permute-start.8 = (bf16[96,256]{1,0:T(8,128)(2,1)S(1)}, bf16[96,256]{1,0:T(8,128)(2,1)S(1)}, u32[]{:S(2)}, u32[]{:S(2)}) collective-permute-start(bf16[96,256]{1,0:T(8,128)(2,1)S(1)} %get-tuple-element.103), channel_id=1, source_target_pairs={{0,1},{1,0},{2,3},{3,2},{4,5},{5,4},{6,7},{7,6},{8,9},{9,8},{10,11... | collective-permute-start | bytes 147464 | tf_op jit(solution)/shard_map/ppermute | solution.py:416
  24.9 4.2 %collective-permute-start.9 = (bf16[96,256]{1,0:T(8,128)(2,1)S(1)}, bf16[96,256]{1,0:T(8,128)(2,1)S(1)}, u32[]{:S(2)}, u32[]{:S(2)}) collective-permute-start(bf16[96,256]{1,0:T(8,128)(2,1)S(1)} %get-tuple-element.104), channel_id=1, source_target_pairs={{0,8},{1,2},{2,1},{3,4},{4,3},{5,6},{6,5},{7,15},{8,0},{9,10},{10,... | collective-permute-start | bytes 147464 | tf_op jit(solution)/shard_map/ppermute | solution.py:416
  29.3 5.1 %collective-permute-start.12 = (bf16[96,512]{1,0:T(8,128)(2,1)S(1)}, bf16[96,512]{1,0:T(8,128)(2,1)S(1)}, u32[]{:S(2)}, u32[]{:S(2)}) collective-permute-start(bf16[96,512]{1,0:T(8,128)(2,1)S(1)} %shard_map.76.zone_ref.refs_7_), channel_id=1, source_target_pairs={{0,8},{1,17},{2,10},{3,19},{4,12},{5,21},{6,14},{7,23},{8,0},{9,25... | collective-permute-start | bytes 294920 | tf_op jit(solution)/shard_map/ppermute | solution.py:435
  30.8 4.6 %collective-permute-start.13 = (bf16[96,512]{1,0:T(8,128)(2,1)S(1)}, bf16[96,512]{1,0:T(8,128)(2,1)S(1)}, u32[]{:S(2)}, u32[]{:S(2)}) collective-permute-start(bf16[96,512]{1,0:T(8,128)(2,1)S(1)} %shard_map.76.zone_ref.refs_7_), channel_id=1, source_target_pairs={{0,16},{1,9},{2,18},{3,11},{4,20},{5,13},{6,22},{7,15},{8,24},{9,1... | collective-permute-start | bytes 294920 | tf_op jit(solution)/shard_map/ppermute | solution.py:435
  36.0 1.4 %collective-permute-start.14 = (bf16[2,2,96,96]{3,2,1,0:T(8,128)(2,1)S(1)}, bf16[2,2,96,96]{3,2,1,0:T(8,128)(2,1)S(1)}, u32[]{:S(2)}, u32[]{:S(2)}) collective-permute-start(bf16[2,2,96,96]{3,2,1,0:T(8,128)(2,1)S(1)} %get-tuple-element.118), channel_id=1, source_target_pairs={{0,1},{1,0},{2,3},{3,2},{4,5},{5,4},{6,7},{7,6},{8,9},{9,8},{10,11... | collective-permute-start | bytes 221192 | tf_op jit(solution)/shard_map/ppermute | solution.py:416
  37.4 4.7 %collective-permute-start.15 = (bf16[2,96,96]{2,1,0:T(8,128)(2,1)S(1)}, bf16[2,96,96]{2,1,0:T(8,128)(2,1)S(1)}, u32[]{:S(2)}, u32[]{:S(2)}) collective-permute-start(bf16[2,96,96]{2,1,0:T(8,128)(2,1)S(1)} %get-tuple-element.120), channel_id=1, source_target_pairs={{0,2},{1,13},{2,0},{3,5},{4,12},{5,3},{6,4},{7,1},{8,10},{9,15},{1... | collective-permute-start | bytes 110600 | tf_op jit(solution)/shard_map/ppermute | solution.py:447
  37.5 5.6 %collective-permute-start.16 = (bf16[2,96,96]{2,1,0:T(8,128)(2,1)S(1)}, bf16[2,96,96]{2,1,0:T(8,128)(2,1)S(1)}, u32[]{:S(2)}, u32[]{:S(2)}) collective-permute-start(bf16[2,96,96]{2,1,0:T(8,128)(2,1)S(1)} %get-tuple-element.119.mine_ref), channel_id=1, source_target_pairs={{0,10},{1,5},{2,8},{3,13},{4,14},{5,1},{6,12},{7,3},{8,2},{9,7},{1... | collective-permute-start | bytes 110600 | tf_op jit(solution)/shard_map/ppermute | solution.py:447
  43.1 1.3 %collective-permute-start.17 = (bf16[96,96]{1,0:T(8,128)(2,1)S(1)}, bf16[96,96]{1,0:T(8,128)(2,1)S(1)}, u32[]{:S(2)}, u32[]{:S(2)}) collective-permute-start(bf16[96,96]{1,0:T(8,128)(2,1)S(1)} %get-tuple-element.122), channel_id=1, source_target_pairs={{0,1},{1,0},{2,3},{3,2},{4,5},{5,4},{6,7},{7,6},{8,9},{9,8},{10,11... | collective-permute-start | bytes 55304 | tf_op jit(solution)/shard_map/ppermute | solution.py:416

commit v6 on v5

--- a/solution.py
+++ b/solution.py
@@ -285,21 +285,27 @@
     filtered_ref[:, owned - rim :] = zone_ref[:, width : width + rim]
 
 
-def by_core(first_ref, second_ref):
-    odd, first, second = is_odd(), first_ref[...], second_ref[...]
-    return jnp.where(odd, second, first), jnp.where(odd, first, second)
-
-
-def neighbour_body(inner_ref, first_ref, second_ref, energy_ref, shift_inner_ref, columns_ref, square_ref, diagonal_ref,
-                   part_ref, found_ref, other_ref, other_energy_ref, toward_ref):
-    beside, across = by_core(first_ref, second_ref)
+def first_neighbour_body(inner_ref, first_ref, energy_ref, shift_inner_ref, columns_ref, square_ref, diagonal_ref,
+                         first_energy_ref, part_ref, found_ref):
+    first = first_ref[...]
     line = diagonal_ref[...] + (shift_inner_ref[...] + spectrum_center)
-    energy = (mm(beside, square_ref[...]) + line * beside.astype(F32)).astype(BF16)
-    part_ref[...] = mm(beside, columns_ref[...])
-    toward_ref[...] = mm(across, columns_ref[...]).astype(BF16)
-    inner_found(found_ref, (inner_ref[...], beside, across), inner_ref, energy_ref)
-    other_ref[...] = mm_nt(across, beside)
-    other_energy_ref[...] = mm_nt(across, energy)
+    first_energy_ref[...] = (mm(first, square_ref[...]) + line * first.astype(F32)).astype(BF16)
+    part_ref[...] = mm(first, columns_ref[...])
+    inner_found(found_ref, (inner_ref[...], first), inner_ref, energy_ref)
+
+
+def turned(first, second):
+    odd = is_odd()
+    return mm_nt(jnp.where(odd, first, second), jnp.where(odd, second, first))
+
+
+def second_neighbour_body(inner_ref, first_ref, second_ref, first_energy_ref, energy_ref, columns_ref,
+                          found_ref, other_ref, other_energy_ref, toward_ref):
+    second = second_ref[...]
+    inner_found(found_ref, (second,), inner_ref, energy_ref)
+    other_ref[...] = turned(first_ref[...], second)
+    other_energy_ref[...] = turned(first_energy_ref[...], second)
+    toward_ref[...] = mm(second, columns_ref[...]).astype(BF16)
 
 
 def inner_found(found_ref, blocks, states_ref, energy_ref):
@@ -323,10 +329,9 @@
 
 def project_body(square_of_four, scale, energy_zone_ref, found_ref, *refs):
     if square_of_four:
-        (part_ref, other_ref, other_energy_ref, toward_ref, shift_zone_ref, border_ref, border_diagonal_ref), refs = refs[:7], refs[7:]
-        *zones, out_ref, give_ref, other_zone_ref, beside_ref, across_ref = refs
-        beside_ref[...], across_ref[...] = by_core(zones[1], zones[2])
-        zones = [zones[0], beside_ref, across_ref]
+        (second_found_ref, part_ref, other_ref, other_energy_ref, toward_ref,
+         shift_zone_ref, border_ref, border_diagonal_ref), refs = refs[:8], refs[8:]
+        *zones, out_ref, give_ref, other_zone_ref = refs
     else:
         *zones, out_ref, give_ref = refs
     count = energy_zone_ref.shape[0]
@@ -345,13 +350,20 @@
 
     if square_of_four:
         zone_energy(zones[1], part_ref[...], shift_zone_ref, border_ref, border_diagonal_ref, other_zone_ref)
-    for distance, zone in enumerate(zones):
-        here = slice(distance * count, (distance + 1) * count)
+    for place, zone in enumerate(zones):
+        distance, found, row = place, found_ref, place
+        if square_of_four and place:
+            distance = jnp.where(odd, 3 - place, place)
+            if place == 2:
+                found, row = second_found_ref, 0
+        here = slice(row * count, (row + 1) * count)
         states, energy = zone_found(zone, zones[0], energy_zone_ref)
-        put(distance, found_ref[here, :count] + states, found_ref[here, count:] + energy)
+        put(distance, found[here, :count] + states, found[here, count:] + energy)
     if square_of_four:
-        states, energy = zone_found(zones[2], zones[1], other_zone_ref)
-        energy = energy + mm_nt(toward_ref[...], zones[1][...])
+        rim = zones[1].shape[1] // 4
+        own = slice(rim, 3 * rim)
+        states = turned(zones[1][:, own], zones[2][:, own])
+        energy = turned(other_zone_ref[...], zones[2][...]) + turned(zones[1][...], toward_ref[...])
         put(3, other_ref[...] + states, other_energy_ref[...] + energy)
         for order, (even, uneven) in enumerate(CORE_WAYS):
             give_ref[order] = out_ref[chip_at(jnp.where(odd, even, uneven))]
@@ -538,17 +550,21 @@
     pair_of = SHAPE((count, count), F32)
     found_of = SHAPE((len(inner_blocks) * count, 2 * count), F32)
     if square_of_four:
-        part_x, found, *other = call(
-            neighbour_body, (sums_of, found_of, pair_of, pair_of, zone),
-            (*inner_blocks, energy, shift_inner, columns, square, diagonal), work // 2,
+        first_energy, part_1, found = call(
+            first_neighbour_body, (inner, sums_of, SHAPE((2 * count, 2 * count), F32)),
+            (*inner_blocks[:2], energy, shift_inner, columns, square, diagonal), work // 2,
         )
-        extra = (part_x, *other, shift_zone, border, border_diagonal)
-        scratch = [pltpu.VMEM((count, 4 * rim), BF16)] * 3
+        second_found, *other = call(
+            second_neighbour_body, (SHAPE((count, 2 * count), F32), pair_of, pair_of, zone),
+            (*inner_blocks, first_energy, energy, columns), work // 4,
+        )
+        extra = (second_found, part_1, *other, shift_zone, border, border_diagonal)
+        scratch = [pltpu.VMEM((count, 4 * rim), BF16)]
     else:
         found = call(gram_body, found_of, (*inner_blocks, energy), work)
     share = count * n_state // n_space
     chips = n_space // 2
-    turned = SHAPE((share, count), F32)
+    output = SHAPE((share, count), F32)
     piece = SHAPE((2 * share, count), BF16)
     both_halves = SHAPE((2, 2 * share, count), BF16)
     mine, give_half = call(
@@ -565,11 +581,11 @@
             gather_body, (SHAPE(piece.shape, F32), piece), (pieces[1], *shares), 0
         )
         got_last = swap(give_last, n_state, n_space, 0)
-        intersection, projected = call(join_body, (turned, turned), (keep, got_last), 0)
+        intersection, projected = call(join_body, (output, output), (keep, got_last), 0)
     else:
         pieces = call(halve_body, (piece,) * chips, (mine, got_half), 0)
         shares = [across(p, "space", 2 * d) for d, p in enumerate(pieces) if d]
-        intersection, projected = call(final_body, (turned, turned), (pieces[0], *shares), 0)
+        intersection, projected = call(final_body, (output, output), (pieces[0], *shares), 0)
     return filtered, intersection.T, projected.T
 
 

time: 45.2 us -> 45.2 us (level)
    pallas_call x17 -> x18, Pallas kernels: 16.1 us -> 16.4 us  [call(): pl.pallas_call(body, out_shape=outs, in_specs=where, out_specs=jax.tree.m...]
where the time goes in v6:
time: 45.2 us; the launch traced here: 45 us
  Pallas kernels  16.4 us (36%)
  starting transfers between devices  16.4 us (36%)
  waiting for transfers between devices  11.4 us (25%)
  between operations  0.81 us (2%)
    pallas_call x18, Pallas kernels, call(): pl.pallas_call(body, out_shape=outs, in_specs=where, out_specs=jax.tree.m...  16.4 us
    ppermute x12, starting transfers between devices, swap(): return lax.ppermute(block, ('state', 'space'), route)  9.07 us
    ppermute x12, waiting for transfers between devices, swap(): return lax.ppermute(block, ('state', 'space'), route)  6.33 us
    ppermute x4, starting transfers between devices, beside(): return lax.ppermute(block, ('state', 'space'), route)  5.32 us
    ppermute x2, waiting for transfers between devices, share_out(): return lax.ppermute(block, ('state', 'space'), route)  3.64 us
    ppermute x2, starting transfers between devices, share_out(): return lax.ppermute(block, ('state', 'space'), route)  2.04 us
    ppermute x4, waiting for transfers between devices, beside(): return lax.ppermute(block, ('state', 'space'), route)  1.44 us
  transfers between devices with their start and end apart: 18, of which 9 were waited for; matrix products, arithmetic and copies ran while one was open for 0% of the time, Pallas kernels for 28%

profile of v6, /device:TPU:0, one launch (start us, length us, event | category | flops | bytes accessed | tf_op | source)
XLA Modules:
  0.0 45.0 jit_solution(3704987021973138706)
XLA Ops:
  0.6 0.8 %shard_map.67 = (bf16[112,128]{1,0:T(8,128)(2,1)S(1)}, bf16[112,128]{1,0:T(8,128)(2,1)S(1)}, f32[1,1024]{1,0:T(1,128)S(1)}, s32[2,512]{1,0:T(2,128)S(1)}) custom-call(bf16[96,1024]{1,0:T(8,128)(2,1)} %states_ref.3, f32[1,1024]{1,0:T(1,128)} %bitcast.3, s32[2,512]{1,0:T(2,128)} %index_ref.1), custom_call_target="tpu_custom_call" | custom-call | bytes 4194304 | tf_op jit(solution)/shard_map/pallas_call | solution.py:26
  2.0 2.6 %collective-permute-start.1 = (bf16[112,128]{1,0:T(8,128)(2,1)S(1)}, bf16[112,128]{1,0:T(8,128)(2,1)S(1)}, u32[]{:S(2)}, u32[]{:S(2)}) collective-permute-start(bf16[112,128]{1,0:T(8,128)(2,1)S(1)} %get-tuple-element.69), channel_id=1, source_target_pairs={{0,8},{1,2},{2,1},{3,4},{4,3},{5,6},{6,5},{7,15},{8,0},{9,10},{10,... | collective-permute-start | bytes 86024 | tf_op jit(solution)/shard_map/ppermute | solution.py:428
  4.6 2.4 %shard_map.68 = (bf16[1280,1024]{1,0:T(8,128)(2,1)S(1)}, bf16[256,1024]{1,0:T(8,128)(2,1)S(1)}, bf16[512,1024]{1,0:T(8,128)(2,1)S(1)}, bf16[96,1024]{1,0:T(8,128...) custom-call(s32[2,512]{1,0:T(2,128)S(1)} %get-tuple-element.66.index_ref, ...), custom_call_target="tpu_custom_call" | custom-call | flops 314572800 | bytes 4194304 | tf_op jit(solution)/shard_map/pallas_call | solution.py:26
  7.8 1.5 %collective-permute-start.3 = (bf16[96,256]{1,0:T(8,128)(2,1)S(1)}, bf16[96,256]{1,0:T(8,128)(2,1)S(1)}, u32[]{:S(2)}, u32[]{:S(2)}) collective-permute-start(bf16[96,256]{1,0:T(8,128)(2,1)S(1)} %get-tuple-element.76), channel_id=1, source_target_pairs={{0,8},{1,2},{2,1},{3,4},{4,3},{5,6},{6,5},{7,15},{8,0},{9,10},{10,... | collective-permute-start | bytes 147464 | tf_op jit(solution)/shard_map/ppermute | solution.py:428
  9.3 2.6 %shard_map.70 = (bf16[96,768]{1,0:T(8,128)(2,1)S(1)}, bf16[768,1024]{1,0:T(8,128)(2,1)S(1)}, bf16[512,512]{1,0:T(8,128)(2,1)S(1)}, f32[1,512]{1,0:T(1,128)S(1)},...) custom-call(bf16[96,768]{1,0:T(8,128)(2,1)S(1)} %get-tuple-element.79.inner_ref.old_ref, ...), custom_call_target="tpu_custom_call" | custom-call | flops 1342177280 | bytes 4194304 | tf_op jit(solution)/shard_map/pallas_call | solution.py:26
  12.4 1.5 %collective-permute-start.5 = (bf16[96,256]{1,0:T(8,128)(2,1)S(1)}, bf16[96,256]{1,0:T(8,128)(2,1)S(1)}, u32[]{:S(2)}, u32[]{:S(2)}) collective-permute-start(bf16[96,256]{1,0:T(8,128)(2,1)S(1)} %get-tuple-element.89), channel_id=1, source_target_pairs={{0,8},{1,2},{2,1},{3,4},{4,3},{5,6},{6,5},{7,15},{8,0},{9,10},{10,... | collective-permute-start | bytes 147464 | tf_op jit(solution)/shard_map/ppermute | solution.py:428
  13.9 2.7 %shard_map.72 = (bf16[96,768]{1,0:T(8,128)(2,1)S(1)}, f32[96,512]{1,0:T(8,128)S(1)}, bf16[768,512]{1,0:T(8,128)(2,1)S(1)}, bf16[256,768]{1,0:T(8,128)(2,1)S(1)}, f32[1,768]{1,0:T(1,128)S(1)}) custom-call(bf16[96,512]{1,0:T(8,128)(2,1)S(1)} %get-tuple-element.90.zone_ref.mid_ref.rest_0_, bf16[96,768]{1,0:T(8,128)(2,1)S(1)} %get-tuple-element.91.inner_ref.old_ref, ...), custom_call_target="tpu_custom_call" | custom-call | flops 671088640 | bytes 4194304 | tf_op jit(solution)/shard_map/pallas_call | solution.py:26
  17.2 1.5 %collective-permute-start.7 = (bf16[96,256]{1,0:T(8,128)(2,1)S(1)}, bf16[96,256]{1,0:T(8,128)(2,1)S(1)}, u32[]{:S(2)}, u32[]{:S(2)}) collective-permute-start(bf16[96,256]{1,0:T(8,128)(2,1)S(1)} %get-tuple-element.97), channel_id=1, source_target_pairs={{0,8},{1,2},{2,1},{3,4},{4,3},{5,6},{6,5},{7,15},{8,0},{9,10},{10,... | collective-permute-start | bytes 147464 | tf_op jit(solution)/shard_map/ppermute | solution.py:428
  18.6 2.5 %shard_map.74 = (bf16[768,768]{1,0:T(8,128)(2,1)S(1)}, f32[1,768]{1,0:T(1,128)S(1)}, bf16[96,768]{1,0:T(8,128)(2,1)}, f32[96,512]{1,0:T(8,128)S(1)}, f32[96,768]{1,0:T(8,128)S(1)}) custom-call(bf16[96,512]{1,0:T(8,128)(2,1)S(1)} %get-tuple-element.98.zone_ref.mid_ref.old_ref, bf16[96,768]{1,0:T(8,128)(2,1)S(1)} %get-tuple-element.99.inner_ref.old_ref, ...), custom_call_target="tpu_custom_call" | custom-call | flops 671088640 | bytes 4194304 | tf_op jit(solution)/shard_map/pallas_call | solution.py:26
  21.9 1.6 %collective-permute-start.10 = (bf16[96,768]{1,0:T(8,128)(2,1)S(1)}, bf16[96,768]{1,0:T(8,128)(2,1)S(1)}, u32[]{:S(2)}, u32[]{:S(2)}) collective-permute-start(bf16[96,768]{1,0:T(8,128)(2,1)S(1)} %shard_map.77.inner_ref), channel_id=1, source_target_pairs={{0,8},{1,17},{2,10},{3,19},{4,12},{5,21},{6,14},{7,23},{8,0},{9,25... | collective-permute-start | bytes 442376 | tf_op jit(solution)/shard_map/ppermute | solution.py:447
  23.4 1.5 %collective-permute-start.11 = (bf16[96,768]{1,0:T(8,128)(2,1)S(1)}, bf16[96,768]{1,0:T(8,128)(2,1)S(1)}, u32[]{:S(2)}, u32[]{:S(2)}) collective-permute-start(bf16[96,768]{1,0:T(8,128)(2,1)S(1)} %shard_map.77.inner_ref), channel_id=1, source_target_pairs={{0,16},{1,9},{2,18},{3,11},{4,20},{5,13},{6,22},{7,15},{8,24},{9,1... | collective-permute-start | bytes 442376 | tf_op jit(solution)/shard_map/ppermute | solution.py:447
  25.5 0.7 %collective-permute-done.8.got_a_ref = bf16[96,256]{1,0:T(8,128)(2,1)S(1)} collective-permute-done((bf16[96,256]{1,0:T(8,128)(2,1)S(1)}, bf16[96,256]{1,0:T(8,128)(2,1)S(1)}, u32[]{:S(2)}, u32[]{:S(2)}) %collective-permute-start.8) | collective-permute-done | bytes 49184 | tf_op jit(solution)/shard_map/ppermute | solution.py:428
  26.2 3.0 %collective-permute-done.9.got_b_ref = bf16[96,256]{1,0:T(8,128)(2,1)S(1)} collective-permute-done((bf16[96,256]{1,0:T(8,128)(2,1)S(1)}, bf16[96,256]{1,0:T(8,128)(2,1)S(1)}, u32[]{:S(2)}, u32[]{:S(2)}) %collective-permute-start.9) | collective-permute-done | bytes 49184 | tf_op jit(solution)/shard_map/ppermute | solution.py:428
  29.3 1.6 %collective-permute-start.12 = (bf16[96,512]{1,0:T(8,128)(2,1)S(1)}, bf16[96,512]{1,0:T(8,128)(2,1)S(1)}, u32[]{:S(2)}, u32[]{:S(2)}) collective-permute-start(bf16[96,512]{1,0:T(8,128)(2,1)S(1)} %shard_map.76.zone_ref.refs_8_), channel_id=1, source_target_pairs={{0,8},{1,17},{2,10},{3,19},{4,12},{5,21},{6,14},{7,23},{8,0},{9,25... | collective-permute-start | bytes 294920 | tf_op jit(solution)/shard_map/ppermute | solution.py:447
  30.8 0.7 %collective-permute-start.13 = (bf16[96,512]{1,0:T(8,128)(2,1)S(1)}, bf16[96,512]{1,0:T(8,128)(2,1)S(1)}, u32[]{:S(2)}, u32[]{:S(2)}) collective-permute-start(bf16[96,512]{1,0:T(8,128)(2,1)S(1)} %shard_map.76.zone_ref.refs_8_), channel_id=1, source_target_pairs={{0,16},{1,9},{2,18},{3,11},{4,20},{5,13},{6,22},{7,15},{8,24},{9,1... | collective-permute-start | bytes 294920 | tf_op jit(solution)/shard_map/ppermute | solution.py:447
  31.5 1.4 %shard_map.78 = (bf16[96,768]{1,0:T(8,128)(2,1)S(1)}, bf16[96,512]{1,0:T(8,128)(2,1)S(1)}, bf16[96,1024]{1,0:T(8,128)(2,1)}) custom-call(bf16[96,512]{1,0:T(8,128)(2,1)S(1)} %shard_map.76.zone_ref.refs_8_, bf16[96,768]{1,0:T(8,128)(2,1)S(1)} %shard_map.77.inner_ref, f32[1,768]{1,0:T(1,128)S(1)} %get-tuple-element.81.shift_inner_ref, ...), custom_call_target="tpu_custom_call" | custom-call | flops 314572800 | bytes 4194304 | tf_op jit(solution)/shard_map/pallas_call | solution.py:26
  32.9 0.7 %shard_map.79 = (bf16[96,768]{1,0:T(8,128)(2,1)S(1)}, f32[96,512]{1,0:T(8,128)S(1)}, f32[192,192]{1,0:T(8,128)S(1)}) custom-call(bf16[96,768]{1,0:T(8,128)(2,1)S(1)} %shard_map.77.inner_ref, bf16[96,768]{1,0:T(8,128)(2,1)S(1)} %collective-permute-done.10.first_ref, bf16[96,768]{1,0:T(8,128)(2,1)S(1)} %get-tuple-element.113.energy_ref, ...), custom_call_target="tpu_custom_call" | custom-call | flops 157286400 | bytes 4194304 | tf_op jit(solution)/shard_map/pallas_call | solution.py:26
  34.3 1.1 %collective-permute-done.13.refs_10_ = bf16[96,512]{1,0:T(8,128)(2,1)S(1)} collective-permute-done((bf16[96,512]{1,0:T(8,128)(2,1)S(1)}, bf16[96,512]{1,0:T(8,128)(2,1)S(1)}, u32[]{:S(2)}, u32[]{:S(2)}) %collective-permute-start.13) | collective-permute-done | bytes 98336 | tf_op jit(solution)/shard_map/ppermute | solution.py:447
  36.1 1.3 %collective-permute-done.14.got_ref = bf16[2,2,96,96]{3,2,1,0:T(8,128)(2,1)S(1)} collective-permute-done((bf16[2,2,96,96]{3,2,1,0:T(8,128)(2,1)S(1)}, bf16[2,2,96,96]{3,2,1,0:T(8,128)(2,1)S(1)}, u32[]{:S(2)}, u32[]{:S(2)}) %collective-permute-start.14) | collective-permute-done | bytes 73760 | tf_op jit(solution)/shard_map/ppermute | solution.py:428
  37.5 2.0 %collective-permute-start.16 = (bf16[2,96,96]{2,1,0:T(8,128)(2,1)S(1)}, bf16[2,96,96]{2,1,0:T(8,128)(2,1)S(1)}, u32[]{:S(2)}, u32[]{:S(2)}) collective-permute-start(bf16[2,96,96]{2,1,0:T(8,128)(2,1)S(1)} %get-tuple-element.123.mine_ref), channel_id=1, source_target_pairs={{0,10},{1,5},{2,8},{3,13},{4,14},{5,1},{6,12},{7,3},{8,2},{9,7},{1... | collective-permute-start | bytes 110600 | tf_op jit(solution)/shard_map/ppermute | solution.py:459
  39.4 2.7 %collective-permute-done.15.first_ref = bf16[2,96,96]{2,1,0:T(8,128)(2,1)S(1)} collective-permute-done((bf16[2,96,96]{2,1,0:T(8,128)(2,1)S(1)}, bf16[2,96,96]{2,1,0:T(8,128)(2,1)S(1)}, u32[]{:S(2)}, u32[]{:S(2)}) %collective-permute-start.15) | collective-permute-done | bytes 36896 | tf_op jit(solution)/shard_map/ppermute | solution.py:459
  42.1 1.0 %collective-permute-done.16.second_ref = bf16[2,96,96]{2,1,0:T(8,128)(2,1)S(1)} collective-permute-done((bf16[2,96,96]{2,1,0:T(8,128)(2,1)S(1)}, bf16[2,96,96]{2,1,0:T(8,128)(2,1)S(1)}, u32[]{:S(2)}, u32[]{:S(2)}) %collective-permute-start.16) | collective-permute-done | bytes 36896 | tf_op jit(solution)/shard_map/ppermute | solution.py:459
  43.2 1.2 %collective-permute-done.17.got_ref = bf16[96,96]{1,0:T(8,128)(2,1)S(1)} collective-permute-done((bf16[96,96]{1,0:T(8,128)(2,1)S(1)}, bf16[96,96]{1,0:T(8,128)(2,1)S(1)}, u32[]{:S(2)}, u32[]{:S(2)}) %collective-permute-start.17) | collective-permute-done | bytes 18464 | tf_op jit(solution)/shard_map/ppermute | solution.py:428
  44.4 0.6 %shard_map.84 = (f32[48,96]{1,0:T(8,128)}, f32[48,96]{1,0:T(8,128)}) custom-call(f32[96,96]{1,0:T(8,128)S(1)} %get-tuple-element.125.keep_ref, bf16[96,96]{1,0:T(8,128)(2,1)S(1)} %collective-permute-done.17.got_ref), custom_call_target="tpu_custom_call" | custom-call | bytes 4194304 | tf_op jit(solution)/shard_map/pallas_call | solution.py:26
  (30 shorter events, 5.4 us)
Async XLA Ops:
  1.5 5.5 %collective-permute-start = (bf16[112,128]{1,0:T(8,128)(2,1)S(1)}, bf16[112,128]{1,0:T(8,128)(2,1)S(1)}, u32[]{:S(2)}, u32[]{:S(2)}) collective-permute-start(bf16[112,128]{1,0:T(8,128)(2,1)S(1)} %get-tuple-element.68), channel_id=1, source_target_pairs={{0,1},{1,0},{2,3},{3,2},{4,5},{5,4},{6,7},{7,6},{8,9},{9,8},{10,11... | collective-permute-start | bytes 86024 | tf_op jit(solution)/shard_map/ppermute | solution.py:428
  2.0 5.0 %collective-permute-start.1 = (bf16[112,128]{1,0:T(8,128)(2,1)S(1)}, bf16[112,128]{1,0:T(8,128)(2,1)S(1)}, u32[]{:S(2)}, u32[]{:S(2)}) collective-permute-start(bf16[112,128]{1,0:T(8,128)(2,1)S(1)} %get-tuple-element.69), channel_id=1, source_target_pairs={{0,8},{1,2},{2,1},{3,4},{4,3},{5,6},{6,5},{7,15},{8,0},{9,10},{10,... | collective-permute-start | bytes 86024 | tf_op jit(solution)/shard_map/ppermute | solution.py:428
  7.6 4.3 %collective-permute-start.2 = (bf16[96,256]{1,0:T(8,128)(2,1)S(1)}, bf16[96,256]{1,0:T(8,128)(2,1)S(1)}, u32[]{:S(2)}, u32[]{:S(2)}) collective-permute-start(bf16[96,256]{1,0:T(8,128)(2,1)S(1)} %get-tuple-element.75), channel_id=1, source_target_pairs={{0,1},{1,0},{2,3},{3,2},{4,5},{5,4},{6,7},{7,6},{8,9},{9,8},{10,11... | collective-permute-start | bytes 147464 | tf_op jit(solution)/shard_map/ppermute | solution.py:428
  7.8 4.1 %collective-permute-start.3 = (bf16[96,256]{1,0:T(8,128)(2,1)S(1)}, bf16[96,256]{1,0:T(8,128)(2,1)S(1)}, u32[]{:S(2)}, u32[]{:S(2)}) collective-permute-start(bf16[96,256]{1,0:T(8,128)(2,1)S(1)} %get-tuple-element.76), channel_id=1, source_target_pairs={{0,8},{1,2},{2,1},{3,4},{4,3},{5,6},{6,5},{7,15},{8,0},{9,10},{10,... | collective-permute-start | bytes 147464 | tf_op jit(solution)/shard_map/ppermute | solution.py:428
  12.2 4.4 %collective-permute-start.4 = (bf16[96,256]{1,0:T(8,128)(2,1)S(1)}, bf16[96,256]{1,0:T(8,128)(2,1)S(1)}, u32[]{:S(2)}, u32[]{:S(2)}) collective-permute-start(bf16[96,256]{1,0:T(8,128)(2,1)S(1)} %get-tuple-element.88), channel_id=1, source_target_pairs={{0,1},{1,0},{2,3},{3,2},{4,5},{5,4},{6,7},{7,6},{8,9},{9,8},{10,11... | collective-permute-start | bytes 147464 | tf_op jit(solution)/shard_map/ppermute | solution.py:428
  12.4 4.2 %collective-permute-start.5 = (bf16[96,256]{1,0:T(8,128)(2,1)S(1)}, bf16[96,256]{1,0:T(8,128)(2,1)S(1)}, u32[]{:S(2)}, u32[]{:S(2)}) collective-permute-start(bf16[96,256]{1,0:T(8,128)(2,1)S(1)} %get-tuple-element.89), channel_id=1, source_target_pairs={{0,8},{1,2},{2,1},{3,4},{4,3},{5,6},{6,5},{7,15},{8,0},{9,10},{10,... | collective-permute-start | bytes 147464 | tf_op jit(solution)/shard_map/ppermute | solution.py:428
  16.9 4.2 %collective-permute-start.6 = (bf16[96,256]{1,0:T(8,128)(2,1)S(1)}, bf16[96,256]{1,0:T(8,128)(2,1)S(1)}, u32[]{:S(2)}, u32[]{:S(2)}) collective-permute-start(bf16[96,256]{1,0:T(8,128)(2,1)S(1)} %get-tuple-element.96), channel_id=1, source_target_pairs={{0,1},{1,0},{2,3},{3,2},{4,5},{5,4},{6,7},{7,6},{8,9},{9,8},{10,11... | collective-permute-start | bytes 147464 | tf_op jit(solution)/shard_map/ppermute | solution.py:428
  17.2 4.1 %collective-permute-start.7 = (bf16[96,256]{1,0:T(8,128)(2,1)S(1)}, bf16[96,256]{1,0:T(8,128)(2,1)S(1)}, u32[]{:S(2)}, u32[]{:S(2)}) collective-permute-start(bf16[96,256]{1,0:T(8,128)(2,1)S(1)} %get-tuple-element.97), channel_id=1, source_target_pairs={{0,8},{1,2},{2,1},{3,4},{4,3},{5,6},{6,5},{7,15},{8,0},{9,10},{10,... | collective-permute-start | bytes 147464 | tf_op jit(solution)/shard_map/ppermute | solution.py:428
  21.9 11.0 %collective-permute-start.10 = (bf16[96,768]{1,0:T(8,128)(2,1)S(1)}, bf16[96,768]{1,0:T(8,128)(2,1)S(1)}, u32[]{:S(2)}, u32[]{:S(2)}) collective-permute-start(bf16[96,768]{1,0:T(8,128)(2,1)S(1)} %shard_map.77.inner_ref), channel_id=1, source_target_pairs={{0,8},{1,17},{2,10},{3,19},{4,12},{5,21},{6,14},{7,23},{8,0},{9,25... | collective-permute-start | bytes 442376 | tf_op jit(solution)/shard_map/ppermute | solution.py:447
  23.4 10.1 %collective-permute-start.11 = (bf16[96,768]{1,0:T(8,128)(2,1)S(1)}, bf16[96,768]{1,0:T(8,128)(2,1)S(1)}, u32[]{:S(2)}, u32[]{:S(2)}) collective-permute-start(bf16[96,768]{1,0:T(8,128)(2,1)S(1)} %shard_map.77.inner_ref), channel_id=1, source_target_pairs={{0,16},{1,9},{2,18},{3,11},{4,20},{5,13},{6,22},{7,15},{8,24},{9,1... | collective-permute-start | bytes 442376 | tf_op jit(solution)/shard_map/ppermute | solution.py:447
  24.9 1.2 %collective-permute-start.8 = (bf16[96,256]{1,0:T(8,128)(2,1)S(1)}, bf16[96,256]{1,0:T(8,128)(2,1)S(1)}, u32[]{:S(2)}, u32[]{:S(2)}) collective-permute-start(bf16[96,256]{1,0:T(8,128)(2,1)S(1)} %get-tuple-element.105), channel_id=1, source_target_pairs={{0,1},{1,0},{2,3},{3,2},{4,5},{5,4},{6,7},{7,6},{8,9},{9,8},{10,11... | collective-permute-start | bytes 147464 | tf_op jit(solution)/shard_map/ppermute | solution.py:428
  24.9 4.2 %collective-permute-start.9 = (bf16[96,256]{1,0:T(8,128)(2,1)S(1)}, bf16[96,256]{1,0:T(8,128)(2,1)S(1)}, u32[]{:S(2)}, u32[]{:S(2)}) collective-permute-start(bf16[96,256]{1,0:T(8,128)(2,1)S(1)} %get-tuple-element.106), channel_id=1, source_target_pairs={{0,8},{1,2},{2,1},{3,4},{4,3},{5,6},{6,5},{7,15},{8,0},{9,10},{10,... | collective-permute-start | bytes 147464 | tf_op jit(solution)/shard_map/ppermute | solution.py:428
  29.3 5.1 %collective-permute-start.12 = (bf16[96,512]{1,0:T(8,128)(2,1)S(1)}, bf16[96,512]{1,0:T(8,128)(2,1)S(1)}, u32[]{:S(2)}, u32[]{:S(2)}) collective-permute-start(bf16[96,512]{1,0:T(8,128)(2,1)S(1)} %shard_map.76.zone_ref.refs_8_), channel_id=1, source_target_pairs={{0,8},{1,17},{2,10},{3,19},{4,12},{5,21},{6,14},{7,23},{8,0},{9,25... | collective-permute-start | bytes 294920 | tf_op jit(solution)/shard_map/ppermute | solution.py:447
  30.8 4.6 %collective-permute-start.13 = (bf16[96,512]{1,0:T(8,128)(2,1)S(1)}, bf16[96,512]{1,0:T(8,128)(2,1)S(1)}, u32[]{:S(2)}, u32[]{:S(2)}) collective-permute-start(bf16[96,512]{1,0:T(8,128)(2,1)S(1)} %shard_map.76.zone_ref.refs_8_), channel_id=1, source_target_pairs={{0,16},{1,9},{2,18},{3,11},{4,20},{5,13},{6,22},{7,15},{8,24},{9,1... | collective-permute-start | bytes 294920 | tf_op jit(solution)/shard_map/ppermute | solution.py:447
  36.0 1.4 %collective-permute-start.14 = (bf16[2,2,96,96]{3,2,1,0:T(8,128)(2,1)S(1)}, bf16[2,2,96,96]{3,2,1,0:T(8,128)(2,1)S(1)}, u32[]{:S(2)}, u32[]{:S(2)}) collective-permute-start(bf16[2,2,96,96]{3,2,1,0:T(8,128)(2,1)S(1)} %get-tuple-element.122), channel_id=1, source_target_pairs={{0,1},{1,0},{2,3},{3,2},{4,5},{5,4},{6,7},{7,6},{8,9},{9,8},{10,11... | collective-permute-start | bytes 221192 | tf_op jit(solution)/shard_map/ppermute | solution.py:428
  37.4 4.7 %collective-permute-start.15 = (bf16[2,96,96]{2,1,0:T(8,128)(2,1)S(1)}, bf16[2,96,96]{2,1,0:T(8,128)(2,1)S(1)}, u32[]{:S(2)}, u32[]{:S(2)}) collective-permute-start(bf16[2,96,96]{2,1,0:T(8,128)(2,1)S(1)} %get-tuple-element.124), channel_id=1, source_target_pairs={{0,2},{1,13},{2,0},{3,5},{4,12},{5,3},{6,4},{7,1},{8,10},{9,15},{1... | collective-permute-start | bytes 110600 | tf_op jit(solution)/shard_map/ppermute | solution.py:459
  37.5 5.6 %collective-permute-start.16 = (bf16[2,96,96]{2,1,0:T(8,128)(2,1)S(1)}, bf16[2,96,96]{2,1,0:T(8,128)(2,1)S(1)}, u32[]{:S(2)}, u32[]{:S(2)}) collective-permute-start(bf16[2,96,96]{2,1,0:T(8,128)(2,1)S(1)} %get-tuple-element.123.mine_ref), channel_id=1, source_target_pairs={{0,10},{1,5},{2,8},{3,13},{4,14},{5,1},{6,12},{7,3},{8,2},{9,7},{1... | collective-permute-start | bytes 110600 | tf_op jit(solution)/shard_map/ppermute | solution.py:459
  43.1 1.3 %collective-permute-start.17 = (bf16[96,96]{1,0:T(8,128)(2,1)S(1)}, bf16[96,96]{1,0:T(8,128)(2,1)S(1)}, u32[]{:S(2)}, u32[]{:S(2)}) collective-permute-start(bf16[96,96]{1,0:T(8,128)(2,1)S(1)} %get-tuple-element.126), channel_id=1, source_target_pairs={{0,1},{1,0},{2,3},{3,2},{4,5},{5,4},{6,7},{7,6},{8,9},{9,8},{10,11... | collective-permute-start | bytes 55304 | tf_op jit(solution)/shard_map/ppermute | solution.py:428

commit v7 on v6

--- a/solution.py
+++ b/solution.py
@@ -211,12 +211,10 @@
     )
 
 
-def second_inner_body(zone_ref, inner_ref, old_ref, shift_inner_ref, picked_ref, hot_ref, wide_inner_ref,
-                      next_ref, part_ref, columns_ref, square_ref, diagonal_ref, zone_hot_ref):
+def second_inner_body(zone_ref, inner_ref, old_ref, shift_inner_ref, picked_ref, hot_ref, wide_inner_ref, zone_hot_ref,
+                      next_ref, part_ref, columns_ref, square_ref, diagonal_ref):
     extent = hot_ref.shape[0]
     width = zone_ref.shape[1] // 2
-    zone_hot_ref[:width, :] = hot_ref[:width, :]
-    zone_hot_ref[width:, :] = hot_ref[extent - width :, :]
     columns_ref[...] = mm_nt(wide_inner_ref[...], zone_hot_ref[...]).astype(BF16)
     picked = (picked_ref[...].astype(F32) + mm(zone_ref[...], zone_hot_ref[...])).astype(BF16)
     sums = mm_nt(picked, wide_inner_ref[...])
@@ -495,12 +493,11 @@
         (states_here, *got, row, outer, wide, picked), work,
     )
     got = exchange(*gave, n_state, n_space)
-    inner_1, wide_inner, border, border_diagonal, partial, picked = call(
+    inner_1, wide_inner, border, border_diagonal, partial, picked, zone_hot = call(
         first_inner_body,
         (inner, SHAPE((inside, cells * nodes), BF16), SHAPE((4 * rim, 4 * rim), BF16), border_line, sums_of,
-         SHAPE((count, cells * nodes), BF16)),
+         SHAPE((count, cells * nodes), BF16), SHAPE((4 * rim, cells * nodes), BF16)),
         (inner_0, picked, shift_inner, hot, wide, cells_here), 8 * extent * rim * cells * nodes,
-        scratch=[pltpu.VMEM((4 * rim, cells * nodes), BF16)],
     )
     inners, zones = [inner_0, inner_1], [zone_0]
     for k in range(1, DEGREE):
@@ -518,8 +515,7 @@
             inner_k, partial, columns, begun, begun_diagonal = call(
                 second_inner_body,
                 (inner, sums_of, SHAPE((inside, 4 * rim), BF16), SHAPE((2 * rim, inside), BF16), line),
-                (*ins, picked, hot, wide_inner), 4 * extent * rim * cells * nodes,
-                scratch=[pltpu.VMEM((4 * rim, cells * nodes), BF16)],
+                (*ins, picked, hot, wide_inner, zone_hot), 4 * extent * rim * cells * nodes,
             )
         elif k == 2:
             square, diagonal, inner_k, partial, opened = call(

time: 45.2 us -> 45.3 us (level)
  starting transfers between devices: 16.4 us -> 17.2 us
  waiting for transfers between devices: 11.4 us -> 10.7 us
    ppermute x2, starting transfers between devices: 2.04 us -> 2.88 us  [share_out(): return lax.ppermute(block, ('state', 'space'), route)]
    ppermute x4, waiting for transfers between devices: 1.44 us -> 0.75 us  [beside(): return lax.ppermute(block, ('state', 'space'), route)]
where the time goes in v7:
time: 45.3 us; the launch traced here: 45.2 us
  starting transfers between devices  17.2 us (38%)
  Pallas kernels  16.4 us (36%)
  waiting for transfers between devices  10.7 us (24%)
  between operations  0.81 us (2%)
    pallas_call x18, Pallas kernels, call(): pl.pallas_call(body, out_shape=outs, in_specs=where, out_specs=jax.tree.m...  16.4 us
    ppermute x12, starting transfers between devices, swap(): return lax.ppermute(block, ('state', 'space'), route)  9.05 us
    ppermute x12, waiting for transfers between devices, swap(): return lax.ppermute(block, ('state', 'space'), route)  6.34 us
    ppermute x4, starting transfers between devices, beside(): return lax.ppermute(block, ('state', 'space'), route)  5.32 us
    ppermute x2, waiting for transfers between devices, share_out(): return lax.ppermute(block, ('state', 'space'), route)  3.64 us
    ppermute x2, starting transfers between devices, share_out(): return lax.ppermute(block, ('state', 'space'), route)  2.88 us
  transfers between devices with their start and end apart: 18, of which 9 were waited for; matrix products, arithmetic and copies ran while one was open for 0% of the time, Pallas kernels for 28%

profile of v7, /device:TPU:0, one launch (start us, length us, event | category | flops | bytes accessed | tf_op | source)
XLA Modules:
  0.0 45.2 jit_solution(483006132227816029)
XLA Ops:
  0.6 0.8 %shard_map.67 = (bf16[112,128]{1,0:T(8,128)(2,1)S(1)}, bf16[112,128]{1,0:T(8,128)(2,1)S(1)}, f32[1,1024]{1,0:T(1,128)S(1)}, s32[2,512]{1,0:T(2,128)S(1)}) custom-call(bf16[96,1024]{1,0:T(8,128)(2,1)} %states_ref.3, f32[1,1024]{1,0:T(1,128)} %bitcast.3, s32[2,512]{1,0:T(2,128)} %index_ref.1), custom_call_target="tpu_custom_call" | custom-call | bytes 4194304 | tf_op jit(solution)/shard_map/pallas_call | solution.py:26
  2.0 2.6 %collective-permute-start.1 = (bf16[112,128]{1,0:T(8,128)(2,1)S(1)}, bf16[112,128]{1,0:T(8,128)(2,1)S(1)}, u32[]{:S(2)}, u32[]{:S(2)}) collective-permute-start(bf16[112,128]{1,0:T(8,128)(2,1)S(1)} %get-tuple-element.70), channel_id=1, source_target_pairs={{0,8},{1,2},{2,1},{3,4},{4,3},{5,6},{6,5},{7,15},{8,0},{9,10},{10,... | collective-permute-start | bytes 86024 | tf_op jit(solution)/shard_map/ppermute | solution.py:426
  4.6 2.4 %shard_map.68 = (bf16[1280,1024]{1,0:T(8,128)(2,1)S(1)}, bf16[256,1024]{1,0:T(8,128)(2,1)S(1)}, bf16[512,1024]{1,0:T(8,128)(2,1)S(1)}, bf16[96,1024]{1,0:T(8,128...) custom-call(s32[2,512]{1,0:T(2,128)S(1)} %get-tuple-element.67.index_ref, ...), custom_call_target="tpu_custom_call" | custom-call | flops 314572800 | bytes 4194304 | tf_op jit(solution)/shard_map/pallas_call | solution.py:26
  7.0 0.6 %shard_map.69 = (bf16[96,768]{1,0:T(8,128)(2,1)S(1)}, bf16[96,512]{1,0:T(8,128)(2,1)S(1)}, f32[1,768]{1,0:T(1,128)S(1)}, f32[1,512]{1,0:T(1,128)S(1)}, bf16[96,1...) custom-call(bf16[96,1024]{1,0:T(8,128)(2,1)S(1)} %get-tuple-element.68.s, ...), custom_call_target="tpu_custom_call" | custom-call | flops 314572800 | bytes 4194304 | tf_op jit(solution)/shard_map/pallas_call | solution.py:26
  7.8 1.5 %collective-permute-start.3 = (bf16[96,256]{1,0:T(8,128)(2,1)S(1)}, bf16[96,256]{1,0:T(8,128)(2,1)S(1)}, u32[]{:S(2)}, u32[]{:S(2)}) collective-permute-start(bf16[96,256]{1,0:T(8,128)(2,1)S(1)} %get-tuple-element.77), channel_id=1, source_target_pairs={{0,8},{1,2},{2,1},{3,4},{4,3},{5,6},{6,5},{7,15},{8,0},{9,10},{10,... | collective-permute-start | bytes 147464 | tf_op jit(solution)/shard_map/ppermute | solution.py:426
  9.3 2.6 %shard_map.70 = (bf16[96,768]{1,0:T(8,128)(2,1)S(1)}, bf16[768,1024]{1,0:T(8,128)(2,1)S(1)}, bf16[512,512]{1,0:T(8,128)(2,1)S(1)}, f32[1,512]{1,0:T(1,128)S(1)},...) custom-call(bf16[96,768]{1,0:T(8,128)(2,1)S(1)} %get-tuple-element.80.inner_ref.old_ref, ...), custom_call_target="tpu_custom_call" | custom-call | flops 1342177280 | bytes 4194304 | tf_op jit(solution)/shard_map/pallas_call | solution.py:26
  12.4 1.5 %collective-permute-start.5 = (bf16[96,256]{1,0:T(8,128)(2,1)S(1)}, bf16[96,256]{1,0:T(8,128)(2,1)S(1)}, u32[]{:S(2)}, u32[]{:S(2)}) collective-permute-start(bf16[96,256]{1,0:T(8,128)(2,1)S(1)} %get-tuple-element.90), channel_id=1, source_target_pairs={{0,8},{1,2},{2,1},{3,4},{4,3},{5,6},{6,5},{7,15},{8,0},{9,10},{10,... | collective-permute-start | bytes 147464 | tf_op jit(solution)/shard_map/ppermute | solution.py:426
  13.9 2.7 %shard_map.72 = (bf16[96,768]{1,0:T(8,128)(2,1)S(1)}, f32[96,512]{1,0:T(8,128)S(1)}, bf16[768,512]{1,0:T(8,128)(2,1)S(1)}, bf16[256,768]{1,0:T(8,128)(2,1)S(1)}, f32[1,768]{1,0:T(1,128)S(1)}) custom-call(bf16[96,512]{1,0:T(8,128)(2,1)S(1)} %get-tuple-element.91.zone_ref.mid_ref.rest_0_, bf16[96,768]{1,0:T(8,128)(2,1)S(1)} %get-tuple-element.92.inner_ref.old_ref, ...), custom_call_target="tpu_custom_call" | custom-call | flops 671088640 | bytes 4194304 | tf_op jit(solution)/shard_map/pallas_call | solution.py:26
  17.2 1.5 %collective-permute-start.7 = (bf16[96,256]{1,0:T(8,128)(2,1)S(1)}, bf16[96,256]{1,0:T(8,128)(2,1)S(1)}, u32[]{:S(2)}, u32[]{:S(2)}) collective-permute-start(bf16[96,256]{1,0:T(8,128)(2,1)S(1)} %get-tuple-element.99), channel_id=1, source_target_pairs={{0,8},{1,2},{2,1},{3,4},{4,3},{5,6},{6,5},{7,15},{8,0},{9,10},{10,... | collective-permute-start | bytes 147464 | tf_op jit(solution)/shard_map/ppermute | solution.py:426
  18.6 2.4 %shard_map.74 = (bf16[768,768]{1,0:T(8,128)(2,1)S(1)}, f32[1,768]{1,0:T(1,128)S(1)}, bf16[96,768]{1,0:T(8,128)(2,1)}, f32[96,512]{1,0:T(8,128)S(1)}, f32[96,768]{1,0:T(8,128)S(1)}) custom-call(bf16[96,512]{1,0:T(8,128)(2,1)S(1)} %get-tuple-element.100.zone_ref.mid_ref.old_ref, bf16[96,768]{1,0:T(8,128)(2,1)S(1)} %get-tuple-element.101.inner_ref.old_ref, ...), custom_call_target="tpu_custom_call" | custom-call | flops 671088640 | bytes 4194304 | tf_op jit(solution)/shard_map/pallas_call | solution.py:26
  21.9 1.6 %collective-permute-start.10 = (bf16[96,768]{1,0:T(8,128)(2,1)S(1)}, bf16[96,768]{1,0:T(8,128)(2,1)S(1)}, u32[]{:S(2)}, u32[]{:S(2)}) collective-permute-start(bf16[96,768]{1,0:T(8,128)(2,1)S(1)} %shard_map.77.inner_ref), channel_id=1, source_target_pairs={{0,8},{1,17},{2,10},{3,19},{4,12},{5,21},{6,14},{7,23},{8,0},{9,25... | collective-permute-start | bytes 442376 | tf_op jit(solution)/shard_map/ppermute | solution.py:445
  23.4 1.5 %collective-permute-start.11 = (bf16[96,768]{1,0:T(8,128)(2,1)S(1)}, bf16[96,768]{1,0:T(8,128)(2,1)S(1)}, u32[]{:S(2)}, u32[]{:S(2)}) collective-permute-start(bf16[96,768]{1,0:T(8,128)(2,1)S(1)} %shard_map.77.inner_ref), channel_id=1, source_target_pairs={{0,16},{1,9},{2,18},{3,11},{4,20},{5,13},{6,22},{7,15},{8,24},{9,1... | collective-permute-start | bytes 442376 | tf_op jit(solution)/shard_map/ppermute | solution.py:445
  25.5 0.7 %collective-permute-done.8.got_a_ref = bf16[96,256]{1,0:T(8,128)(2,1)S(1)} collective-permute-done((bf16[96,256]{1,0:T(8,128)(2,1)S(1)}, bf16[96,256]{1,0:T(8,128)(2,1)S(1)}, u32[]{:S(2)}, u32[]{:S(2)}) %collective-permute-start.8) | collective-permute-done | bytes 49184 | tf_op jit(solution)/shard_map/ppermute | solution.py:426
  26.2 3.0 %collective-permute-done.9.got_b_ref = bf16[96,256]{1,0:T(8,128)(2,1)S(1)} collective-permute-done((bf16[96,256]{1,0:T(8,128)(2,1)S(1)}, bf16[96,256]{1,0:T(8,128)(2,1)S(1)}, u32[]{:S(2)}, u32[]{:S(2)}) %collective-permute-start.9) | collective-permute-done | bytes 49184 | tf_op jit(solution)/shard_map/ppermute | solution.py:426
  29.3 0.9 %collective-permute-start.13 = (bf16[96,512]{1,0:T(8,128)(2,1)S(1)}, bf16[96,512]{1,0:T(8,128)(2,1)S(1)}, u32[]{:S(2)}, u32[]{:S(2)}) collective-permute-start(bf16[96,512]{1,0:T(8,128)(2,1)S(1)} %shard_map.76.zone_ref.refs_8_), channel_id=1, source_target_pairs={{0,16},{1,9},{2,18},{3,11},{4,20},{5,13},{6,22},{7,15},{8,24},{9,1... | collective-permute-start | bytes 294920 | tf_op jit(solution)/shard_map/ppermute | solution.py:445
  30.1 1.4 %collective-permute-start.12 = (bf16[96,512]{1,0:T(8,128)(2,1)S(1)}, bf16[96,512]{1,0:T(8,128)(2,1)S(1)}, u32[]{:S(2)}, u32[]{:S(2)}) collective-permute-start(bf16[96,512]{1,0:T(8,128)(2,1)S(1)} %shard_map.76.zone_ref.refs_8_), channel_id=1, source_target_pairs={{0,8},{1,17},{2,10},{3,19},{4,12},{5,21},{6,14},{7,23},{8,0},{9,25... | collective-permute-start | bytes 294920 | tf_op jit(solution)/shard_map/ppermute | solution.py:445
  31.5 1.3 %shard_map.78 = (bf16[96,768]{1,0:T(8,128)(2,1)S(1)}, bf16[96,512]{1,0:T(8,128)(2,1)S(1)}, bf16[96,1024]{1,0:T(8,128)(2,1)}) custom-call(bf16[96,512]{1,0:T(8,128)(2,1)S(1)} %shard_map.76.zone_ref.refs_8_, bf16[96,768]{1,0:T(8,128)(2,1)S(1)} %shard_map.77.inner_ref, f32[1,768]{1,0:T(1,128)S(1)} %get-tuple-element.82.shift_inner_ref, ...), custom_call_target="tpu_custom_call" | custom-call | flops 314572800 | bytes 4194304 | tf_op jit(solution)/shard_map/pallas_call | solution.py:26
  32.9 0.7 %shard_map.79 = (bf16[96,768]{1,0:T(8,128)(2,1)S(1)}, f32[96,512]{1,0:T(8,128)S(1)}, f32[192,192]{1,0:T(8,128)S(1)}) custom-call(bf16[96,768]{1,0:T(8,128)(2,1)S(1)} %shard_map.77.inner_ref, bf16[96,768]{1,0:T(8,128)(2,1)S(1)} %collective-permute-done.10.first_ref, bf16[96,768]{1,0:T(8,128)(2,1)S(1)} %get-tuple-element.115.energy_ref, ...), custom_call_target="tpu_custom_call" | custom-call | flops 157286400 | bytes 4194304 | tf_op jit(solution)/shard_map/pallas_call | solution.py:26
  35.4 1.3 %collective-permute-done.14.got_ref = bf16[2,2,96,96]{3,2,1,0:T(8,128)(2,1)S(1)} collective-permute-done((bf16[2,2,96,96]{3,2,1,0:T(8,128)(2,1)S(1)}, bf16[2,2,96,96]{3,2,1,0:T(8,128)(2,1)S(1)}, u32[]{:S(2)}, u32[]{:S(2)}) %collective-permute-start.14) | collective-permute-done | bytes 73760 | tf_op jit(solution)/shard_map/ppermute | solution.py:426
  36.8 2.8 %collective-permute-start.16 = (bf16[2,96,96]{2,1,0:T(8,128)(2,1)S(1)}, bf16[2,96,96]{2,1,0:T(8,128)(2,1)S(1)}, u32[]{:S(2)}, u32[]{:S(2)}) collective-permute-start(bf16[2,96,96]{2,1,0:T(8,128)(2,1)S(1)} %get-tuple-element.125.mine_ref), channel_id=1, source_target_pairs={{0,10},{1,5},{2,8},{3,13},{4,14},{5,1},{6,12},{7,3},{8,2},{9,7},{1... | collective-permute-start | bytes 110600 | tf_op jit(solution)/shard_map/ppermute | solution.py:457
  39.6 2.1 %collective-permute-done.15.first_ref = bf16[2,96,96]{2,1,0:T(8,128)(2,1)S(1)} collective-permute-done((bf16[2,96,96]{2,1,0:T(8,128)(2,1)S(1)}, bf16[2,96,96]{2,1,0:T(8,128)(2,1)S(1)}, u32[]{:S(2)}, u32[]{:S(2)}) %collective-permute-start.15) | collective-permute-done | bytes 36896 | tf_op jit(solution)/shard_map/ppermute | solution.py:457
  41.8 1.5 %collective-permute-done.16.second_ref = bf16[2,96,96]{2,1,0:T(8,128)(2,1)S(1)} collective-permute-done((bf16[2,96,96]{2,1,0:T(8,128)(2,1)S(1)}, bf16[2,96,96]{2,1,0:T(8,128)(2,1)S(1)}, u32[]{:S(2)}, u32[]{:S(2)}) %collective-permute-start.16) | collective-permute-done | bytes 36896 | tf_op jit(solution)/shard_map/ppermute | solution.py:457
  43.4 1.2 %collective-permute-done.17.got_ref = bf16[96,96]{1,0:T(8,128)(2,1)S(1)} collective-permute-done((bf16[96,96]{1,0:T(8,128)(2,1)S(1)}, bf16[96,96]{1,0:T(8,128)(2,1)S(1)}, u32[]{:S(2)}, u32[]{:S(2)}) %collective-permute-start.17) | collective-permute-done | bytes 18464 | tf_op jit(solution)/shard_map/ppermute | solution.py:426
  44.5 0.6 %shard_map.84 = (f32[48,96]{1,0:T(8,128)}, f32[48,96]{1,0:T(8,128)}) custom-call(f32[96,96]{1,0:T(8,128)S(1)} %get-tuple-element.127.keep_ref, bf16[96,96]{1,0:T(8,128)(2,1)S(1)} %collective-permute-done.17.got_ref), custom_call_target="tpu_custom_call" | custom-call | bytes 4194304 | tf_op jit(solution)/shard_map/pallas_call | solution.py:26
  (30 shorter events, 5.2 us)
Async XLA Ops:
  1.5 5.5 %collective-permute-start = (bf16[112,128]{1,0:T(8,128)(2,1)S(1)}, bf16[112,128]{1,0:T(8,128)(2,1)S(1)}, u32[]{:S(2)}, u32[]{:S(2)}) collective-permute-start(bf16[112,128]{1,0:T(8,128)(2,1)S(1)} %get-tuple-element.69), channel_id=1, source_target_pairs={{0,1},{1,0},{2,3},{3,2},{4,5},{5,4},{6,7},{7,6},{8,9},{9,8},{10,11... | collective-permute-start | bytes 86024 | tf_op jit(solution)/shard_map/ppermute | solution.py:426
  2.0 5.0 %collective-permute-start.1 = (bf16[112,128]{1,0:T(8,128)(2,1)S(1)}, bf16[112,128]{1,0:T(8,128)(2,1)S(1)}, u32[]{:S(2)}, u32[]{:S(2)}) collective-permute-start(bf16[112,128]{1,0:T(8,128)(2,1)S(1)} %get-tuple-element.70), channel_id=1, source_target_pairs={{0,8},{1,2},{2,1},{3,4},{4,3},{5,6},{6,5},{7,15},{8,0},{9,10},{10,... | collective-permute-start | bytes 86024 | tf_op jit(solution)/shard_map/ppermute | solution.py:426
  7.6 4.3 %collective-permute-start.2 = (bf16[96,256]{1,0:T(8,128)(2,1)S(1)}, bf16[96,256]{1,0:T(8,128)(2,1)S(1)}, u32[]{:S(2)}, u32[]{:S(2)}) collective-permute-start(bf16[96,256]{1,0:T(8,128)(2,1)S(1)} %get-tuple-element.76), channel_id=1, source_target_pairs={{0,1},{1,0},{2,3},{3,2},{4,5},{5,4},{6,7},{7,6},{8,9},{9,8},{10,11... | collective-permute-start | bytes 147464 | tf_op jit(solution)/shard_map/ppermute | solution.py:426
  7.8 4.1 %collective-permute-start.3 = (bf16[96,256]{1,0:T(8,128)(2,1)S(1)}, bf16[96,256]{1,0:T(8,128)(2,1)S(1)}, u32[]{:S(2)}, u32[]{:S(2)}) collective-permute-start(bf16[96,256]{1,0:T(8,128)(2,1)S(1)} %get-tuple-element.77), channel_id=1, source_target_pairs={{0,8},{1,2},{2,1},{3,4},{4,3},{5,6},{6,5},{7,15},{8,0},{9,10},{10,... | collective-permute-start | bytes 147464 | tf_op jit(solution)/shard_map/ppermute | solution.py:426
  12.2 4.4 %collective-permute-start.4 = (bf16[96,256]{1,0:T(8,128)(2,1)S(1)}, bf16[96,256]{1,0:T(8,128)(2,1)S(1)}, u32[]{:S(2)}, u32[]{:S(2)}) collective-permute-start(bf16[96,256]{1,0:T(8,128)(2,1)S(1)} %get-tuple-element.89), channel_id=1, source_target_pairs={{0,1},{1,0},{2,3},{3,2},{4,5},{5,4},{6,7},{7,6},{8,9},{9,8},{10,11... | collective-permute-start | bytes 147464 | tf_op jit(solution)/shard_map/ppermute | solution.py:426
  12.4 4.2 %collective-permute-start.5 = (bf16[96,256]{1,0:T(8,128)(2,1)S(1)}, bf16[96,256]{1,0:T(8,128)(2,1)S(1)}, u32[]{:S(2)}, u32[]{:S(2)}) collective-permute-start(bf16[96,256]{1,0:T(8,128)(2,1)S(1)} %get-tuple-element.90), channel_id=1, source_target_pairs={{0,8},{1,2},{2,1},{3,4},{4,3},{5,6},{6,5},{7,15},{8,0},{9,10},{10,... | collective-permute-start | bytes 147464 | tf_op jit(solution)/shard_map/ppermute | solution.py:426
  16.9 4.2 %collective-permute-start.6 = (bf16[96,256]{1,0:T(8,128)(2,1)S(1)}, bf16[96,256]{1,0:T(8,128)(2,1)S(1)}, u32[]{:S(2)}, u32[]{:S(2)}) collective-permute-start(bf16[96,256]{1,0:T(8,128)(2,1)S(1)} %get-tuple-element.98), channel_id=1, source_target_pairs={{0,1},{1,0},{2,3},{3,2},{4,5},{5,4},{6,7},{7,6},{8,9},{9,8},{10,11... | collective-permute-start | bytes 147464 | tf_op jit(solution)/shard_map/ppermute | solution.py:426
  17.2 4.1 %collective-permute-start.7 = (bf16[96,256]{1,0:T(8,128)(2,1)S(1)}, bf16[96,256]{1,0:T(8,128)(2,1)S(1)}, u32[]{:S(2)}, u32[]{:S(2)}) collective-permute-start(bf16[96,256]{1,0:T(8,128)(2,1)S(1)} %get-tuple-element.99), channel_id=1, source_target_pairs={{0,8},{1,2},{2,1},{3,4},{4,3},{5,6},{6,5},{7,15},{8,0},{9,10},{10,... | collective-permute-start | bytes 147464 | tf_op jit(solution)/shard_map/ppermute | solution.py:426
  21.9 11.0 %collective-permute-start.10 = (bf16[96,768]{1,0:T(8,128)(2,1)S(1)}, bf16[96,768]{1,0:T(8,128)(2,1)S(1)}, u32[]{:S(2)}, u32[]{:S(2)}) collective-permute-start(bf16[96,768]{1,0:T(8,128)(2,1)S(1)} %shard_map.77.inner_ref), channel_id=1, source_target_pairs={{0,8},{1,17},{2,10},{3,19},{4,12},{5,21},{6,14},{7,23},{8,0},{9,25... | collective-permute-start | bytes 442376 | tf_op jit(solution)/shard_map/ppermute | solution.py:445
  23.4 10.1 %collective-permute-start.11 = (bf16[96,768]{1,0:T(8,128)(2,1)S(1)}, bf16[96,768]{1,0:T(8,128)(2,1)S(1)}, u32[]{:S(2)}, u32[]{:S(2)}) collective-permute-start(bf16[96,768]{1,0:T(8,128)(2,1)S(1)} %shard_map.77.inner_ref), channel_id=1, source_target_pairs={{0,16},{1,9},{2,18},{3,11},{4,20},{5,13},{6,22},{7,15},{8,24},{9,1... | collective-permute-start | bytes 442376 | tf_op jit(solution)/shard_map/ppermute | solution.py:445
  24.9 1.2 %collective-permute-start.8 = (bf16[96,256]{1,0:T(8,128)(2,1)S(1)}, bf16[96,256]{1,0:T(8,128)(2,1)S(1)}, u32[]{:S(2)}, u32[]{:S(2)}) collective-permute-start(bf16[96,256]{1,0:T(8,128)(2,1)S(1)} %get-tuple-element.107), channel_id=1, source_target_pairs={{0,1},{1,0},{2,3},{3,2},{4,5},{5,4},{6,7},{7,6},{8,9},{9,8},{10,11... | collective-permute-start | bytes 147464 | tf_op jit(solution)/shard_map/ppermute | solution.py:426
  24.9 4.2 %collective-permute-start.9 = (bf16[96,256]{1,0:T(8,128)(2,1)S(1)}, bf16[96,256]{1,0:T(8,128)(2,1)S(1)}, u32[]{:S(2)}, u32[]{:S(2)}) collective-permute-start(bf16[96,256]{1,0:T(8,128)(2,1)S(1)} %get-tuple-element.108), channel_id=1, source_target_pairs={{0,8},{1,2},{2,1},{3,4},{4,3},{5,6},{6,5},{7,15},{8,0},{9,10},{10,... | collective-permute-start | bytes 147464 | tf_op jit(solution)/shard_map/ppermute | solution.py:426
  29.3 5.1 %collective-permute-start.13 = (bf16[96,512]{1,0:T(8,128)(2,1)S(1)}, bf16[96,512]{1,0:T(8,128)(2,1)S(1)}, u32[]{:S(2)}, u32[]{:S(2)}) collective-permute-start(bf16[96,512]{1,0:T(8,128)(2,1)S(1)} %shard_map.76.zone_ref.refs_8_), channel_id=1, source_target_pairs={{0,16},{1,9},{2,18},{3,11},{4,20},{5,13},{6,22},{7,15},{8,24},{9,1... | collective-permute-start | bytes 294920 | tf_op jit(solution)/shard_map/ppermute | solution.py:445
  30.1 4.6 %collective-permute-start.12 = (bf16[96,512]{1,0:T(8,128)(2,1)S(1)}, bf16[96,512]{1,0:T(8,128)(2,1)S(1)}, u32[]{:S(2)}, u32[]{:S(2)}) collective-permute-start(bf16[96,512]{1,0:T(8,128)(2,1)S(1)} %shard_map.76.zone_ref.refs_8_), channel_id=1, source_target_pairs={{0,8},{1,17},{2,10},{3,19},{4,12},{5,21},{6,14},{7,23},{8,0},{9,25... | collective-permute-start | bytes 294920 | tf_op jit(solution)/shard_map/ppermute | solution.py:445
  35.3 1.4 %collective-permute-start.14 = (bf16[2,2,96,96]{3,2,1,0:T(8,128)(2,1)S(1)}, bf16[2,2,96,96]{3,2,1,0:T(8,128)(2,1)S(1)}, u32[]{:S(2)}, u32[]{:S(2)}) collective-permute-start(bf16[2,2,96,96]{3,2,1,0:T(8,128)(2,1)S(1)} %get-tuple-element.124), channel_id=1, source_target_pairs={{0,1},{1,0},{2,3},{3,2},{4,5},{5,4},{6,7},{7,6},{8,9},{9,8},{10,11... | collective-permute-start | bytes 221192 | tf_op jit(solution)/shard_map/ppermute | solution.py:426
  36.7 5.0 %collective-permute-start.15 = (bf16[2,96,96]{2,1,0:T(8,128)(2,1)S(1)}, bf16[2,96,96]{2,1,0:T(8,128)(2,1)S(1)}, u32[]{:S(2)}, u32[]{:S(2)}) collective-permute-start(bf16[2,96,96]{2,1,0:T(8,128)(2,1)S(1)} %get-tuple-element.126), channel_id=1, source_target_pairs={{0,2},{1,13},{2,0},{3,5},{4,12},{5,3},{6,4},{7,1},{8,10},{9,15},{1... | collective-permute-start | bytes 110600 | tf_op jit(solution)/shard_map/ppermute | solution.py:457
  36.8 6.5 %collective-permute-start.16 = (bf16[2,96,96]{2,1,0:T(8,128)(2,1)S(1)}, bf16[2,96,96]{2,1,0:T(8,128)(2,1)S(1)}, u32[]{:S(2)}, u32[]{:S(2)}) collective-permute-start(bf16[2,96,96]{2,1,0:T(8,128)(2,1)S(1)} %get-tuple-element.125.mine_ref), channel_id=1, source_target_pairs={{0,10},{1,5},{2,8},{3,13},{4,14},{5,1},{6,12},{7,3},{8,2},{9,7},{1... | collective-permute-start | bytes 110600 | tf_op jit(solution)/shard_map/ppermute | solution.py:457
  43.3 1.3 %collective-permute-start.17 = (bf16[96,96]{1,0:T(8,128)(2,1)S(1)}, bf16[96,96]{1,0:T(8,128)(2,1)S(1)}, u32[]{:S(2)}, u32[]{:S(2)}) collective-permute-start(bf16[96,96]{1,0:T(8,128)(2,1)S(1)} %get-tuple-element.128), channel_id=1, source_target_pairs={{0,1},{1,0},{2,3},{3,2},{4,5},{5,4},{6,7},{7,6},{8,9},{9,8},{10,11... | collective-permute-start | bytes 55304 | tf_op jit(solution)/shard_map/ppermute | solution.py:426
